TPU v7x, 1024 devices: a whole 8x8x8 slice. The times are simulated.
1024 devices in a mesh: dp: 32 (over y_hi, z, core), mp: 32 (over y_lo, x).
Axes of the slice: x: 8, y: 8 (y_hi: 2, y_lo: 4; y = y_hi * 4 + y_lo), z: 8, core: 2. Of those that a mesh axis runs over, the one named last changes fastest.
Arguments:
- visual: bfloat16 [256, 32, 6144], P('dp', None, 'mp'), may hold values from -6 to 6
- vis_gain: float32 [6144], replicated, may hold values from 0.1 to 1.9
- text: bfloat16 [256, 32, 4096], P(None, 'dp'), may hold values from -6 to 6
- text_gain: float32 [4096], replicated, may hold values from 0.1 to 1.9
- query_weight: bfloat16 [4096, 4096], P(None, 'mp'), may hold values from -0.375 to 0.375
- key_weight: bfloat16 [6144, 4096], P(None, 'mp'), may hold values from -0.078125 to 0.078125
- value_weight: bfloat16 [6144, 4096], P(None, 'mp'), may hold values from -0.078125 to 0.078125
- out_weight: bfloat16 [4096, 4096], P('mp'), may hold values from -0.09375 to 0.09375
Outputs:
- mixed: bfloat16 [256, 32, 4096], P('mp', 'dp')
All inputs are finite; a program needn't handle non-finite values.
Results may differ from a plain program's by a relative error of at most 0.015.
Values may be sent and summed in bfloat16 or wider, within the bound.
No kernel may reach another device: no remote copies, remote signals or barrier semaphores. Data moves between devices by JAX's collectives and lax.ppermute only.
A program may use at most 32 MiB of HBM per device.

v0:
```python
import jax
import jax.numpy as jnp
from jax import lax
from jax.sharding import Mesh
from jax.sharding import PartitionSpec as P

DEC = 4096
HEAD_DIM = 128
MP = ("mp_0", "mp_1")


epsilon = 1e-06


def laid_out(blocks, dim):
    lengths = list(blocks.shape[1:])
    lengths[dim] *= blocks.shape[0]
    return jnp.moveaxis(blocks, 0, dim).reshape(lengths)


def all_blocks(array, axes, turns):
    blocks = array
    for k in turns:
        blocks = lax.all_gather(blocks, axes[k])
    done = turns[::-1]
    back = [done.index(k) for k in range(len(axes))]
    blocks = blocks.transpose(*back, *range(len(axes), blocks.ndim))
    return blocks.reshape(-1, *array.shape)


def whole_of(array, axes, turns, dim):
    return laid_out(all_blocks(array, axes, turns), dim)


def reduced_to_own(blocks, axes, turns):
    lengths = [lax.axis_size(a) for a in axes]
    blocks = blocks.reshape(*lengths, *blocks.shape[1:])
    blocks = blocks.transpose(*turns, *range(len(axes), blocks.ndim))
    blocks = blocks.reshape(-1, *blocks.shape[len(axes) :])
    for k in turns:
        blocks = lax.psum_scatter(blocks, axes[k], scatter_dimension=0, tiled=True)
    return blocks[0]


def cut_along(array, dim, devices):
    before, after = (array.shape[:dim], array.shape[dim + 1 :])
    return jnp.moveaxis(array.reshape(*before, devices, -1, *after), dim, 0)


def summed_rows_2(array, axes, turns, dim):
    devices = lax.axis_size(axes)
    return reduced_to_own(cut_along(array, dim, devices), axes, turns)


def layer_norm(values, gain):
    average = jnp.mean(values, axis=-1, keepdims=True)
    centred = values - average
    spread = jnp.mean(centred * centred, axis=-1, keepdims=True)
    return centred * lax.rsqrt(spread + epsilon) * gain


def body(visual, vis_gain, text, text_gain, query_weight, key_weight, value_weight, out_weight):
    relayed = lax.all_to_all(visual, "dp", split_axis=1, concat_axis=0, tiled=True)
    vis_tokens, images_here, feature_count = relayed.shape
    full_width = feature_count * lax.axis_size(MP)
    vis_rows = vis_tokens * images_here
    kv_columns = key_weight.shape[1]
    whole = whole_of(relayed, MP, (0, 1), 2)
    normed = layer_norm(whole.astype(jnp.float32), vis_gain).astype(jnp.bfloat16)
    normed = normed.reshape(vis_rows, full_width)
    keys = jnp.dot(normed, key_weight, preferred_element_type=jnp.float32).astype(jnp.bfloat16)
    values = jnp.dot(normed, value_weight, preferred_element_type=jnp.float32).astype(jnp.bfloat16)
    heads_here = kv_columns // HEAD_DIM
    text_tokens = text.shape[0]
    text_f = text.astype(jnp.float32)
    text_norm = (
        text_f * lax.rsqrt(jnp.mean(text_f * text_f, axis=-1, keepdims=True) + epsilon) * text_gain
    ).astype(jnp.bfloat16)
    queries = jnp.dot(
        text_norm.reshape(text_tokens * images_here, DEC),
        query_weight,
        preferred_element_type=jnp.float32,
    ).astype(jnp.bfloat16)
    queries = queries.reshape(text_tokens, images_here, heads_here, HEAD_DIM)
    keys = keys.reshape(vis_tokens, images_here, heads_here, HEAD_DIM)
    values = values.reshape(vis_tokens, images_here, heads_here, HEAD_DIM)
    scores = jnp.einsum(
        "tihd,vihd->ihtv", queries, keys, preferred_element_type=jnp.float32
    ) / jnp.sqrt(jnp.float32(HEAD_DIM))
    probs = jax.nn.softmax(scores, axis=-1).astype(jnp.bfloat16)
    context = jnp.einsum(
        "ihtv,vihd->tihd", probs, values, preferred_element_type=jnp.float32
    ).astype(jnp.bfloat16)
    context = context.reshape(text_tokens * images_here, kv_columns)
    summed = summed_rows_2(
        jnp.dot(context, out_weight, preferred_element_type=jnp.float32).astype(jnp.bfloat16),
        MP,
        (1, 0),
        0,
    ).astype(jnp.float32)
    tokens_here = text_tokens // lax.axis_size(MP)
    residual = lax.dynamic_slice_in_dim(text, lax.axis_index(MP) * tokens_here, tokens_here, 0)
    return (residual.astype(jnp.float32) + summed.reshape(tokens_here, images_here, DEC)).astype(
        jnp.bfloat16
    )


def solution(mesh):
    split = Mesh(mesh.devices.reshape(mesh.shape["dp"], 4, 8), ("dp", "mp_0", "mp_1"))
    in_specs = (
        P("dp", None, MP),
        P(),
        P(None, "dp", None),
        P(),
        P(None, MP),
        P(None, MP),
        P(None, MP),
        P(MP, None),
    )
    out_specs = P(MP, "dp", None)
    return jax.shard_map(body, mesh=split, in_specs=in_specs, out_specs=out_specs, check_vma=False)
```

profile of v0, /device:TPU:2, one launch (start us, length us, event | category | flops | bytes accessed | tf_op | source)
XLA Modules:
  0.0 208.6 jit_solution(8736905444603677529)
XLA Ops:
  6.5 0.0 copy-start
  6.5 0.0 copy-start.6
  6.5 0.0 copy-start.7
  6.5 0.0 all-gather.3.cloned.1.call-start
  6.5 1.1 copy.16
  7.7 35.6 %all_to_all.15 = bf16[8,32,192]{2,0,1:T(8,128)(2,1)S(1)} all-to-all(bf16[8,32,192]{2,0,1:T(8,128)(2,1)S(1)} %copy.16), channel_id=1, replica_groups=mesh['dp'=32,'mp_0'=4,'mp_1'=8] {'dp'}, dimensions={1} | all-to-all | bytes 196608 | tf_op jit(solution)/shard_map/all_to_all | solution.py:63
  43.3 0.1 copy.17
  43.4 15.5 %all_gather.13 = bf16[4,256,1,192]{1,3,2,0:T(8,128)(2,1)} all-gather(bf16[1,256,1,192]{1,3,2,0:T(8,128)(2,1)S(1)} %copy.17), channel_id=1, replica_groups=mesh['dp'=32,'mp_0'=4,'mp_1'=8] {'mp_0'}, dimensions={0}, use_global_device_ids=true | all-gather | bytes 491520 | tf_op jit(solution)/shard_map/all_gather | solution.py:24
  59.0 0.0 all-gather.3.cloned.1.call-update
  59.0 0.0 reduce-scatter.3.cloned.1.call-start
  59.0 2.1 fusion.3
  61.1 0.0 copy-done.6
  61.2 0.0 copy-done.7
  61.2 2.4 %fusion.11 = bf16[256,128]{1,0:T(8,128)(2,1)S(1)} fusion(bf16[4096,128]{1,0:T(8,128)(2,1)S(1)} %copy-done.6, bf16[256,1,4096]{2,0,1:T(8,128)(2,1)} %param.10, f32[4096]{0:T(1024)S(1)} %copy-done.7, f32[256]{0:T(256)S(1)} %add_rsqrt_fusion), kind=kOutput, calls=%fused_computation.17 | convolution fusion | flops 272662528 | bytes 3228672 | tf_op jit(solution)/shard_map/dot_general | solution.py:79
  63.6 37.7 %all-gather.3.cloned.1.call-done = bf16[32,256,1,192]{1,3,2,0:T(8,128)(2,1)} async-done(((bf16[4,256,1,192]{1,3,2,0:T(8,128)(2,1)}), bf16[32,256,1,192]{1,3,2,0:T(8,128)(2,1)}) %all-gather.3.cloned.1.call-update) | async-done | bytes 3145744 | tf_op jit(solution)/shard_map/all_gather | solution.py:24
  101.3 0.0 copy-start.2
  101.3 2.9 %convert_reduce_fusion = f32[256]{0:T(256)S(1)} fusion(bf16[32,256,1,192]{1,3,2,0:T(8,128)(2,1)} %all-gather.3.cloned.1.call-done), kind=kLoop, calls=%fused_computation.15 | loop fusion | flops 3145472 | bytes 3146752 | tf_op jit(solution)/shard_map/reduce_sum | solution.py:56
  104.1 0.0 copy-done.2
  104.2 0.8 convert_element_type.129
  104.9 0.7 copy.18
  105.6 0.0 copy-start.5
  105.6 0.8 multiply_reduce_fusion
  106.5 0.0 copy-done.5
  106.5 0.0 copy-start.3
  106.5 1.0 fusion.2
  107.5 0.0 copy-start.1
  107.5 1.7 copy-done.1
  109.2 0.0 copy-done.3
  109.2 1.0 convolution_convert_fusion.2
  110.2 0.0 copy-done
  110.2 0.0 copy-start.4
  110.2 3.1 %fusion.21 = (f32[256]{0:T(256)S(1)}, f32[256,256]{0,1:T(8,128)S(1)}) fusion(bf16[256,128]{1,0:T(8,128)(2,1)S(1)} %fusion.11, bf16[256,6144]{0,1:T(8,128)(2,1)} %copy-done.1, bf16[6144,128]{1,0:T(8,128)(2,1)S(1)} %copy-done), kind=kOutput, calls=%fused_computation.32 | convolution fusion | flops 419593984 | bytes 5047296 | tf_op jit(solution)/shard_map/tihd,vihd->ihtv/dot_general | solution.py:87
  113.4 0.1 fusion.15
  113.4 0.0 copy-done.4
  113.4 2.2 %convolution_convert_fusion = bf16[256,4096]{1,0:T(8,128)(2,1)} fusion(bf16[128,4096]{1,0:T(8,128)(2,1)S(1)} %copy-done.4, bf16[256,128]{1,0:T(8,128)(2,1)S(1)} %convolution_convert_fusion.2, f32[256,256]{0,1:T(8,128)S(1)} %get-tuple-element.6, f32[256]{0:T(256)S(1)} %fusion.15, f32[256]{0:T(256)S(1)} %get-tuple-element.5), kind=kOutput, calls=%fused_computation.7 | convolution fusion | flops 286490624 | bytes 3475456 | tf_op jit(solution)/shard_map/dot_general | solution.py:96
  115.7 3.2 %copy.19 = bf16[8,4,8,4096]{3,2,1,0:T(8,128)(2,1)} copy(bf16[8,4,8,4096]{3,2,0,1:T(8,128)(2,1)} %bitcast.53) | data formatting | bytes 4194304 | tf_op jit(solution)/shard_map/transpose | solution.py:38
  118.8 0.0 reduce-scatter.3.cloned.1.call-update
  118.9 0.0 reduce-scatter.5.cloned.1.call-start
  118.9 47.5 %reduce-scatter.3.cloned.1.call-done = bf16[4,8,4096]{2,1,0:T(8,128)(2,1)} async-done(((bf16[32,8,4096]{2,1,0:T(8,128)(2,1)}), bf16[4,8,4096]{2,1,0:T(8,128)(2,1)}) %reduce-scatter.3.cloned.1.call-update) | async-done | bytes 262160 | tf_op jit(solution)/shard_map/reduce_scatter | solution.py:41
  166.4 0.0 reduce-scatter.5.cloned.1.call-update
  166.4 34.1 %reduce-scatter.5.cloned.1.call-done = bf16[1,8,4096]{2,1,0:T(8,128)(2,1)} async-done(((bf16[4,8,4096]{2,1,0:T(8,128)(2,1)}), bf16[1,8,4096]{2,1,0:T(8,128)(2,1)}) %reduce-scatter.5.cloned.1.call-update) | async-done | bytes 65552 | tf_op jit(solution)/shard_map/reduce_scatter | solution.py:41
  200.5 1.5 fusion.16
  (3 shorter events, 0.0 us)
Async XLA Ops:
  6.5 103.7 %copy-start = (bf16[6144,128]{1,0:T(8,128)(2,1)S(1)}, bf16[6144,128]{1,0:T(8,128)(2,1)}, u32[]{:S(2)}) copy-start(bf16[6144,128]{1,0:T(8,128)(2,1)} %param.13) | copy-start | bytes 4718596
  6.5 54.6 %copy-start.6 = (bf16[4096,128]{1,0:T(8,128)(2,1)S(1)}, bf16[4096,128]{1,0:T(8,128)(2,1)}, u32[]{:S(2)}) copy-start(bf16[4096,128]{1,0:T(8,128)(2,1)} %param.12) | copy-start | bytes 3145732
  6.5 54.6 %copy-start.7 = (f32[4096]{0:T(1024)S(1)}, f32[4096]{0:T(1024)}, u32[]{:S(2)}) copy-start(f32[4096]{0:T(1024)} %param.11) | copy-start | bytes 49156
  6.5 94.7 %all-gather.3.cloned.1.call-start = ((), (), s32[]{:S(2)}) async-start(), calls=%async_computation.5 | async-start | bytes 3538944 | tf_op jit(solution)/shard_map/all_gather | solution.py:24
  59.0 107.4 %reduce-scatter.3.cloned.1.call-start = ((), (), s32[]{:S(2)}) async-start(), calls=%async_computation.3 | async-start | bytes 2359296 | tf_op jit(solution)/shard_map/reduce_scatter | solution.py:41
  101.3 2.9 %copy-start.2 = (bf16[32,256,1,192]{1,3,2,0:T(8,128)(2,1)S(1)}, bf16[32,256,1,192]{1,3,2,0:T(8,128)(2,1)}, u32[]{:S(2)}) copy-start(bf16[32,256,1,192]{1,3,2,0:T(8,128)(2,1)} %all-gather.3.cloned.1.call-done) | copy-start | bytes 9437188
  105.6 0.9 copy-start.5
  106.5 2.7 %copy-start.3 = (bf16[6144,128]{1,0:T(8,128)(2,1)S(1)}, bf16[6144,128]{1,0:T(8,128)(2,1)}, u32[]{:S(2)}) copy-start(bf16[6144,128]{1,0:T(8,128)(2,1)} %param.14) | copy-start | bytes 4718596
  107.5 1.7 copy-start.1
  110.2 3.2 %copy-start.4 = (bf16[128,4096]{1,0:T(8,128)(2,1)S(1)}, bf16[128,4096]{1,0:T(8,128)(2,1)}, u32[]{:S(2)}) copy-start(bf16[128,4096]{1,0:T(8,128)(2,1)} %param.15) | copy-start | bytes 3145732
  118.9 81.7 %reduce-scatter.5.cloned.1.call-start = ((), (), s32[]{:S(2)}) async-start(), calls=%async_computation.4 | async-start | bytes 327680 | tf_op jit(solution)/shard_map/reduce_scatter | solution.py:41
Sparse Core Ops, SparseCore 0:
  59.1 42.0 all-gather.2
  119.0 47.3 reduce-scatter.2
  169.8 30.6 reduce-scatter.4
where the time goes:
time: 209 us
  waiting for transfers between devices  119 us (57%)
  blocking collectives  51.2 us (24%)
  between operations  13.2 us (6%)
  other arithmetic  9.2 us (4%)
  matrix products  8.8 us (4%)
  local copies, waits for them, and re-layouts  6.73 us (3%)
    reduce_scatter x2, waiting for transfers between devices, reduced_to_own(): blocks = lax.psum_scatter(blocks, axes[k], scatter_dimension=0, tiled=True)  81.6 us
    all_gather x1, waiting for transfers between devices, all_blocks(): blocks = lax.all_gather(blocks, axes[k])  37.7 us
    all_to_all x1, blocking collectives, body(): lax.all_to_all(visual, 'dp', split_axis=1, concat_axis=0, tiled=True)  35.6 us
    all_gather x1, blocking collectives, all_blocks(): blocks = lax.all_gather(blocks, axes[k])  15.5 us
  transfers between devices with their start and end apart: 3, of which 3 were waited for; matrix products, arithmetic and copies ran while one was open for 2% of the time, Pallas kernels for 0%

commit v1 on v0

v1 whole, which is shorter than its diff:
```python
import jax
import jax.numpy as jnp
from jax import lax
from jax.sharding import Mesh
from jax.sharding import PartitionSpec as P


DEC = 4096
HEAD_DIM = 128
MP = ("mp_0", "mp_1")
SCALE = 8192.0

epsilon = 1e-06


def attend(visual, vis_gain, text, text_gain, query_weight, key_weight, value_weight, out_weight):
    rows, cols = lax.axis_size("mp_0"), lax.axis_size("mp_1")
    devices = rows * cols
    scaled = (visual.astype(jnp.float32) * SCALE).astype(jnp.float16)
    relayed = lax.all_to_all(scaled, "dp", split_axis=1, concat_axis=0, tiled=True)
    vis_tokens, _, features = relayed.shape
    block = relayed.reshape(vis_tokens, features).T
    column = lax.all_to_all(jnp.broadcast_to(block, (rows, features, vis_tokens)), "mp_0", 0, 0, tiled=True)
    row = lax.axis_index("mp_0")
    width = DEC // rows
    column, out_weight = lax.optimization_barrier((column, out_weight))
    out_rows = []
    for step in range(rows):
        chunk = lax.dynamic_slice_in_dim(out_weight, (row ^ step) * width, width, 1)
        out_rows.append(lax.ppermute(chunk, "mp_0", [(k, k ^ step) for k in range(rows)]) if step else chunk)
    whole = lax.all_gather(column.reshape(rows * features, vis_tokens), "mp_1", axis=0, tiled=True)
    whole = whole.reshape(cols, rows, features, vis_tokens).transpose(1, 0, 2, 3)
    whole = whole.reshape(devices * features, vis_tokens).astype(jnp.float32)
    centred = whole - jnp.mean(whole, axis=0, keepdims=True)
    spread = jnp.mean(centred * centred, axis=0, keepdims=True)
    normed = (centred * lax.rsqrt(spread + epsilon * SCALE * SCALE) * vis_gain[:, None]).astype(jnp.bfloat16)
    keys = lax.dot_general(
        normed, key_weight, (((0,), (0,)), ((), ())), preferred_element_type=jnp.float32
    ).astype(jnp.bfloat16)
    values = lax.dot_general(
        normed, value_weight, (((0,), (0,)), ((), ())), preferred_element_type=jnp.float32
    ).astype(jnp.bfloat16)
    text_tokens = text.shape[0]
    flat = text.reshape(text_tokens, DEC)
    text_f = flat.astype(jnp.float32)
    text_norm = (
        text_f * lax.rsqrt(jnp.mean(text_f * text_f, axis=-1, keepdims=True) + epsilon) * text_gain
    ).astype(jnp.bfloat16)
    queries = jnp.dot(text_norm, query_weight, preferred_element_type=jnp.float32).astype(jnp.bfloat16)
    scores = jnp.einsum("td,vd->tv", queries, keys, preferred_element_type=jnp.float32) / jnp.sqrt(
        jnp.float32(HEAD_DIM)
    )
    probs = jax.nn.softmax(scores, axis=-1).astype(jnp.bfloat16)
    context = jnp.einsum("tv,vd->td", probs, values, preferred_element_type=jnp.float32).astype(jnp.bfloat16)
    group = lax.all_to_all(jnp.broadcast_to(context, (rows, *context.shape)), "mp_0", 0, 0, tiled=True)
    group = jnp.concatenate([lax.dynamic_index_in_dim(group, row ^ k, 0, False) for k in range(rows)], axis=1)
    part = jnp.dot(group, jnp.concatenate(out_rows), preferred_element_type=jnp.float32).astype(jnp.bfloat16)
    tokens_here = text_tokens // devices
    parts = lax.all_to_all(part.reshape(devices, tokens_here, DEC // rows), MP, 0, 0, tiled=True)
    summed = jnp.sum(parts.reshape(rows, cols, tokens_here, DEC // rows).astype(jnp.float32), axis=1)
    summed = summed.transpose(1, 0, 2).reshape(tokens_here, DEC)
    residual = lax.dynamic_slice_in_dim(flat, lax.axis_index(MP) * tokens_here, tokens_here, 0)
    return (residual.astype(jnp.float32) + summed).astype(jnp.bfloat16).reshape(tokens_here, 1, DEC)


def solution(mesh):
    split = Mesh(mesh.devices.reshape(mesh.shape["dp"], 4, 8), ("dp", "mp_0", "mp_1"))
    in_specs = (
        P("dp", None, MP),
        P(),
        P(None, "dp", None),
        P(),
        P(None, MP),
        P(None, MP),
        P(None, MP),
        P(MP, None),
    )
    out_specs = P(MP, "dp", None)
    return jax.shard_map(attend, mesh=split, in_specs=in_specs, out_specs=out_specs, check_vma=False)
```

time: 209 us -> 161 us (0.77)
  waiting for transfers between devices: 119 us -> 37.3 us
  starting transfers between devices: 0.09 us -> 27.1 us
  blocking collectives: 51.2 us -> 70.8 us
  between operations: 13.2 us -> 0.21 us
    reduce_scatter x2 -> x0, waiting for transfers between devices: 81.6 us -> none  [reduced_to_own(): blocks = lax.psum_scatter(blocks, axes[k], scatter_dimension=0, tiled=True)]
    all_gather x1 -> x0, waiting for transfers between devices: 37.7 us -> none  [all_blocks(): blocks = lax.all_gather(blocks, axes[k])]
    all_to_all x0 -> x3, waiting for transfers between devices: none -> 21.7 us  [the longest x1 14.8 us: attend(): lax.all_to_all(part.reshape(devices, tokens_here, DEC // rows), MP, 0, 0,...]
    all_gather x1, blocking collectives: 15.5 us -> 35.2 us  [attend(): lax.all_gather(column.reshape(rows * features, vis_tokens), 'mp_1', axis=...]
    all_to_all x0 -> x3, starting transfers between devices: none -> 17 us  [the longest x1 10.1 us: attend(): lax.all_to_all(part.reshape(devices, tokens_here, DEC // rows), MP, 0, 0,...]
    ppermute x0 -> x3, waiting for transfers between devices: none -> 15.6 us  [attend(): lax.ppermute(chunk, 'mp_0', [(k, k ^ step) for k in range(rows)])]
    ppermute x0 -> x3, starting transfers between devices: none -> 10.1 us  [attend(): lax.ppermute(chunk, 'mp_0', [(k, k ^ step) for k in range(rows)])]
    transpose x1, local copies, waits for them, and re-layouts: 3.16 us -> 0.15 us  [attend(): block = relayed.reshape(vis_tokens, features).T]
  transfers between devices with their start and end apart: 3 -> 6, of which waited for: 3 -> 4; matrix products, arithmetic and copies ran while one was open for 2% -> 3% of each run, Pallas kernels for 0% -> 0%
where the time goes in v1:
time: 161 us
  blocking collectives  70.8 us (44%)
  waiting for transfers between devices  37.3 us (23%)
  starting transfers between devices  27.1 us (17%)
  matrix products  9.2 us (6%)
  other arithmetic  8.88 us (6%)
  local copies, waits for them, and re-layouts  4.99 us (3%)
  Pallas kernels  2 us (1%)
    all_to_all x1, blocking collectives, attend(): lax.all_to_all(scaled, 'dp', split_axis=1, concat_axis=0, tiled=True)  35.6 us
    all_gather x1, blocking collectives, attend(): lax.all_gather(column.reshape(rows * features, vis_tokens), 'mp_1', axis=...  35.2 us
    ppermute x3, waiting for transfers between devices, attend(): lax.ppermute(chunk, 'mp_0', [(k, k ^ step) for k in range(rows)])  15.6 us
    all_to_all x1, waiting for transfers between devices, attend(): lax.all_to_all(part.reshape(devices, tokens_here, DEC // rows), MP, 0, 0,...  14.8 us
    all_to_all x1, starting transfers between devices, attend(): lax.all_to_all(part.reshape(devices, tokens_here, DEC // rows), MP, 0, 0,...  10.1 us
    ppermute x3, starting transfers between devices, attend(): lax.ppermute(chunk, 'mp_0', [(k, k ^ step) for k in range(rows)])  10.1 us
    all_to_all x1, waiting for transfers between devices, attend(): lax.all_to_all(jnp.broadcast_to(block, (rows, features, vis_tokens)), 'mp...  6.91 us
    dot_general x1, matrix products, attend(): jnp.einsum('td,vd->tv', queries, keys, preferred_element_type=jnp.float32)  3.9 us
  transfers between devices with their start and end apart: 6, of which 4 were waited for; matrix products, arithmetic and copies ran while one was open for 3% of the time, Pallas kernels for 0%

profile of v1, /device:TPU:2, one launch (start us, length us, event | category | flops | bytes accessed | tf_op | source)
XLA Modules:
  0.0 160.5 jit_solution(17960562064565475735)
XLA Ops:
  0.0 0.0 copy-start
  0.0 0.0 copy-start.6
  0.0 0.0 copy-start.5
  0.0 1.1 multiply_convert_fusion
  1.2 35.6 %all_to_all.30 = f16[8,32,192]{2,0,1:T(8,128)(2,1)S(1)} all-to-all(f16[8,32,192]{2,0,1:T(8,128)(2,1)S(1)} %multiply_convert_fusion), channel_id=1, replica_groups=mesh['dp'=32,'mp_0'=4,'mp_1'=8] {'dp'}, dimensions={1} | all-to-all | bytes 196608 | tf_op jit(solution)/shard_map/all_to_all | solution.py:20
  36.8 0.1 copy.16
  36.9 0.8 broadcast_in_dim.4
  37.7 3.5 %all-to-all-start.1 = ((f16[4,192,256]{2,1,0:T(8,128)(2,1)}), f16[4,192,256]{2,1,0:T(8,128)(2,1)S(1)}, u32[]{:S(2)}, u32[]{:S(2)}) async-start(f16[4,192,256]{2,1,0:T(8,128)(2,1)} %broadcast_in_dim.4), calls=%async_computation.1 | async-start | bytes 786432 | tf_op jit(solution)/shard_map/all_to_all | solution.py:23
  41.2 2.1 %fusion.3 = f32[256]{0:T(256)S(1)} fusion(bf16[256,1,4096]{2,0,1:T(8,128)(2,1)} %param.10), kind=kLoop, calls=%fused_computation.7 | loop fusion | flops 3145472 | bytes 2098176 | tf_op jit(solution)/shard_map/reduce_sum | solution.py:47
  43.3 0.0 copy-done.6
  43.3 0.0 copy-done.5
  43.3 2.4 %fusion.12 = bf16[256,128]{1,0:T(8,128)(2,1)S(1)} fusion(bf16[4096,128]{1,0:T(8,128)(2,1)S(1)} %copy-done.5, bf16[256,1,4096]{2,0,1:T(8,128)(2,1)} %param.10, f32[4096]{0:T(1024)S(1)} %copy-done.6, f32[256]{0:T(256)S(1)} %add_rsqrt_fusion.1), kind=kOutput, calls=%fused_computation.18 | convolution fusion | flops 272662528 | bytes 3228672 | tf_op jit(solution)/shard_map/dot_general | solution.py:49
  45.7 6.9 %all-to-all-done.1 = f16[4,192,256]{2,1,0:T(8,128)(2,1)S(1)} async-done(((f16[4,192,256]{2,1,0:T(8,128)(2,1)}), f16[4,192,256]{2,1,0:T(8,128)(2,1)S(1)}, u32[]{:S(2)}, u32[]{:S(2)}) %all-to-all-start.1) | async-done | bytes 393248 | tf_op jit(solution)/shard_map/all_to_all | solution.py:23
  52.6 35.2 %all-gather.1 = f16[6144,256]{1,0:T(8,128)(2,1)S(1)} all-gather(f16[768,256]{1,0:T(8,128)(2,1)S(1)} %bitcast.52), channel_id=1, replica_groups=mesh['dp'=32,'mp_0'=4,'mp_1'=8] {'mp_1'}, dimensions={0}, use_global_device_ids=true | all-gather | bytes 3538944 | tf_op jit(solution)/shard_map/all_gather | solution.py:31
  87.8 0.5 convert_element_type.96
  88.3 0.8 convert_reduce_fusion
  89.2 0.8 multiply_reduce_fusion
  90.0 0.0 copy-start.4
  90.0 0.7 copy.17
  90.7 0.0 copy-done.4
  90.8 0.0 copy-start.2
  90.8 1.0 fusion.2
  91.7 0.0 copy-start.1
  91.8 1.6 %copy-done.1 = bf16[6144,256]{1,0:T(8,128)(2,1)} copy-done((bf16[6144,256]{1,0:T(8,128)(2,1)}, bf16[6144,256]{1,0:T(8,128)(2,1)S(1)}, u32[]{:S(2)}) %copy-start.1) | copy-done | bytes 3145752
  93.4 0.0 copy-done.2
  93.4 1.7 %fusion.30 = f32[256,128]{1,0:T(8,128)} fusion(bf16[6144,256]{1,0:T(8,128)(2,1)S(1)} %fusion.2, bf16[6144,128]{1,0:T(8,128)(2,1)S(1)} %copy-done.2), kind=kOutput, calls=%fused_computation.49 | convolution fusion | flops 402653184 | bytes 4849664 | tf_op jit(solution)/shard_map/dot_general | solution.py:40
  95.1 0.0 copy-done
  95.1 0.0 copy-start.3
  95.1 3.9 %convolution_multiply_fusion = f32[256,256]{1,0:T(8,128)} fusion(bf16[256,128]{1,0:T(8,128)(2,1)S(1)} %fusion.12, bf16[6144,256]{1,0:T(8,128)(2,1)} %copy-done.1, bf16[6144,128]{1,0:T(8,128)(2,1)S(1)} %copy-done), kind=kOutput, calls=%fused_computation.17 | convolution fusion | flops 419528704 | bytes 5046272 | tf_op jit(solution)/shard_map/td,vd->tv/dot_general | solution.py:50
  99.0 2.0 %online-softmax = f32[256,128]{1,0:T(8,128)} custom-call(f32[256,256]{1,0:T(8,128)} %convolution_multiply_fusion, f32[256,128]{1,0:T(8,128)} %fusion.30), custom_call_target="tpu_custom_call" | custom-call | tf_op online-softmax
  101.0 0.9 convert_element_type.87
  101.9 0.7 broadcast_in_dim.5
  102.6 3.4 %all-to-all-start.2 = ((bf16[4,256,128]{2,1,0:T(8,128)(2,1)}), bf16[4,256,128]{2,1,0:T(8,128)(2,1)S(1)}, u32[]{:S(2)}, u32[]{:S(2)}) async-start(bf16[4,256,128]{2,1,0:T(8,128)(2,1)} %broadcast_in_dim.5), calls=%async_computation.2 | async-start | bytes 524288 | tf_op jit(solution)/shard_map/all_to_all | solution.py:55
  106.1 0.0 copy-done.3
  106.1 0.9 constant_dynamic-slice_fusion.3
  107.0 3.8 %collective-permute-start = (bf16[128,1024]{1,0:T(8,128)(2,1)}, bf16[128,1024]{1,0:T(8,128)(2,1)S(1)}, u32[]{:S(2)}, u32[]{:S(2)}) collective-permute-start(bf16[128,1024]{1,0:T(8,128)(2,1)} %get-tuple-element.12), channel_id=1, source_target_pairs={{0,8},{8,0},{16,24},{24,16},{1,9},{9,1},{17,25},{25,17},{2,10},{10... | collective-permute-start | bytes 786440 | tf_op jit(solution)/shard_map/ppermute | solution.py:30
  110.8 4.3 %collective-permute-start.1 = (bf16[128,1024]{1,0:T(8,128)(2,1)}, bf16[128,1024]{1,0:T(8,128)(2,1)S(1)}, u32[]{:S(2)}, u32[]{:S(2)}) collective-permute-start(bf16[128,1024]{1,0:T(8,128)(2,1)} %get-tuple-element.11), channel_id=1, source_target_pairs={{0,16},{8,24},{16,0},{24,8},{1,17},{9,25},{17,1},{25,9},{2,18},{10... | collective-permute-start | bytes 786440 | tf_op jit(solution)/shard_map/ppermute | solution.py:30
  115.1 2.0 %collective-permute-start.2 = (bf16[128,1024]{1,0:T(8,128)(2,1)S(1)}, bf16[128,1024]{1,0:T(8,128)(2,1)S(1)}, u32[]{:S(2)}, u32[]{:S(2)}) collective-permute-start(bf16[128,1024]{1,0:T(8,128)(2,1)S(1)} %get-tuple-element.10), channel_id=1, source_target_pairs={{0,24},{8,16},{16,8},{24,0},{1,25},{9,17},{17,9},{25,1},{2,26},{10... | collective-permute-start | bytes 786440 | tf_op jit(solution)/shard_map/ppermute | solution.py:30
  117.1 0.0 all-to-all-done.2
  117.2 2.2 %collective-permute-done = bf16[128,1024]{1,0:T(8,128)(2,1)S(1)} collective-permute-done((bf16[128,1024]{1,0:T(8,128)(2,1)}, bf16[128,1024]{1,0:T(8,128)(2,1)S(1)}, u32[]{:S(2)}, u32[]{:S(2)}) %collective-permute-start) | collective-permute-done | bytes 262176 | tf_op jit(solution)/shard_map/ppermute | solution.py:30
  119.4 13.4 %collective-permute-done.1 = bf16[128,1024]{1,0:T(8,128)(2,1)S(1)} collective-permute-done((bf16[128,1024]{1,0:T(8,128)(2,1)}, bf16[128,1024]{1,0:T(8,128)(2,1)S(1)}, u32[]{:S(2)}, u32[]{:S(2)}) %collective-permute-start.1) | collective-permute-done | bytes 262176 | tf_op jit(solution)/shard_map/ppermute | solution.py:30
  132.8 0.0 collective-permute-done.2
  132.8 1.2 fusion.11
  134.0 10.1 %all-to-all-start.3 = ((bf16[32,8,1024]{2,1,0:T(8,128)(2,1)}), bf16[32,8,1024]{2,1,0:T(8,128)(2,1)S(1)}, u32[]{:S(2)}, u32[]{:S(2)}) async-start(bf16[32,8,1024]{2,1,0:T(8,128)(2,1)} %fusion.11), calls=%async_computation.3 | async-start | bytes 1048576 | tf_op jit(solution)/shard_map/all_to_all | solution.py:59
  144.1 14.8 %all-to-all-done.3 = bf16[32,8,1024]{2,1,0:T(8,128)(2,1)S(1)} async-done(((bf16[32,8,1024]{2,1,0:T(8,128)(2,1)}), bf16[32,8,1024]{2,1,0:T(8,128)(2,1)S(1)}, u32[]{:S(2)}, u32[]{:S(2)}) %all-to-all-start.3) | async-done | bytes 524320 | tf_op jit(solution)/shard_map/all_to_all | solution.py:59
  159.0 0.1 convert_reduce_fusion.1
  159.0 1.5 add_convert_fusion
  (4 shorter events, 0.1 us)
Async XLA Ops:
  0.0 95.1 %copy-start = (bf16[6144,128]{1,0:T(8,128)(2,1)S(1)}, bf16[6144,128]{1,0:T(8,128)(2,1)}, u32[]{:S(2)}) copy-start(bf16[6144,128]{1,0:T(8,128)(2,1)} %param.13) | copy-start | bytes 4718596
  0.0 43.3 %copy-start.6 = (f32[4096]{0:T(1024)S(1)}, f32[4096]{0:T(1024)}, u32[]{:S(2)}) copy-start(f32[4096]{0:T(1024)} %param.11) | copy-start | bytes 49156
  0.0 43.3 %copy-start.5 = (bf16[4096,128]{1,0:T(8,128)(2,1)S(1)}, bf16[4096,128]{1,0:T(8,128)(2,1)}, u32[]{:S(2)}) copy-start(bf16[4096,128]{1,0:T(8,128)(2,1)} %param.12) | copy-start | bytes 3145732
  37.7 14.9 %all-to-all-start.1 = ((f16[4,192,256]{2,1,0:T(8,128)(2,1)}), f16[4,192,256]{2,1,0:T(8,128)(2,1)S(1)}, u32[]{:S(2)}, u32[]{:S(2)}) async-start(f16[4,192,256]{2,1,0:T(8,128)(2,1)} %broadcast_in_dim.4), calls=%async_computation.1 | async-start | bytes 786432 | tf_op jit(solution)/shard_map/all_to_all | solution.py:23
  90.0 0.7 copy-start.4
  90.8 2.6 %copy-start.2 = (bf16[6144,128]{1,0:T(8,128)(2,1)S(1)}, bf16[6144,128]{1,0:T(8,128)(2,1)}, u32[]{:S(2)}) copy-start(bf16[6144,128]{1,0:T(8,128)(2,1)} %param.14) | copy-start | bytes 4718596
  91.7 1.7 %copy-start.1 = (bf16[6144,256]{1,0:T(8,128)(2,1)}, bf16[6144,256]{1,0:T(8,128)(2,1)S(1)}, u32[]{:S(2)}) copy-start(bf16[6144,256]{1,0:T(8,128)(2,1)S(1)} %fusion.2) | copy-start | bytes 9437188
  95.1 11.0 %copy-start.3 = (bf16[128,4096]{1,0:T(8,128)(2,1)S(1)}, bf16[128,4096]{1,0:T(8,128)(2,1)}, u32[]{:S(2)}) copy-start(bf16[128,4096]{1,0:T(8,128)(2,1)} %param.15) | copy-start | bytes 3145732
  102.6 14.5 %all-to-all-start.2 = ((bf16[4,256,128]{2,1,0:T(8,128)(2,1)}), bf16[4,256,128]{2,1,0:T(8,128)(2,1)S(1)}, u32[]{:S(2)}, u32[]{:S(2)}) async-start(bf16[4,256,128]{2,1,0:T(8,128)(2,1)} %broadcast_in_dim.5), calls=%async_computation.2 | async-start | bytes 524288 | tf_op jit(solution)/shard_map/all_to_all | solution.py:55
  107.0 12.4 %collective-permute-start = (bf16[128,1024]{1,0:T(8,128)(2,1)}, bf16[128,1024]{1,0:T(8,128)(2,1)S(1)}, u32[]{:S(2)}, u32[]{:S(2)}) collective-permute-start(bf16[128,1024]{1,0:T(8,128)(2,1)} %get-tuple-element.12), channel_id=1, source_target_pairs={{0,8},{8,0},{16,24},{24,16},{1,9},{9,1},{17,25},{25,17},{2,10},{10... | collective-permute-start | bytes 786440 | tf_op jit(solution)/shard_map/ppermute | solution.py:30
  110.8 22.0 %collective-permute-start.1 = (bf16[128,1024]{1,0:T(8,128)(2,1)}, bf16[128,1024]{1,0:T(8,128)(2,1)S(1)}, u32[]{:S(2)}, u32[]{:S(2)}) collective-permute-start(bf16[128,1024]{1,0:T(8,128)(2,1)} %get-tuple-element.11), channel_id=1, source_target_pairs={{0,16},{8,24},{16,0},{24,8},{1,17},{9,25},{17,1},{25,9},{2,18},{10... | collective-permute-start | bytes 786440 | tf_op jit(solution)/shard_map/ppermute | solution.py:30
  115.1 17.7 %collective-permute-start.2 = (bf16[128,1024]{1,0:T(8,128)(2,1)S(1)}, bf16[128,1024]{1,0:T(8,128)(2,1)S(1)}, u32[]{:S(2)}, u32[]{:S(2)}) collective-permute-start(bf16[128,1024]{1,0:T(8,128)(2,1)S(1)} %get-tuple-element.10), channel_id=1, source_target_pairs={{0,24},{8,16},{16,8},{24,0},{1,25},{9,17},{17,9},{25,1},{2,26},{10... | collective-permute-start | bytes 786440 | tf_op jit(solution)/shard_map/ppermute | solution.py:30
  134.0 24.9 %all-to-all-start.3 = ((bf16[32,8,1024]{2,1,0:T(8,128)(2,1)}), bf16[32,8,1024]{2,1,0:T(8,128)(2,1)S(1)}, u32[]{:S(2)}, u32[]{:S(2)}) async-start(bf16[32,8,1024]{2,1,0:T(8,128)(2,1)} %fusion.11), calls=%async_computation.3 | async-start | bytes 1048576 | tf_op jit(solution)/shard_map/all_to_all | solution.py:59

commit v2 on v1

v2 whole, which is shorter than its diff:
```python
import jax
import jax.numpy as jnp
from jax import lax
from jax.experimental import pallas as pl
from jax.experimental.pallas import tpu as pltpu
from jax.sharding import Mesh
from jax.sharding import PartitionSpec as P


DEC = 4096
HEAD_DIM = 128
DP = ("dp_0", "dp_1")
ROW = ("row_0", "row_1")
COL = ("col_0", "col_1")
MP = ROW + COL
QUAD = ("row_1", "col_1")
LANES = 128
CHUNK = 64
SCALE = 8192.0

epsilon = 1e-06


def attention_kernel(whole_ref, gain_ref, key_ref, value_ref, queries_ref, contexts_ref, normed_ref, scale_ref):
    cols, tokens, depth = whole_ref.shape
    rows = key_ref.shape[0] // cols
    count = cols * depth
    places = [(c, pl.ds(k, LANES)) for c in range(cols) for k in range(0, depth, LANES)]

    def normalize(step, carry):
        here = pl.ds(pl.multiple_of(step * CHUNK, CHUNK), CHUNK)
        sums = jnp.zeros((CHUNK, LANES), jnp.float32)
        for c, k in places:
            sums += whole_ref[c, here, k].astype(jnp.float32)
        mean = jnp.sum(sums, axis=1, keepdims=True) / count
        squares = jnp.zeros((CHUNK, LANES), jnp.float32)
        for c, k in places:
            centred = whole_ref[c, here, k].astype(jnp.float32) - mean
            squares += centred * centred
            normed_ref[c, here, k] = (centred * gain_ref[c : c + 1, k]).astype(jnp.bfloat16)
        spread = jnp.sum(squares, axis=1, keepdims=True) / count
        scale_ref[here, :] = jnp.broadcast_to(lax.rsqrt(spread + epsilon * SCALE * SCALE), (CHUNK, LANES))
        return carry

    lax.fori_loop(0, tokens // CHUNK, normalize, 0)
    projected = jnp.zeros((tokens, 2 * HEAD_DIM), jnp.float32)
    for c in range(cols):
        both = [jnp.concatenate([ref[r * cols + c] for r in range(rows)], axis=0) for ref in (key_ref, value_ref)]
        projected += jnp.dot(normed_ref[c], jnp.concatenate(both, axis=1), preferred_element_type=jnp.float32)
    keys = (projected[:, :HEAD_DIM] * scale_ref[...]).astype(jnp.bfloat16)
    values = (projected[:, HEAD_DIM:] * scale_ref[...]).astype(jnp.bfloat16)
    scores = lax.dot_general(queries_ref[...], keys, (((1,), (1,)), ((), ())), preferred_element_type=jnp.float32)
    scores *= HEAD_DIM**-0.5
    weights = jnp.exp(scores - jnp.max(scores, axis=1, keepdims=True))
    probs = (weights / jnp.sum(weights, axis=1, keepdims=True)).astype(jnp.bfloat16)
    context = jnp.dot(probs, values, preferred_element_type=jnp.float32).astype(jnp.bfloat16)
    for k in range(contexts_ref.shape[0]):
        contexts_ref[k] = context


def attend(visual, vis_gain, text, text_gain, query_weight, key_weight, value_weight, out_weight):
    rows, cols, quad = (lax.axis_size(a) for a in (ROW, COL, QUAD))
    halves, planes = (lax.axis_size(a) for a in DP)
    devices = rows * cols
    tokens, _, features = visual.shape
    text_tokens = text.shape[0]
    scaled = (visual.astype(jnp.float32) * SCALE).astype(jnp.float16)
    scaled = scaled.reshape(tokens, halves, planes, features).transpose(2, 1, 0, 3)
    relayed = lax.all_to_all(scaled, "dp_1", 0, 0, tiled=True)
    half_tokens = planes * tokens
    blocks = relayed.transpose(1, 3, 0, 2).reshape(halves, 1, features, half_tokens)
    blocks = jnp.broadcast_to(blocks, (halves, rows, features, half_tokens))
    column = lax.all_to_all(
        blocks.reshape(halves * rows, features, half_tokens), ("dp_0",) + ROW, 0, 0, tiled=True
    )
    member = lax.axis_index(QUAD)
    width = DEC // quad
    out_rows = []
    for step in range(quad):
        chunk = lax.dynamic_slice_in_dim(out_weight, (member ^ step) * width, width, 1)
        out_rows.append(lax.ppermute(chunk, QUAD, [(k, k ^ step) for k in range(quad)]) if step else chunk)
    column = column.reshape(halves, rows * features, half_tokens).transpose(0, 2, 1)
    column = column.reshape(halves * half_tokens, rows * features)
    whole = lax.all_gather(column, COL, axis=0, tiled=True)
    whole = whole.astype(jnp.bfloat16).reshape(cols, halves * half_tokens, rows * features)
    flat = text.reshape(text_tokens, DEC)
    text_f = flat.astype(jnp.float32)
    text_norm = (
        text_f * lax.rsqrt(jnp.mean(text_f * text_f, axis=-1, keepdims=True) + epsilon) * text_gain
    ).astype(jnp.bfloat16)
    queries = jnp.dot(text_norm, query_weight, preferred_element_type=jnp.float32).astype(jnp.bfloat16)
    gain = vis_gain.reshape(rows, cols, features).transpose(1, 0, 2).reshape(cols, rows * features)
    in_vmem = [
        pltpu.with_memory_space_constraint(v, pltpu.VMEM)
        for v in (
            whole,
            gain,
            key_weight.reshape(devices, features, HEAD_DIM),
            value_weight.reshape(devices, features, HEAD_DIM),
            queries,
        )
    ]
    contexts = pl.pallas_call(
        attention_kernel,
        out_shape=jax.ShapeDtypeStruct((quad, text_tokens, HEAD_DIM), jnp.bfloat16),
        in_specs=[pl.BlockSpec(memory_space=pltpu.VMEM)] * len(in_vmem),
        out_specs=pl.BlockSpec(memory_space=pltpu.VMEM),
        scratch_shapes=[
            pltpu.VMEM(whole.shape, jnp.bfloat16),
            pltpu.VMEM((whole.shape[1], LANES), jnp.float32),
        ],
        compiler_params=pltpu.CompilerParams(vmem_limit_bytes=12 << 20),
        name="attention",
    )(*in_vmem)
    group = lax.all_to_all(contexts, QUAD, 0, 0, tiled=True)
    group = jnp.concatenate([lax.dynamic_index_in_dim(group, member ^ k, 0, False) for k in range(quad)], axis=1)
    part = jnp.dot(group, jnp.concatenate(out_rows), preferred_element_type=jnp.float32).astype(jnp.bfloat16)
    tokens_here = text_tokens // devices
    parts = lax.all_to_all(part.reshape(devices, tokens_here, width), MP, 0, 0, tiled=True)
    parts = parts.reshape(*(lax.axis_size(a) for a in MP), tokens_here, width)
    summed = jnp.sum(parts.astype(jnp.float32), axis=(0, 2))
    summed = summed.transpose(2, 0, 1, 3).reshape(tokens_here, DEC)
    residual = lax.dynamic_slice_in_dim(flat, lax.axis_index(MP) * tokens_here, tokens_here, 0)
    return (residual.astype(jnp.float32) + summed).astype(jnp.bfloat16).reshape(tokens_here, 1, DEC)


def solution(mesh):
    split = Mesh(mesh.devices.reshape(2, mesh.shape["dp"] // 2, 2, 2, 4, 2), DP + MP)
    in_specs = (
        P(DP, None, MP),
        P(),
        P(None, DP, None),
        P(),
        P(None, MP),
        P(None, MP),
        P(None, MP),
        P(MP, None),
    )
    out_specs = P(MP, DP, None)
    return jax.shard_map(attend, mesh=split, in_specs=in_specs, out_specs=out_specs, check_vma=False)
```

time: 161 us -> 147 us (0.913)
  blocking collectives: 70.8 us -> 35.4 us
  starting transfers between devices: 27.1 us -> 46.7 us
  waiting for transfers between devices: 37.3 us -> 44.4 us
  matrix products: 9.2 us -> 3.25 us
  other arithmetic: 8.88 us -> 3.85 us
  local copies, waits for them, and re-layouts: 4.99 us -> 8.3 us
  Pallas kernels: 2 us -> 4.2 us
    all_to_all x1 -> x0, blocking collectives: 35.6 us -> none  [attend(): lax.all_to_all(scaled, 'dp', split_axis=1, concat_axis=0, tiled=True)]
    all_to_all x3 -> x4, starting transfers between devices: 17 us -> 37.4 us  [the longest x1 16.9 us: attend(): relayed = lax.all_to_all(scaled, 'dp_1', 0, 0, tiled=True)]
    all_to_all x3 -> x4, waiting for transfers between devices: 21.7 us -> 37.5 us  [the longest x1 15.5 us: attend(): lax.all_to_all(part.reshape(devices, tokens_here, width), MP, 0, 0, tiled...]
    ppermute x3, waiting for transfers between devices: 15.6 us -> 6.91 us  [attend(): lax.ppermute(chunk, QUAD, [(k, k ^ step) for k in range(quad)])]
    dot_general x2 -> x0, matrix products: 5.58 us -> none  [the longest x1 3.9 us: attend(): jnp.einsum('td,vd->tv', queries, keys, preferred_element_type=jnp.float32)]
    pallas_call x0 -> x1, Pallas kernels: none -> 4.2 us  [attend(): pl.pallas_call(attention_kernel, out_shape=jax.ShapeDtypeStruct((quad, te...]
    transpose x1 -> x3, local copies, waits for them, and re-layouts: 0.15 us -> 2.76 us  [the longest x1 2.01 us: attend(): column.reshape(halves, rows * features, half_tokens).transpose(0, 2, 1)]
    unnamed x1 -> x0, Pallas kernels: 2 us -> none
  transfers between devices with their start and end apart: 6 -> 7, of which waited for: 4 -> 4; matrix products, arithmetic and copies ran while one was open for 3% -> 3% of each run, Pallas kernels for 0% -> 0%
where the time goes in v2:
time: 147 us; the launch traced here: 146 us
  starting transfers between devices  46.7 us (32%)
  waiting for transfers between devices  44.4 us (30%)
  blocking collectives  35.4 us (24%)
  local copies, waits for them, and re-layouts  8.3 us (6%)
  Pallas kernels  4.2 us (3%)
  other arithmetic  3.85 us (3%)
  matrix products  3.25 us (2%)
    all_gather x1, blocking collectives, attend(): whole = lax.all_gather(column, COL, axis=0, tiled=True)  35.4 us
    all_to_all x1, starting transfers between devices, attend(): relayed = lax.all_to_all(scaled, 'dp_1', 0, 0, tiled=True)  16.9 us
    all_to_all x1, waiting for transfers between devices, attend(): lax.all_to_all(part.reshape(devices, tokens_here, width), MP, 0, 0, tiled...  15.5 us
    all_to_all x1, waiting for transfers between devices, attend(): lax.all_to_all(blocks.reshape(halves * rows, features, half_tokens), ('dp...  14.3 us
    ppermute x3, starting transfers between devices, attend(): lax.ppermute(chunk, QUAD, [(k, k ^ step) for k in range(quad)])  9.2 us
    all_to_all x1, starting transfers between devices, attend(): lax.all_to_all(part.reshape(devices, tokens_here, width), MP, 0, 0, tiled...  8.65 us
    all_to_all x1, waiting for transfers between devices, attend(): relayed = lax.all_to_all(scaled, 'dp_1', 0, 0, tiled=True)  7.73 us
    all_to_all x1, starting transfers between devices, attend(): lax.all_to_all(blocks.reshape(halves * rows, features, half_tokens), ('dp...  7.56 us
  transfers between devices with their start and end apart: 7, of which 4 were waited for; matrix products, arithmetic and copies ran while one was open for 3% of the time, Pallas kernels for 0%

profile of v2, /device:TPU:2, one launch (start us, length us, event | category | flops | bytes accessed | tf_op | source)
XLA Modules:
  0.0 146.2 jit_solution(10509900570093581896)
XLA Ops:
  0.0 0.0 copy-start
  0.0 0.0 copy-start.3
  0.0 1.1 multiply_convert_fusion
  1.1 0.7 copy.20
  1.8 0.0 copy-start.4
  1.8 16.9 %all-to-all-start = ((f16[16,2,8,192]{3,2,1,0:T(8,128)(2,1)}), f16[16,2,8,192]{3,2,1,0:T(8,128)(2,1)S(1)}, u32[]{:S(2)}, u32[]{:S(2)}) async-start(f16[16,2,8,192]{3,2,1,0:T(8,128)(2,1)} %copy.20), calls=%async_computation | async-start | bytes 262144 | tf_op jit(solution)/shard_map/all_to_all | solution.py:69
  18.8 0.8 reshape.58
  19.6 0.1 reshape.59.gain_ref
  19.7 7.7 %all-to-all-done = f16[16,2,8,192]{3,2,1,0:T(8,128)(2,1)S(1)} async-done(((f16[16,2,8,192]{3,2,1,0:T(8,128)(2,1)}), f16[16,2,8,192]{3,2,1,0:T(8,128)(2,1)S(1)}, u32[]{:S(2)}, u32[]{:S(2)}) %all-to-all-start) | async-done | bytes 98336 | tf_op jit(solution)/shard_map/all_to_all | solution.py:69
  27.4 0.2 copy.22
  27.6 0.8 broadcast_in_dim.10
  28.4 7.6 %all-to-all-start.1 = ((f16[8,192,128]{2,1,0:T(8,128)(2,1)}), f16[8,192,128]{2,1,0:T(8,128)(2,1)}, u32[]{:S(2)}, u32[]{:S(2)}) async-start(f16[8,192,128]{2,1,0:T(8,128)(2,1)} %bitcast.46), calls=%async_computation.1 | async-start | bytes 786432 | tf_op jit(solution)/shard_map/all_to_all | solution.py:73
  36.0 0.0 copy-done.3
  36.0 0.5 fusion
  36.5 0.0 copy-done
  36.5 0.0 copy-done.4
  36.5 0.8 fusion.9.queries_ref
  37.3 14.3 %all-to-all-done.1 = f16[8,192,128]{2,1,0:T(8,128)(2,1)} async-done(((f16[8,192,128]{2,1,0:T(8,128)(2,1)}), f16[8,192,128]{2,1,0:T(8,128)(2,1)}, u32[]{:S(2)}, u32[]{:S(2)}) %all-to-all-start.1) | async-done | bytes 393248 | tf_op jit(solution)/shard_map/all_to_all | solution.py:73
  51.6 2.0 %copy.23 = f16[2,128,768]{2,1,0:T(8,128)(2,1)} copy(f16[2,128,768]{1,2,0:T(8,128)(2,1)} %bitcast.6) | data formatting | bytes 786432 | tf_op jit(solution)/shard_map/transpose | solution.py:82
  53.6 35.4 %all-gather.1 = f16[2048,768]{1,0:T(8,128)(2,1)S(1)} all-gather(f16[256,768]{1,0:T(8,128)(2,1)} %bitcast.45), channel_id=1, replica_groups=mesh['dp_0'=2,'dp_1'=16,'row_0'=2,'row_1'=2,'col_0'=4,'col_1'=2] {'col_0..., dimensions={0}, use_global_device_ids=true | all-gather | bytes 3538944 | tf_op jit(solution)/shard_map/all_gather | solution.py:84
  89.0 0.0 copy-start.1
  89.0 0.0 copy-start.2
  89.0 0.5 convert_element_type.41
  89.5 0.9 copy-done.1
  90.4 0.5 copy-done.2
  90.9 4.2 %attention.1 = bf16[4,256,128]{2,1,0:T(8,128)(2,1)} custom-call(bf16[8,256,768]{2,1,0:T(8,128)(2,1)S(1)} %bitcast.42, f32[8,768]{1,0:T(8,128)S(1)} %reshape.59.gain_ref, bf16[32,192,128]{2,1,0:T(8,128)(2,1)S(1)} %bitcast.43, bf16[32,192,128]{2,1,0:T(8,128)(2,1)S(1)} %bitcast.44, bf16[256,128]{1,0:T(8,128)(2,1)S(1)} %fusion.9.queries_ref), custom_call_target="tpu_custom_call" | custom-call | tf_op jit(solution)/shard_map/attention/pallas_call | solution.py:103
  95.1 4.3 %all-to-all-start.2 = ((bf16[4,256,128]{2,1,0:T(8,128)(2,1)}), bf16[4,256,128]{2,1,0:T(8,128)(2,1)S(1)}, u32[]{:S(2)}, u32[]{:S(2)}) async-start(bf16[4,256,128]{2,1,0:T(8,128)(2,1)} %attention.1), calls=%async_computation.2 | async-start | bytes 524288 | tf_op jit(solution)/shard_map/all_to_all | solution.py:115
  99.4 2.2 %constant_dynamic-slice_fusion.3 = (bf16[128,1024]{1,0:T(8,128)(2,1)}, bf16[128,1024]{1,0:T(8,128)(2,1)}, bf16[128,1024]{1,0:T(8,128)(2,1)}, bf16[128,1024]{1,0:T(8,128)(2,1)}) fusion(bf16[128,4096]{1,0:T(8,128)(2,1)} %param.15, s32[]{:T(128)S(6)} %select_n.33, s32[]{:T(128)S(6)} %select_n.34, s32[]{:T(128)S(6)} %select_n.36, s32[]{:T(128)S(6)} %select_n.35), kind=kLoop, calls=%fused_computation.37 | loop fusion | bytes 2097168 | tf_op jit(solution)/shard_map/dynamic_slice | solution.py:80
  101.6 2.0 %collective-permute-start = (bf16[128,1024]{1,0:T(8,128)(2,1)}, bf16[128,1024]{1,0:T(8,128)(2,1)}, u32[]{:S(2)}, u32[]{:S(2)}) collective-permute-start(bf16[128,1024]{1,0:T(8,128)(2,1)} %get-tuple-element.6), channel_id=1, source_target_pairs={{0,1},{1,0},{8,9},{9,8},{2,3},{3,2},{10,11},{11,10},{4,5},{5,4},{1... | collective-permute-start | bytes 786440 | tf_op jit(solution)/shard_map/ppermute | solution.py:81
  103.6 3.9 %collective-permute-start.1 = (bf16[128,1024]{1,0:T(8,128)(2,1)}, bf16[128,1024]{1,0:T(8,128)(2,1)}, u32[]{:S(2)}, u32[]{:S(2)}) collective-permute-start(bf16[128,1024]{1,0:T(8,128)(2,1)} %get-tuple-element.8), channel_id=1, source_target_pairs={{0,8},{1,9},{8,0},{9,1},{2,10},{3,11},{10,2},{11,3},{4,12},{5,13},... | collective-permute-start | bytes 786440 | tf_op jit(solution)/shard_map/ppermute | solution.py:81
  107.5 3.4 %collective-permute-start.2 = (bf16[128,1024]{1,0:T(8,128)(2,1)}, bf16[128,1024]{1,0:T(8,128)(2,1)}, u32[]{:S(2)}, u32[]{:S(2)}) collective-permute-start(bf16[128,1024]{1,0:T(8,128)(2,1)} %get-tuple-element.7), channel_id=1, source_target_pairs={{0,9},{1,8},{8,1},{9,0},{2,11},{3,10},{10,3},{11,2},{4,13},{5,12},... | collective-permute-start | bytes 786440 | tf_op jit(solution)/shard_map/ppermute | solution.py:81
  110.9 0.0 all-to-all-done.2
  110.9 0.0 collective-permute-done
  110.9 6.9 %collective-permute-done.1 = bf16[128,1024]{1,0:T(8,128)(2,1)} collective-permute-done((bf16[128,1024]{1,0:T(8,128)(2,1)}, bf16[128,1024]{1,0:T(8,128)(2,1)}, u32[]{:S(2)}, u32[]{:S(2)}) %collective-permute-start.1) | collective-permute-done | bytes 262176 | tf_op jit(solution)/shard_map/ppermute | solution.py:81
  117.8 0.0 collective-permute-done.2
  117.8 2.4 %fusion.8 = bf16[32,8,1024]{2,1,0:T(8,128)(2,1)} fusion(bf16[128,1024]{1,0:T(8,128)(2,1)} %collective-permute-done.2, bf16[128,1024]{1,0:T(8,128)(2,1)} %collective-permute-done.1, bf16[128,1024]{1,0:T(8,128)(2,1)} %collective-permute-done, bf16[128,1024]{1,0:T(8,128)(2,1)} %get-tuple-element.5, bf16[256,128]{1,0:T(8,128)(2,1)S(1)} %get-tuple-element.10, ...), kind=kOutput, calls=%fused_computation.10 | convolution fusion | flops 273940480 | bytes 1835008 | tf_op jit(solution)/shard_map/dot_general | solution.py:117
  120.3 8.6 %all-to-all-start.3 = ((bf16[32,8,1024]{2,1,0:T(8,128)(2,1)}), bf16[32,8,1024]{2,1,0:T(8,128)(2,1)}, u32[]{:S(2)}, u32[]{:S(2)}) async-start(bf16[32,8,1024]{2,1,0:T(8,128)(2,1)} %fusion.8), calls=%async_computation.3 | async-start | bytes 1048576 | tf_op jit(solution)/shard_map/all_to_all | solution.py:119
  128.9 15.5 %all-to-all-done.3 = bf16[32,8,1024]{2,1,0:T(8,128)(2,1)} async-done(((bf16[32,8,1024]{2,1,0:T(8,128)(2,1)}), bf16[32,8,1024]{2,1,0:T(8,128)(2,1)}, u32[]{:S(2)}, u32[]{:S(2)}) %all-to-all-start.3) | async-done | bytes 524320 | tf_op jit(solution)/shard_map/all_to_all | solution.py:119
  144.4 1.1 convert_reduce_fusion
  145.5 0.7 add_convert_fusion
  (4 shorter events, 0.1 us)
Async XLA Ops:
  0.0 36.5 %copy-start = (bf16[4096,128]{1,0:T(8,128)(2,1)S(1)}, bf16[4096,128]{1,0:T(8,128)(2,1)}, u32[]{:S(2)}) copy-start(bf16[4096,128]{1,0:T(8,128)(2,1)} %param.12) | copy-start | bytes 3145732
  0.0 36.0 %copy-start.3 = (bf16[256,1,4096]{2,0,1:T(8,128)(2,1)S(1)}, bf16[256,1,4096]{2,0,1:T(8,128)(2,1)}, u32[]{:S(2)}) copy-start(bf16[256,1,4096]{2,0,1:T(8,128)(2,1)} %param.10) | copy-start | bytes 6291460
  1.8 34.7 %copy-start.4 = (f32[4096]{0:T(1024)S(1)}, f32[4096]{0:T(1024)}, u32[]{:S(2)}) copy-start(f32[4096]{0:T(1024)} %param.11) | copy-start | bytes 49156
  1.8 25.6 %all-to-all-start = ((f16[16,2,8,192]{3,2,1,0:T(8,128)(2,1)}), f16[16,2,8,192]{3,2,1,0:T(8,128)(2,1)S(1)}, u32[]{:S(2)}, u32[]{:S(2)}) async-start(f16[16,2,8,192]{3,2,1,0:T(8,128)(2,1)} %copy.20), calls=%async_computation | async-start | bytes 262144 | tf_op jit(solution)/shard_map/all_to_all | solution.py:69
  28.4 23.2 %all-to-all-start.1 = ((f16[8,192,128]{2,1,0:T(8,128)(2,1)}), f16[8,192,128]{2,1,0:T(8,128)(2,1)}, u32[]{:S(2)}, u32[]{:S(2)}) async-start(f16[8,192,128]{2,1,0:T(8,128)(2,1)} %bitcast.46), calls=%async_computation.1 | async-start | bytes 786432 | tf_op jit(solution)/shard_map/all_to_all | solution.py:73
  89.0 1.4 copy-start.1
  89.0 1.9 %copy-start.2 = (bf16[6144,128]{1,0:T(8,128)(2,1)S(1)}, bf16[6144,128]{1,0:T(8,128)(2,1)}, u32[]{:S(2)}) copy-start(bf16[6144,128]{1,0:T(8,128)(2,1)} %param.14) | copy-start | bytes 4718596
  95.1 15.8 %all-to-all-start.2 = ((bf16[4,256,128]{2,1,0:T(8,128)(2,1)}), bf16[4,256,128]{2,1,0:T(8,128)(2,1)S(1)}, u32[]{:S(2)}, u32[]{:S(2)}) async-start(bf16[4,256,128]{2,1,0:T(8,128)(2,1)} %attention.1), calls=%async_computation.2 | async-start | bytes 524288 | tf_op jit(solution)/shard_map/all_to_all | solution.py:115
  101.6 9.3 %collective-permute-start = (bf16[128,1024]{1,0:T(8,128)(2,1)}, bf16[128,1024]{1,0:T(8,128)(2,1)}, u32[]{:S(2)}, u32[]{:S(2)}) collective-permute-start(bf16[128,1024]{1,0:T(8,128)(2,1)} %get-tuple-element.6), channel_id=1, source_target_pairs={{0,1},{1,0},{8,9},{9,8},{2,3},{3,2},{10,11},{11,10},{4,5},{5,4},{1... | collective-permute-start | bytes 786440 | tf_op jit(solution)/shard_map/ppermute | solution.py:81
  103.6 14.2 %collective-permute-start.1 = (bf16[128,1024]{1,0:T(8,128)(2,1)}, bf16[128,1024]{1,0:T(8,128)(2,1)}, u32[]{:S(2)}, u32[]{:S(2)}) collective-permute-start(bf16[128,1024]{1,0:T(8,128)(2,1)} %get-tuple-element.8), channel_id=1, source_target_pairs={{0,8},{1,9},{8,0},{9,1},{2,10},{3,11},{10,2},{11,3},{4,12},{5,13},... | collective-permute-start | bytes 786440 | tf_op jit(solution)/shard_map/ppermute | solution.py:81
  107.5 10.4 %collective-permute-start.2 = (bf16[128,1024]{1,0:T(8,128)(2,1)}, bf16[128,1024]{1,0:T(8,128)(2,1)}, u32[]{:S(2)}, u32[]{:S(2)}) collective-permute-start(bf16[128,1024]{1,0:T(8,128)(2,1)} %get-tuple-element.7), channel_id=1, source_target_pairs={{0,9},{1,8},{8,1},{9,0},{2,11},{3,10},{10,3},{11,2},{4,13},{5,12},... | collective-permute-start | bytes 786440 | tf_op jit(solution)/shard_map/ppermute | solution.py:81
  120.3 24.1 %all-to-all-start.3 = ((bf16[32,8,1024]{2,1,0:T(8,128)(2,1)}), bf16[32,8,1024]{2,1,0:T(8,128)(2,1)}, u32[]{:S(2)}, u32[]{:S(2)}) async-start(bf16[32,8,1024]{2,1,0:T(8,128)(2,1)} %fusion.8), calls=%async_computation.3 | async-start | bytes 1048576 | tf_op jit(solution)/shard_map/all_to_all | solution.py:119

commit v3 on v2

--- a/solution.py
+++ b/solution.py
@@ -21,7 +21,23 @@
 epsilon = 1e-06
 
 
-def attention_kernel(whole_ref, gain_ref, key_ref, value_ref, queries_ref, contexts_ref, normed_ref, scale_ref):
+def attention_kernel(
+    whole_ref,
+    gain_ref,
+    queries_ref,
+    key_hbm_ref,
+    value_hbm_ref,
+    contexts_ref,
+    key_ref,
+    value_ref,
+    semaphores,
+    normed_ref,
+    scale_ref,
+):
+    key_copy = pltpu.make_async_copy(key_hbm_ref, key_ref, semaphores.at[0])
+    value_copy = pltpu.make_async_copy(value_hbm_ref, value_ref, semaphores.at[1])
+    key_copy.start()
+    value_copy.start()
     cols, tokens, depth = whole_ref.shape
     rows = key_ref.shape[0] // cols
     count = cols * depth
@@ -43,6 +59,8 @@
         return carry
 
     lax.fori_loop(0, tokens // CHUNK, normalize, 0)
+    key_copy.wait()
+    value_copy.wait()
     projected = jnp.zeros((tokens, 2 * HEAD_DIM), jnp.float32)
     for c in range(cols):
         both = [jnp.concatenate([ref[r * cols + c] for r in range(rows)], axis=0) for ref in (key_ref, value_ref)]
@@ -58,70 +76,101 @@
         contexts_ref[k] = context
 
 
+def project_kernel(member_ref, group_ref, *refs):
+    *chunk_refs, part_ref = refs
+    part = jnp.zeros(part_ref.shape, jnp.float32)
+    for k, chunk_ref in enumerate(chunk_refs):
+        part += jnp.dot(group_ref[member_ref[0] ^ k], chunk_ref[...], preferred_element_type=jnp.float32)
+    part_ref[...] = part.astype(jnp.bfloat16)
+
+
+def finish_kernel(parts_ref, residual_ref, mixed_ref):
+    row_0, row_1, col_0, col_1, _, width = parts_ref.shape
+    for r in range(row_1):
+        for c in range(col_1):
+            here = pl.ds((r * col_1 + c) * width, width)
+            total = residual_ref[:, here]
+            for i in range(row_0):
+                for j in range(col_0):
+                    total += parts_ref[i, r, j, c].astype(jnp.float32)
+            mixed_ref[:, here] = total.astype(jnp.bfloat16)
+
+
+def in_vmem(value):
+    return pltpu.with_memory_space_constraint(value, pltpu.VMEM)
+
+
 def attend(visual, vis_gain, text, text_gain, query_weight, key_weight, value_weight, out_weight):
     rows, cols, quad = (lax.axis_size(a) for a in (ROW, COL, QUAD))
     halves, planes = (lax.axis_size(a) for a in DP)
     devices = rows * cols
     tokens, _, features = visual.shape
     text_tokens = text.shape[0]
-    scaled = (visual.astype(jnp.float32) * SCALE).astype(jnp.float16)
-    scaled = scaled.reshape(tokens, halves, planes, features).transpose(2, 1, 0, 3)
-    relayed = lax.all_to_all(scaled, "dp_1", 0, 0, tiled=True)
-    half_tokens = planes * tokens
-    blocks = relayed.transpose(1, 3, 0, 2).reshape(halves, 1, features, half_tokens)
-    blocks = jnp.broadcast_to(blocks, (halves, rows, features, half_tokens))
-    column = lax.all_to_all(
-        blocks.reshape(halves * rows, features, half_tokens), ("dp_0",) + ROW, 0, 0, tiled=True
-    )
+    tokens_here = text_tokens // devices
+    width = DEC // quad
     member = lax.axis_index(QUAD)
-    width = DEC // quad
+    relayed = visual.reshape(tokens, halves, planes, features).transpose(2, 1, 0, 3)
+    relayed = lax.all_to_all(relayed, "dp_1", 0, 0, tiled=True)
     out_rows = []
     for step in range(quad):
         chunk = lax.dynamic_slice_in_dim(out_weight, (member ^ step) * width, width, 1)
         out_rows.append(lax.ppermute(chunk, QUAD, [(k, k ^ step) for k in range(quad)]) if step else chunk)
-    column = column.reshape(halves, rows * features, half_tokens).transpose(0, 2, 1)
-    column = column.reshape(halves * half_tokens, rows * features)
-    whole = lax.all_gather(column, COL, axis=0, tiled=True)
-    whole = whole.astype(jnp.bfloat16).reshape(cols, halves * half_tokens, rows * features)
+    half_tokens = planes * tokens
+    blocks = relayed.transpose(1, 3, 0, 2).reshape(halves, 1, features, half_tokens)
+    blocks = (blocks.astype(jnp.float32) * SCALE).astype(jnp.float16)
+    blocks = jnp.broadcast_to(blocks, (halves, rows, features, half_tokens))
+    blocks = blocks.reshape(halves * rows, features, half_tokens)
+    column = lax.all_to_all(blocks, ("dp_0",) + ROW, 0, 0, tiled=True)
     flat = text.reshape(text_tokens, DEC)
     text_f = flat.astype(jnp.float32)
     text_norm = (
         text_f * lax.rsqrt(jnp.mean(text_f * text_f, axis=-1, keepdims=True) + epsilon) * text_gain
     ).astype(jnp.bfloat16)
     queries = jnp.dot(text_norm, query_weight, preferred_element_type=jnp.float32).astype(jnp.bfloat16)
+    residual = lax.dynamic_slice_in_dim(flat, lax.axis_index(MP) * tokens_here, tokens_here, 0)
+    residual = residual.astype(jnp.float32)
     gain = vis_gain.reshape(rows, cols, features).transpose(1, 0, 2).reshape(cols, rows * features)
-    in_vmem = [
-        pltpu.with_memory_space_constraint(v, pltpu.VMEM)
-        for v in (
-            whole,
-            gain,
-            key_weight.reshape(devices, features, HEAD_DIM),
-            value_weight.reshape(devices, features, HEAD_DIM),
-            queries,
-        )
-    ]
+    column = column.reshape(halves, rows * features, half_tokens).transpose(0, 2, 1)
+    column = column.reshape(halves * half_tokens, rows * features)
+    whole = lax.all_gather(column, COL, axis=0, tiled=True)
+    whole = whole.astype(jnp.bfloat16).reshape(cols, halves * half_tokens, rows * features)
+    operands = [in_vmem(v) for v in (whole, gain, queries)]
+    operands += [w.reshape(devices, features, HEAD_DIM) for w in (key_weight, value_weight)]
     contexts = pl.pallas_call(
         attention_kernel,
         out_shape=jax.ShapeDtypeStruct((quad, text_tokens, HEAD_DIM), jnp.bfloat16),
-        in_specs=[pl.BlockSpec(memory_space=pltpu.VMEM)] * len(in_vmem),
+        in_specs=[pl.BlockSpec(memory_space=pltpu.VMEM)] * 3 + [pl.BlockSpec(memory_space=pltpu.HBM)] * 2,
         out_specs=pl.BlockSpec(memory_space=pltpu.VMEM),
         scratch_shapes=[
+            *(pltpu.VMEM(w.shape, jnp.bfloat16) for w in operands[3:]),
+            pltpu.SemaphoreType.DMA((2,)),
             pltpu.VMEM(whole.shape, jnp.bfloat16),
             pltpu.VMEM((whole.shape[1], LANES), jnp.float32),
         ],
         compiler_params=pltpu.CompilerParams(vmem_limit_bytes=12 << 20),
         name="attention",
-    )(*in_vmem)
+    )(*operands)
     group = lax.all_to_all(contexts, QUAD, 0, 0, tiled=True)
-    group = jnp.concatenate([lax.dynamic_index_in_dim(group, member ^ k, 0, False) for k in range(quad)], axis=1)
-    part = jnp.dot(group, jnp.concatenate(out_rows), preferred_element_type=jnp.float32).astype(jnp.bfloat16)
-    tokens_here = text_tokens // devices
+    operands = [in_vmem(v) for v in (group, *out_rows)]
+    part = pl.pallas_call(
+        project_kernel,
+        out_shape=jax.ShapeDtypeStruct((text_tokens, width), jnp.bfloat16),
+        in_specs=[pl.BlockSpec(memory_space=pltpu.SMEM)] + [pl.BlockSpec(memory_space=pltpu.VMEM)] * len(operands),
+        out_specs=pl.BlockSpec(memory_space=pltpu.VMEM),
+        compiler_params=pltpu.CompilerParams(vmem_limit_bytes=12 << 20),
+        name="project",
+    )(member.reshape(1), *operands)
     parts = lax.all_to_all(part.reshape(devices, tokens_here, width), MP, 0, 0, tiled=True)
     parts = parts.reshape(*(lax.axis_size(a) for a in MP), tokens_here, width)
-    summed = jnp.sum(parts.astype(jnp.float32), axis=(0, 2))
-    summed = summed.transpose(2, 0, 1, 3).reshape(tokens_here, DEC)
-    residual = lax.dynamic_slice_in_dim(flat, lax.axis_index(MP) * tokens_here, tokens_here, 0)
-    return (residual.astype(jnp.float32) + summed).astype(jnp.bfloat16).reshape(tokens_here, 1, DEC)
+    mixed = pl.pallas_call(
+        finish_kernel,
+        out_shape=jax.ShapeDtypeStruct((tokens_here, DEC), jnp.bfloat16),
+        in_specs=[pl.BlockSpec(memory_space=pltpu.VMEM)] * 2,
+        out_specs=pl.BlockSpec(memory_space=pltpu.VMEM),
+        compiler_params=pltpu.CompilerParams(vmem_limit_bytes=12 << 20),
+        name="finish",
+    )(in_vmem(parts), in_vmem(residual))
+    return mixed.reshape(tokens_here, 1, DEC)
 
 
 def solution(mesh):

time: 147 us -> 140 us (0.952)
  matrix products: 3.25 us -> 0.81 us
  Pallas kernels: 4.2 us -> 6.6 us
  waiting for transfers between devices: 44.4 us -> 42.1 us
  other arithmetic: 3.85 us -> 1.87 us
  local copies, waits for them, and re-layouts: 8.3 us -> 6.52 us
    dot_general x1 -> x0, matrix products: 2.44 us -> none  [attend(): jnp.dot(group, jnp.concatenate(out_rows), preferred_element_type=jnp.floa...]
    all_to_all x1, waiting for transfers between devices: 15.5 us -> 13.1 us  [attend(): lax.all_to_all(part.reshape(devices, tokens_here, width), MP, 0, 0, tiled...]
    pallas_call x0 -> x2, Pallas kernels: none -> 2.19 us  [the longest x1 1.48 us: attend(): pl.pallas_call(project_kernel, out_shape=jax.ShapeDtypeStruct((text_token...]
    dynamic_slice x1, local copies, waits for them, and re-layouts: 2.21 us -> 0.08 us  [attend(): lax.dynamic_slice_in_dim(out_weight, (member ^ step) * width, width, 1)]
  transfers between devices with their start and end apart: 7 -> 7, of which waited for: 4 -> 5; matrix products, arithmetic and copies ran while one was open for 3% -> 2% of each run, Pallas kernels for 0% -> 0%
where the time goes in v3:
time: 140 us; the launch traced here: 139 us
  starting transfers between devices  46.1 us (33%)
  waiting for transfers between devices  42.1 us (30%)
  blocking collectives  35.2 us (25%)
  Pallas kernels  6.6 us (5%)
  local copies, waits for them, and re-layouts  6.52 us (5%)
  other arithmetic  1.87 us (1%)
    all_gather x1, blocking collectives, attend(): whole = lax.all_gather(column, COL, axis=0, tiled=True)  35.2 us
    all_to_all x1, starting transfers between devices, attend(): relayed = lax.all_to_all(relayed, 'dp_1', 0, 0, tiled=True)  16.8 us
    all_to_all x1, waiting for transfers between devices, attend(): column = lax.all_to_all(blocks, ('dp_0',) + ROW, 0, 0, tiled=True)  14.3 us
    all_to_all x1, waiting for transfers between devices, attend(): lax.all_to_all(part.reshape(devices, tokens_here, width), MP, 0, 0, tiled...  13.1 us
    ppermute x3, starting transfers between devices, attend(): lax.ppermute(chunk, QUAD, [(k, k ^ step) for k in range(quad)])  9.21 us
    all_to_all x1, starting transfers between devices, attend(): lax.all_to_all(part.reshape(devices, tokens_here, width), MP, 0, 0, tiled...  8.2 us
    all_to_all x1, waiting for transfers between devices, attend(): relayed = lax.all_to_all(relayed, 'dp_1', 0, 0, tiled=True)  7.71 us
    all_to_all x1, starting transfers between devices, attend(): column = lax.all_to_all(blocks, ('dp_0',) + ROW, 0, 0, tiled=True)  7.56 us
  transfers between devices with their start and end apart: 7, of which 5 were waited for; matrix products, arithmetic and copies ran while one was open for 2% of the time, Pallas kernels for 0%

profile of v3, /device:TPU:2, one launch (start us, length us, event | category | flops | bytes accessed | tf_op | source)
XLA Modules:
  0.0 139.3 jit_solution(6941790447932187773)
XLA Ops:
  0.0 0.0 copy-start
  0.0 0.0 copy-start.3
  0.0 0.0 copy-start.5
  0.0 1.8 %copy.20 = bf16[16,2,8,192]{3,2,1,0:T(8,128)(2,1)} copy(bf16[16,2,8,192]{3,0,1,2:T(8,128)(2,1)} %bitcast.41) | data formatting | bytes 196608 | tf_op jit(solution)/shard_map/transpose | solution.py:112
  1.8 16.8 %all-to-all-start = ((bf16[16,2,8,192]{3,2,1,0:T(8,128)(2,1)}), bf16[16,2,8,192]{3,2,1,0:T(8,128)(2,1)S(1)}, u32[]{:S(2)}, u32[]{:S(2)}) async-start(bf16[16,2,8,192]{3,2,1,0:T(8,128)(2,1)} %copy.20), calls=%async_computation | async-start | bytes 262144 | tf_op jit(solution)/shard_map/all_to_all | solution.py:113
  18.6 0.8 reshape.76
  19.4 0.1 reshape.77.gain_ref
  19.5 7.7 %all-to-all-done = bf16[16,2,8,192]{3,2,1,0:T(8,128)(2,1)S(1)} async-done(((bf16[16,2,8,192]{3,2,1,0:T(8,128)(2,1)}), bf16[16,2,8,192]{3,2,1,0:T(8,128)(2,1)S(1)}, u32[]{:S(2)}, u32[]{:S(2)}) %all-to-all-start) | async-done | bytes 98336 | tf_op jit(solution)/shard_map/all_to_all | solution.py:113
  27.3 0.2 copy.22
  27.5 0.8 broadcast_in_dim.2
  28.3 7.6 %all-to-all-start.1 = ((f16[8,192,128]{2,1,0:T(8,128)(2,1)}), f16[8,192,128]{2,1,0:T(8,128)(2,1)}, u32[]{:S(2)}, u32[]{:S(2)}) async-start(f16[8,192,128]{2,1,0:T(8,128)(2,1)} %bitcast.39), calls=%async_computation.1 | async-start | bytes 786432 | tf_op jit(solution)/shard_map/all_to_all | solution.py:123
  35.8 0.0 copy-done.3
  35.8 0.5 fusion
  36.3 0.0 copy-done
  36.3 0.0 copy-done.5
  36.4 0.8 fusion.8.queries_ref
  37.2 14.3 %all-to-all-done.1 = f16[8,192,128]{2,1,0:T(8,128)(2,1)} async-done(((f16[8,192,128]{2,1,0:T(8,128)(2,1)}), f16[8,192,128]{2,1,0:T(8,128)(2,1)}, u32[]{:S(2)}, u32[]{:S(2)}) %all-to-all-start.1) | async-done | bytes 393248 | tf_op jit(solution)/shard_map/all_to_all | solution.py:123
  51.4 1.3 copy.23
  52.8 35.2 %all-gather.1 = f16[2048,768]{1,0:T(8,128)(2,1)S(1)} all-gather(f16[256,768]{1,0:T(8,128)(2,1)S(1)} %bitcast.38), channel_id=1, replica_groups=mesh['dp_0'=2,'dp_1'=16,'row_0'=2,'row_1'=2,'col_0'=4,'col_1'=2] {'col_0..., dimensions={0}, use_global_device_ids=true | all-gather | bytes 3538944 | tf_op jit(solution)/shard_map/all_gather | solution.py:135
  88.0 0.0 copy-start.1
  88.0 0.0 copy-start.2
  88.0 0.5 convert_element_type.48
  88.5 0.9 copy-done.1
  89.4 0.5 copy-done.2
  89.9 0.0 copy-start.4
  89.9 4.4 %attention.1 = bf16[4,256,128]{2,1,0:T(8,128)(2,1)} custom-call(bf16[8,256,768]{2,1,0:T(8,128)(2,1)S(1)} %bitcast.34, f32[8,768]{1,0:T(8,128)S(1)} %reshape.77.gain_ref, bf16[256,128]{1,0:T(8,128)(2,1)S(1)} %fusion.8.queries_ref, bf16[32,192,128]{2,1,0:T(8,128)(2,1)S(1)} %bitcast.36, bf16[32,192,128]{2,1,0:T(8,128)(2,1)S(1)} %bitcast.37), custom_call_target="tpu_custom_call" | custom-call | tf_op jit(solution)/shard_map/attention/pallas_call | solution.py:139
  94.3 4.3 %all-to-all-start.2 = ((bf16[4,256,128]{2,1,0:T(8,128)(2,1)}), bf16[4,256,128]{2,1,0:T(8,128)(2,1)S(1)}, u32[]{:S(2)}, u32[]{:S(2)}) async-start(bf16[4,256,128]{2,1,0:T(8,128)(2,1)} %attention.1), calls=%async_computation.2 | async-start | bytes 524288 | tf_op jit(solution)/shard_map/all_to_all | solution.py:153
  98.6 0.0 copy-done.4
  98.6 0.1 constant_dynamic-slice_fusion
  98.7 2.0 %collective-permute-start = (bf16[128,1024]{1,0:T(8,128)(2,1)S(1)}, bf16[128,1024]{1,0:T(8,128)(2,1)S(1)}, u32[]{:S(2)}, u32[]{:S(2)}) collective-permute-start(bf16[128,1024]{1,0:T(8,128)(2,1)S(1)} %get-tuple-element.6), channel_id=1, source_target_pairs={{0,1},{1,0},{8,9},{9,8},{2,3},{3,2},{10,11},{11,10},{4,5},{5,4},{1... | collective-permute-start | bytes 786440 | tf_op jit(solution)/shard_map/ppermute | solution.py:117
  100.7 3.9 %collective-permute-start.1 = (bf16[128,1024]{1,0:T(8,128)(2,1)S(1)}, bf16[128,1024]{1,0:T(8,128)(2,1)S(1)}, u32[]{:S(2)}, u32[]{:S(2)}) collective-permute-start(bf16[128,1024]{1,0:T(8,128)(2,1)S(1)} %get-tuple-element.8), channel_id=1, source_target_pairs={{0,8},{1,9},{8,0},{9,1},{2,10},{3,11},{10,2},{11,3},{4,12},{5,13},... | collective-permute-start | bytes 786440 | tf_op jit(solution)/shard_map/ppermute | solution.py:117
  104.6 3.4 %collective-permute-start.2 = (bf16[128,1024]{1,0:T(8,128)(2,1)S(1)}, bf16[128,1024]{1,0:T(8,128)(2,1)S(1)}, u32[]{:S(2)}, u32[]{:S(2)}) collective-permute-start(bf16[128,1024]{1,0:T(8,128)(2,1)S(1)} %get-tuple-element.5), channel_id=1, source_target_pairs={{0,9},{1,8},{8,1},{9,0},{2,11},{3,10},{10,3},{11,2},{4,13},{5,12},... | collective-permute-start | bytes 786440 | tf_op jit(solution)/shard_map/ppermute | solution.py:117
  108.0 0.4 collective-permute-done.refs_1_
  108.4 6.7 %collective-permute-done.1.refs_2_ = bf16[128,1024]{1,0:T(8,128)(2,1)S(1)} collective-permute-done((bf16[128,1024]{1,0:T(8,128)(2,1)S(1)}, bf16[128,1024]{1,0:T(8,128)(2,1)S(1)}, u32[]{:S(2)}, u32[]{:S(2)}) %collective-permute-start.1) | collective-permute-done | bytes 262176 | tf_op jit(solution)/shard_map/ppermute | solution.py:117
  115.0 0.0 collective-permute-done.2.refs_3_
  115.0 0.0 all-to-all-done.2.group_ref
  115.0 1.5 %project.1 = bf16[256,1024]{1,0:T(8,128)(2,1)} custom-call(s32[1]{0:T(128)} %bitcast.member_ref, bf16[4,256,128]{2,1,0:T(8,128)(2,1)S(1)} %all-to-all-done.2.group_ref, bf16[128,1024]{1,0:T(8,128)(2,1)S(1)} %get-tuple-element.7.refs_0_, bf16[128,1024]{1,0:T(8,128)(2,1)S(1)} %collective-permute-done.refs_1_, ...), custom_call_target="tpu_custom_call" | custom-call | tf_op jit(solution)/shard_map/project/pallas_call | solution.py:155
  116.5 8.2 %all-to-all-start.3 = ((bf16[32,8,1024]{2,1,0:T(8,128)(2,1)}), bf16[32,8,1024]{2,1,0:T(8,128)(2,1)S(1)}, u32[]{:S(2)}, u32[]{:S(2)}) async-start(bf16[32,8,1024]{2,1,0:T(8,128)(2,1)} %bitcast.15), calls=%async_computation.3 | async-start | bytes 1048576 | tf_op jit(solution)/shard_map/all_to_all | solution.py:163
  124.7 0.9 bitcast_convert_fusion.residual_ref
  125.6 13.1 %all-to-all-done.3 = bf16[32,8,1024]{2,1,0:T(8,128)(2,1)S(1)} async-done(((bf16[32,8,1024]{2,1,0:T(8,128)(2,1)}), bf16[32,8,1024]{2,1,0:T(8,128)(2,1)S(1)}, u32[]{:S(2)}, u32[]{:S(2)}) %all-to-all-start.3) | async-done | bytes 524320 | tf_op jit(solution)/shard_map/all_to_all | solution.py:163
  138.6 0.7 finish.1
  (3 shorter events, 0.1 us)
Async XLA Ops:
  0.0 36.3 %copy-start = (bf16[4096,128]{1,0:T(8,128)(2,1)S(1)}, bf16[4096,128]{1,0:T(8,128)(2,1)}, u32[]{:S(2)}) copy-start(bf16[4096,128]{1,0:T(8,128)(2,1)} %param.12) | copy-start | bytes 3145732
  0.0 35.8 %copy-start.3 = (bf16[256,1,4096]{2,0,1:T(8,128)(2,1)S(1)}, bf16[256,1,4096]{2,0,1:T(8,128)(2,1)}, u32[]{:S(2)}) copy-start(bf16[256,1,4096]{2,0,1:T(8,128)(2,1)} %param.10) | copy-start | bytes 6291460
  0.0 36.3 %copy-start.5 = (f32[4096]{0:T(1024)S(1)}, f32[4096]{0:T(1024)}, u32[]{:S(2)}) copy-start(f32[4096]{0:T(1024)} %param.11) | copy-start | bytes 49156
  1.8 25.4 %all-to-all-start = ((bf16[16,2,8,192]{3,2,1,0:T(8,128)(2,1)}), bf16[16,2,8,192]{3,2,1,0:T(8,128)(2,1)S(1)}, u32[]{:S(2)}, u32[]{:S(2)}) async-start(bf16[16,2,8,192]{3,2,1,0:T(8,128)(2,1)} %copy.20), calls=%async_computation | async-start | bytes 262144 | tf_op jit(solution)/shard_map/all_to_all | solution.py:113
  28.3 23.2 %all-to-all-start.1 = ((f16[8,192,128]{2,1,0:T(8,128)(2,1)}), f16[8,192,128]{2,1,0:T(8,128)(2,1)}, u32[]{:S(2)}, u32[]{:S(2)}) async-start(f16[8,192,128]{2,1,0:T(8,128)(2,1)} %bitcast.39), calls=%async_computation.1 | async-start | bytes 786432 | tf_op jit(solution)/shard_map/all_to_all | solution.py:123
  88.0 1.4 %copy-start.1 = (bf16[6144,128]{1,0:T(8,128)(2,1)S(1)}, bf16[6144,128]{1,0:T(8,128)(2,1)}, u32[]{:S(2)}) copy-start(bf16[6144,128]{1,0:T(8,128)(2,1)} %param.13) | copy-start | bytes 4718596
  88.0 1.9 %copy-start.2 = (bf16[6144,128]{1,0:T(8,128)(2,1)S(1)}, bf16[6144,128]{1,0:T(8,128)(2,1)}, u32[]{:S(2)}) copy-start(bf16[6144,128]{1,0:T(8,128)(2,1)} %param.14) | copy-start | bytes 4718596
  89.9 8.8 %copy-start.4 = (bf16[128,4096]{1,0:T(8,128)(2,1)S(1)}, bf16[128,4096]{1,0:T(8,128)(2,1)}, u32[]{:S(2)}) copy-start(bf16[128,4096]{1,0:T(8,128)(2,1)} %param.15) | copy-start | bytes 3145732
  94.3 20.7 %all-to-all-start.2 = ((bf16[4,256,128]{2,1,0:T(8,128)(2,1)}), bf16[4,256,128]{2,1,0:T(8,128)(2,1)S(1)}, u32[]{:S(2)}, u32[]{:S(2)}) async-start(bf16[4,256,128]{2,1,0:T(8,128)(2,1)} %attention.1), calls=%async_computation.2 | async-start | bytes 524288 | tf_op jit(solution)/shard_map/all_to_all | solution.py:153
  98.7 9.6 %collective-permute-start = (bf16[128,1024]{1,0:T(8,128)(2,1)S(1)}, bf16[128,1024]{1,0:T(8,128)(2,1)S(1)}, u32[]{:S(2)}, u32[]{:S(2)}) collective-permute-start(bf16[128,1024]{1,0:T(8,128)(2,1)S(1)} %get-tuple-element.6), channel_id=1, source_target_pairs={{0,1},{1,0},{8,9},{9,8},{2,3},{3,2},{10,11},{11,10},{4,5},{5,4},{1... | collective-permute-start | bytes 786440 | tf_op jit(solution)/shard_map/ppermute | solution.py:117
  100.7 14.3 %collective-permute-start.1 = (bf16[128,1024]{1,0:T(8,128)(2,1)S(1)}, bf16[128,1024]{1,0:T(8,128)(2,1)S(1)}, u32[]{:S(2)}, u32[]{:S(2)}) collective-permute-start(bf16[128,1024]{1,0:T(8,128)(2,1)S(1)} %get-tuple-element.8), channel_id=1, source_target_pairs={{0,8},{1,9},{8,0},{9,1},{2,10},{3,11},{10,2},{11,3},{4,12},{5,13},... | collective-permute-start | bytes 786440 | tf_op jit(solution)/shard_map/ppermute | solution.py:117
  104.6 10.4 %collective-permute-start.2 = (bf16[128,1024]{1,0:T(8,128)(2,1)S(1)}, bf16[128,1024]{1,0:T(8,128)(2,1)S(1)}, u32[]{:S(2)}, u32[]{:S(2)}) collective-permute-start(bf16[128,1024]{1,0:T(8,128)(2,1)S(1)} %get-tuple-element.5), channel_id=1, source_target_pairs={{0,9},{1,8},{8,1},{9,0},{2,11},{3,10},{10,3},{11,2},{4,13},{5,12},... | collective-permute-start | bytes 786440 | tf_op jit(solution)/shard_map/ppermute | solution.py:117
  116.5 22.1 %all-to-all-start.3 = ((bf16[32,8,1024]{2,1,0:T(8,128)(2,1)}), bf16[32,8,1024]{2,1,0:T(8,128)(2,1)S(1)}, u32[]{:S(2)}, u32[]{:S(2)}) async-start(bf16[32,8,1024]{2,1,0:T(8,128)(2,1)} %bitcast.15), calls=%async_computation.3 | async-start | bytes 1048576 | tf_op jit(solution)/shard_map/all_to_all | solution.py:163

commit v4 on v3

--- a/solution.py
+++ b/solution.py
@@ -19,6 +19,14 @@
 SCALE = 8192.0
 
 epsilon = 1e-06
+
+
+def in_vmem(value):
+    return pltpu.with_memory_space_constraint(value, pltpu.VMEM)
+
+
+def in_hbm(value):
+    return pltpu.with_memory_space_constraint(value, pltpu.HBM)
 
 
 def attention_kernel(
@@ -76,11 +84,47 @@
         contexts_ref[k] = context
 
 
+def pick_kernel(origins_ref, *refs):
+    *source_refs, semaphores = refs
+    picked_refs = source_refs[-(origins_ref.shape[0] // semaphores.shape[1]) :]
+    source_refs = source_refs[: semaphores.shape[1]]
+    copies = []
+    for k, picked_ref in enumerate(picked_refs):
+        for j, source_ref in enumerate(source_refs):
+            origin = pl.multiple_of(origins_ref[k * len(source_refs) + j], picked_ref.shape[2])
+            columns = source_ref.at[:, pl.ds(origin, picked_ref.shape[2])]
+            copies.append(pltpu.make_async_copy(columns, picked_ref.at[j], semaphores.at[k, j]))
+            copies[-1].start()
+    for copy in copies:
+        copy.wait()
+
+
+def pick_columns(sources, origins, *shapes):
+    return pl.pallas_call(
+        pick_kernel,
+        out_shape=shapes,
+        in_specs=[pl.BlockSpec(memory_space=pltpu.SMEM)] + [pl.BlockSpec(memory_space=pl.ANY)] * len(sources),
+        out_specs=[pl.BlockSpec(memory_space=pl.ANY)] * len(shapes),
+        scratch_shapes=[pltpu.SemaphoreType.DMA((len(shapes), len(sources)))],
+        compiler_params=pltpu.CompilerParams(vmem_limit_bytes=1 << 20),
+        name="pick",
+    )(jnp.stack(origins).astype(jnp.int32), in_hbm(sources[0]), *sources[1:])
+
+
+def turn_kernel(column_ref, turned_ref):
+    halves, _, half_tokens = column_ref.shape
+    for h in range(halves):
+        turned = column_ref[h].astype(jnp.float32).T
+        turned_ref[pl.ds(h * half_tokens, half_tokens), :] = turned.astype(jnp.bfloat16)
+
+
 def project_kernel(member_ref, group_ref, *refs):
     *chunk_refs, part_ref = refs
     part = jnp.zeros(part_ref.shape, jnp.float32)
-    for k, chunk_ref in enumerate(chunk_refs):
-        part += jnp.dot(group_ref[member_ref[0] ^ k], chunk_ref[...], preferred_element_type=jnp.float32)
+    for across_x, chunk_ref in enumerate(chunk_refs):
+        for across_y in range(chunk_ref.shape[0]):
+            there = member_ref[0] ^ (2 * across_y + across_x)
+            part += jnp.dot(group_ref[there], chunk_ref[across_y], preferred_element_type=jnp.float32)
     part_ref[...] = part.astype(jnp.bfloat16)
 
 
@@ -94,10 +138,6 @@
                 for j in range(col_0):
                     total += parts_ref[i, r, j, c].astype(jnp.float32)
             mixed_ref[:, here] = total.astype(jnp.bfloat16)
-
-
-def in_vmem(value):
-    return pltpu.with_memory_space_constraint(value, pltpu.VMEM)
 
 
 def attend(visual, vis_gain, text, text_gain, query_weight, key_weight, value_weight, out_weight):
@@ -111,13 +151,17 @@
     member = lax.axis_index(QUAD)
     relayed = visual.reshape(tokens, halves, planes, features).transpose(2, 1, 0, 3)
     relayed = lax.all_to_all(relayed, "dp_1", 0, 0, tiled=True)
-    out_rows = []
-    for step in range(quad):
-        chunk = lax.dynamic_slice_in_dim(out_weight, (member ^ step) * width, width, 1)
-        out_rows.append(lax.ppermute(chunk, QUAD, [(k, k ^ step) for k in range(quad)]) if step else chunk)
+    row, col = (lax.axis_index(a) for a in QUAD)
+    swap = [(0, 1), (1, 0)]
+    half = DEC // 2
+    quarter = jax.ShapeDtypeStruct((2, HEAD_DIM, width), jnp.bfloat16)
+    send = pick_columns([out_weight], [(1 - row) * half], jax.ShapeDtypeStruct((1, HEAD_DIM, half), jnp.bfloat16))[0]
+    beyond = lax.ppermute(send, QUAD[0], swap)[0]
+    origins = [[row * half + c * width, c * width] for c in (col, 1 - col)]
+    keep, send = pick_columns([out_weight, beyond], origins[0] + origins[1], quarter, quarter)
+    out_rows = [keep, lax.ppermute(send, QUAD[1], swap)]
     half_tokens = planes * tokens
     blocks = relayed.transpose(1, 3, 0, 2).reshape(halves, 1, features, half_tokens)
-    blocks = (blocks.astype(jnp.float32) * SCALE).astype(jnp.float16)
     blocks = jnp.broadcast_to(blocks, (halves, rows, features, half_tokens))
     blocks = blocks.reshape(halves * rows, features, half_tokens)
     column = lax.all_to_all(blocks, ("dp_0",) + ROW, 0, 0, tiled=True)
@@ -130,12 +174,19 @@
     residual = lax.dynamic_slice_in_dim(flat, lax.axis_index(MP) * tokens_here, tokens_here, 0)
     residual = residual.astype(jnp.float32)
     gain = vis_gain.reshape(rows, cols, features).transpose(1, 0, 2).reshape(cols, rows * features)
-    column = column.reshape(halves, rows * features, half_tokens).transpose(0, 2, 1)
-    column = column.reshape(halves * half_tokens, rows * features)
+    column = pl.pallas_call(
+        turn_kernel,
+        out_shape=jax.ShapeDtypeStruct((halves * half_tokens, rows * features), jnp.bfloat16),
+        in_specs=[pl.BlockSpec(memory_space=pltpu.VMEM)],
+        out_specs=pl.BlockSpec(memory_space=pltpu.VMEM),
+        compiler_params=pltpu.CompilerParams(vmem_limit_bytes=4 << 20),
+        name="turn",
+    )(in_vmem(column.reshape(halves, rows * features, half_tokens)))
+    column = (column.astype(jnp.float32) * SCALE).astype(jnp.float16)
     whole = lax.all_gather(column, COL, axis=0, tiled=True)
     whole = whole.astype(jnp.bfloat16).reshape(cols, halves * half_tokens, rows * features)
     operands = [in_vmem(v) for v in (whole, gain, queries)]
-    operands += [w.reshape(devices, features, HEAD_DIM) for w in (key_weight, value_weight)]
+    operands += [in_hbm(w.reshape(devices, features, HEAD_DIM)) for w in (key_weight, value_weight)]
     contexts = pl.pallas_call(
         attention_kernel,
         out_shape=jax.ShapeDtypeStruct((quad, text_tokens, HEAD_DIM), jnp.bfloat16),

time: 140 us -> 130 us (0.929)
  waiting for transfers between devices: 42.1 us -> 30.3 us
  local copies, waits for them, and re-layouts: 6.52 us -> 2.83 us
  Pallas kernels: 6.6 us -> 9.24 us
  starting transfers between devices: 46.1 us -> 44.3 us
  other arithmetic: 1.87 us -> 3.59 us
  blocking collectives: 35.2 us -> 36.8 us
  matrix products: 0.81 us -> 2.4 us
    all_to_all x1, waiting for transfers between devices: 14.3 us -> 6.64 us  [attend(): column = lax.all_to_all(blocks, ('dp_0',) + ROW, 0, 0, tiled=True)]
    ppermute x3 -> x2, waiting for transfers between devices: 7.07 us -> 0.01 us  [the longest x1 0.01 us: attend(): beyond = lax.ppermute(send, QUAD[0], swap)[0]]
    all_to_all x1, waiting for transfers between devices: 0.01 us -> 4.62 us  [attend(): group = lax.all_to_all(contexts, QUAD, 0, 0, tiled=True)]
    all_to_all x1, waiting for transfers between devices: 7.71 us -> 3.97 us  [attend(): relayed = lax.all_to_all(relayed, 'dp_1', 0, 0, tiled=True)]
    ppermute x3 -> x2, starting transfers between devices: 9.21 us -> 6.04 us  [the longest x1 3.6 us: attend(): beyond = lax.ppermute(send, QUAD[0], swap)[0]]
    pallas_call x0 -> x3, Pallas kernels: none -> 2.84 us  [the longest x2 2.67 us: pick_columns(): pl.pallas_call(pick_kernel, out_shape=shapes, in_specs=[pl.BlockSpec(memo...]
    all_to_all x1, waiting for transfers between devices: 13.1 us -> 15.1 us  [attend(): lax.all_to_all(part.reshape(devices, tokens_here, width), MP, 0, 0, tiled...]
    reduce_sum x1, other arithmetic: 0.49 us -> 2.08 us  [attend(): jnp.mean(text_f * text_f, axis=-1, keepdims=True) + epsilon]
  transfers between devices with their start and end apart: 7 -> 6, of which waited for: 5 -> 4; matrix products, arithmetic and copies ran while one was open for 2% -> 5% of each run, Pallas kernels for 0% -> 5%
where the time goes in v4:
time: 130 us
  starting transfers between devices  44.3 us (34%)
  blocking collectives  36.8 us (28%)
  waiting for transfers between devices  30.3 us (23%)
  Pallas kernels  9.24 us (7%)
  other arithmetic  3.59 us (3%)
  local copies, waits for them, and re-layouts  2.83 us (2%)
  matrix products  2.4 us (2%)
    all_gather x1, blocking collectives, attend(): whole = lax.all_gather(column, COL, axis=0, tiled=True)  36.8 us
    all_to_all x1, starting transfers between devices, attend(): relayed = lax.all_to_all(relayed, 'dp_1', 0, 0, tiled=True)  16.8 us
    all_to_all x1, waiting for transfers between devices, attend(): lax.all_to_all(part.reshape(devices, tokens_here, width), MP, 0, 0, tiled...  15.1 us
    all_to_all x1, starting transfers between devices, attend(): lax.all_to_all(part.reshape(devices, tokens_here, width), MP, 0, 0, tiled...  9.25 us
    all_to_all x1, starting transfers between devices, attend(): column = lax.all_to_all(blocks, ('dp_0',) + ROW, 0, 0, tiled=True)  7.56 us
    all_to_all x1, waiting for transfers between devices, attend(): column = lax.all_to_all(blocks, ('dp_0',) + ROW, 0, 0, tiled=True)  6.64 us
    all_to_all x1, starting transfers between devices, attend(): group = lax.all_to_all(contexts, QUAD, 0, 0, tiled=True)  4.69 us
    all_to_all x1, waiting for transfers between devices, attend(): group = lax.all_to_all(contexts, QUAD, 0, 0, tiled=True)  4.62 us
  transfers between devices with their start and end apart: 6, of which 4 were waited for; matrix products, arithmetic and copies ran while one was open for 5% of the time, Pallas kernels for 5%

profile of v4, /device:TPU:2, one launch (start us, length us, event | category | flops | bytes accessed | tf_op | source)
XLA Modules:
  0.0 129.6 jit_solution(4114367517243562550)
XLA Ops:
  0.0 0.0 copy-start
  0.0 0.0 copy-start.1
  0.0 0.0 copy-start.2
  0.0 1.7 %copy.15 = bf16[16,2,8,192]{3,2,1,0:T(8,128)(2,1)} copy(bf16[16,2,8,192]{3,0,1,2:T(8,128)(2,1)} %bitcast.44) | data formatting | bytes 196608 | tf_op jit(solution)/shard_map/transpose | solution.py:152
  1.7 16.8 %all-to-all-start = ((bf16[16,2,8,192]{3,2,1,0:T(8,128)(2,1)}), bf16[16,2,8,192]{3,2,1,0:T(8,128)(2,1)S(1)}, u32[]{:S(2)}, u32[]{:S(2)}) async-start(bf16[16,2,8,192]{3,2,1,0:T(8,128)(2,1)} %copy.15), calls=%async_computation | async-start | bytes 262144 | tf_op jit(solution)/shard_map/all_to_all | solution.py:153
  18.5 1.1 pick.2
  19.6 3.6 %collective-permute-start = (bf16[1,128,2048]{2,1,0:T(8,128)(2,1)S(1)}, bf16[1,128,2048]{2,1,0:T(8,128)(2,1)S(1)}, u32[]{:S(2)}, u32[]{:S(2)}) collective-permute-start(bf16[1,128,2048]{2,1,0:T(8,128)(2,1)S(1)} %pick.2), channel_id=1, source_target_pairs={{0,8},{8,0},{1,9},{9,1},{2,10},{10,2},{3,11},{11,3},{4,12},{12,4},... | collective-permute-start | bytes 1572872 | tf_op jit(solution)/shard_map/ppermute | solution.py:159
  23.2 4.0 %all-to-all-done = bf16[16,2,8,192]{3,2,1,0:T(8,128)(2,1)S(1)} async-done(((bf16[16,2,8,192]{3,2,1,0:T(8,128)(2,1)}), bf16[16,2,8,192]{3,2,1,0:T(8,128)(2,1)S(1)}, u32[]{:S(2)}, u32[]{:S(2)}) %all-to-all-start) | async-done | bytes 98336 | tf_op jit(solution)/shard_map/all_to_all | solution.py:153
  27.2 0.1 copy.17
  27.3 0.8 broadcast_in_dim.10
  28.1 7.6 %all-to-all-start.1 = ((bf16[8,192,128]{2,1,0:T(8,128)(2,1)}), bf16[8,192,128]{2,1,0:T(8,128)(2,1)S(1)}, u32[]{:S(2)}, u32[]{:S(2)}) async-start(bf16[8,192,128]{2,1,0:T(8,128)(2,1)} %bitcast.5), calls=%async_computation.1 | async-start | bytes 786432 | tf_op jit(solution)/shard_map/all_to_all | solution.py:167
  35.7 2.1 %fusion = f32[256]{0:T(256)S(1)} fusion(bf16[256,1,4096]{2,0,1:T(8,128)(2,1)} %param.10), kind=kLoop, calls=%fused_computation.2 | loop fusion | flops 3145472 | bytes 2098176 | tf_op jit(solution)/shard_map/reduce_sum | solution.py:171
  37.7 0.0 copy-done.1
  37.7 0.1 reshape.58
  37.8 0.1 reshape.59.gain_ref
  37.9 0.1 pad_add_fusion.origins_ref
  38.0 0.0 copy-done
  38.0 0.0 copy-done.2
  38.0 2.4 %fusion.8.queries_ref = bf16[256,128]{1,0:T(8,128)(2,1)S(1)} fusion(bf16[4096,128]{1,0:T(8,128)(2,1)S(1)} %copy-done, bf16[256,1,4096]{2,0,1:T(8,128)(2,1)} %param.10, f32[4096]{0:T(1024)S(1)} %copy-done.2, f32[256]{0:T(256)S(1)} %add_rsqrt_fusion), kind=kOutput, calls=%fused_computation.9 | convolution fusion | flops 272662528 | bytes 3228672 | tf_op jit(solution)/shard_map/dot_general | solution.py:173
  40.4 0.0 collective-permute-done
  40.4 1.6 %pick.3 = (bf16[2,128,1024]{2,1,0:T(8,128)(2,1)S(1)}, bf16[2,128,1024]{2,1,0:T(8,128)(2,1)S(1)}) custom-call(s32[4]{0:T(128)S(1)} %pad_add_fusion.origins_ref, bf16[128,4096]{1,0:T(8,128)(2,1)} %refs_0_.3, bf16[128,2048]{1,0:T(8,128)(2,1)S(1)} %bitcast.40), custom_call_target="tpu_custom_call" | custom-call | tf_op jit(solution)/shard_map/pick/pallas_call | solution.py:103
  42.1 2.4 %collective-permute-start.1 = (bf16[2,128,1024]{2,1,0:T(8,128)(2,1)S(1)}, bf16[2,128,1024]{2,1,0:T(8,128)(2,1)S(1)}, u32[]{:S(2)}, u32[]{:S(2)}) collective-permute-start(bf16[2,128,1024]{2,1,0:T(8,128)(2,1)S(1)} %get-tuple-element.8), channel_id=1, source_target_pairs={{0,1},{1,0},{2,3},{3,2},{4,5},{5,4},{6,7},{7,6},{8,9},{9,8},{10,11... | collective-permute-start | bytes 1572872 | tf_op jit(solution)/shard_map/ppermute | solution.py:162
  44.5 6.6 %all-to-all-done.1 = bf16[8,192,128]{2,1,0:T(8,128)(2,1)S(1)} async-done(((bf16[8,192,128]{2,1,0:T(8,128)(2,1)}), bf16[8,192,128]{2,1,0:T(8,128)(2,1)S(1)}, u32[]{:S(2)}, u32[]{:S(2)}) %all-to-all-start.1) | async-done | bytes 393248 | tf_op jit(solution)/shard_map/all_to_all | solution.py:167
  51.2 0.2 turn.1
  51.3 0.1 multiply_convert_fusion
  51.4 36.8 %all-gather.1 = f16[2048,768]{1,0:T(8,128)(2,1)S(1)} all-gather(f16[256,768]{1,0:T(8,128)(2,1)S(1)} %multiply_convert_fusion), channel_id=1, replica_groups=mesh['dp_0'=2,'dp_1'=16,'row_0'=2,'row_1'=2,'col_0'=4,'col_1'=2] {'col_0..., dimensions={0}, use_global_device_ids=true | all-gather | bytes 3538944 | tf_op jit(solution)/shard_map/all_gather | solution.py:186
  88.2 0.5 convert_element_type.28
  88.7 4.2 %attention.1 = bf16[4,256,128]{2,1,0:T(8,128)(2,1)} custom-call(bf16[8,256,768]{2,1,0:T(8,128)(2,1)S(1)} %bitcast.37, f32[8,768]{1,0:T(8,128)S(1)} %reshape.59.gain_ref, bf16[256,128]{1,0:T(8,128)(2,1)S(1)} %fusion.8.queries_ref, bf16[32,192,128]{2,1,0:T(8,128)(2,1)} %bitcast.41, bf16[32,192,128]{2,1,0:T(8,128)(2,1)} %bitcast.42), custom_call_target="tpu_custom_call" | custom-call | tf_op jit(solution)/shard_map/attention/pallas_call | solution.py:190
  92.9 4.7 %all-to-all-start.2 = ((bf16[4,256,128]{2,1,0:T(8,128)(2,1)}), bf16[4,256,128]{2,1,0:T(8,128)(2,1)S(1)}, u32[]{:S(2)}, u32[]{:S(2)}) async-start(bf16[4,256,128]{2,1,0:T(8,128)(2,1)} %attention.1), calls=%async_computation.2 | async-start | bytes 524288 | tf_op jit(solution)/shard_map/all_to_all | solution.py:204
  97.6 0.0 collective-permute-done.1.refs_1_
  97.6 4.6 %all-to-all-done.2.group_ref = bf16[4,256,128]{2,1,0:T(8,128)(2,1)S(1)} async-done(((bf16[4,256,128]{2,1,0:T(8,128)(2,1)}), bf16[4,256,128]{2,1,0:T(8,128)(2,1)S(1)}, u32[]{:S(2)}, u32[]{:S(2)}) %all-to-all-start.2) | async-done | bytes 262176 | tf_op jit(solution)/shard_map/all_to_all | solution.py:204
  102.2 1.5 %project.1 = bf16[256,1024]{1,0:T(8,128)(2,1)} custom-call(s32[1]{0:T(128)} %bitcast.member_ref, bf16[4,256,128]{2,1,0:T(8,128)(2,1)S(1)} %all-to-all-done.2.group_ref, bf16[2,128,1024]{2,1,0:T(8,128)(2,1)S(1)} %get-tuple-element.7.refs_0_, bf16[2,128,1024]{2,1,0:T(8,128)(2,1)S(1)} %collective-permute-done.1.refs_1_), custom_call_target="tpu_custom_call" | custom-call | tf_op jit(solution)/shard_map/project/pallas_call | solution.py:206
  103.7 9.2 %all-to-all-start.3 = ((bf16[32,8,1024]{2,1,0:T(8,128)(2,1)}), bf16[32,8,1024]{2,1,0:T(8,128)(2,1)S(1)}, u32[]{:S(2)}, u32[]{:S(2)}) async-start(bf16[32,8,1024]{2,1,0:T(8,128)(2,1)} %bitcast.19), calls=%async_computation.3 | async-start | bytes 1048576 | tf_op jit(solution)/shard_map/all_to_all | solution.py:214
  113.0 0.9 bitcast_convert_fusion.residual_ref
  113.8 15.1 %all-to-all-done.3 = bf16[32,8,1024]{2,1,0:T(8,128)(2,1)S(1)} async-done(((bf16[32,8,1024]{2,1,0:T(8,128)(2,1)}), bf16[32,8,1024]{2,1,0:T(8,128)(2,1)S(1)}, u32[]{:S(2)}, u32[]{:S(2)}) %all-to-all-start.3) | async-done | bytes 524320 | tf_op jit(solution)/shard_map/all_to_all | solution.py:214
  128.9 0.7 finish.1
  (3 shorter events, 0.0 us)
Async XLA Ops:
  0.0 38.0 %copy-start = (bf16[4096,128]{1,0:T(8,128)(2,1)S(1)}, bf16[4096,128]{1,0:T(8,128)(2,1)}, u32[]{:S(2)}) copy-start(bf16[4096,128]{1,0:T(8,128)(2,1)} %param.12) | copy-start | bytes 3145732
  0.0 37.7 %copy-start.1 = (f32[6144]{0:T(1024)S(1)}, f32[6144]{0:T(1024)}, u32[]{:S(2)}) copy-start(f32[6144]{0:T(1024)} %param.9) | copy-start | bytes 73732
  0.0 38.0 %copy-start.2 = (f32[4096]{0:T(1024)S(1)}, f32[4096]{0:T(1024)}, u32[]{:S(2)}) copy-start(f32[4096]{0:T(1024)} %param.11) | copy-start | bytes 49156
  1.7 25.4 %all-to-all-start = ((bf16[16,2,8,192]{3,2,1,0:T(8,128)(2,1)}), bf16[16,2,8,192]{3,2,1,0:T(8,128)(2,1)S(1)}, u32[]{:S(2)}, u32[]{:S(2)}) async-start(bf16[16,2,8,192]{3,2,1,0:T(8,128)(2,1)} %copy.15), calls=%async_computation | async-start | bytes 262144 | tf_op jit(solution)/shard_map/all_to_all | solution.py:153
  19.6 20.8 %collective-permute-start = (bf16[1,128,2048]{2,1,0:T(8,128)(2,1)S(1)}, bf16[1,128,2048]{2,1,0:T(8,128)(2,1)S(1)}, u32[]{:S(2)}, u32[]{:S(2)}) collective-permute-start(bf16[1,128,2048]{2,1,0:T(8,128)(2,1)S(1)} %pick.2), channel_id=1, source_target_pairs={{0,8},{8,0},{1,9},{9,1},{2,10},{10,2},{3,11},{11,3},{4,12},{12,4},... | collective-permute-start | bytes 1572872 | tf_op jit(solution)/shard_map/ppermute | solution.py:159
  28.1 23.1 %all-to-all-start.1 = ((bf16[8,192,128]{2,1,0:T(8,128)(2,1)}), bf16[8,192,128]{2,1,0:T(8,128)(2,1)S(1)}, u32[]{:S(2)}, u32[]{:S(2)}) async-start(bf16[8,192,128]{2,1,0:T(8,128)(2,1)} %bitcast.5), calls=%async_computation.1 | async-start | bytes 786432 | tf_op jit(solution)/shard_map/all_to_all | solution.py:167
  42.1 55.5 %collective-permute-start.1 = (bf16[2,128,1024]{2,1,0:T(8,128)(2,1)S(1)}, bf16[2,128,1024]{2,1,0:T(8,128)(2,1)S(1)}, u32[]{:S(2)}, u32[]{:S(2)}) collective-permute-start(bf16[2,128,1024]{2,1,0:T(8,128)(2,1)S(1)} %get-tuple-element.8), channel_id=1, source_target_pairs={{0,1},{1,0},{2,3},{3,2},{4,5},{5,4},{6,7},{7,6},{8,9},{9,8},{10,11... | collective-permute-start | bytes 1572872 | tf_op jit(solution)/shard_map/ppermute | solution.py:162
  92.9 9.3 %all-to-all-start.2 = ((bf16[4,256,128]{2,1,0:T(8,128)(2,1)}), bf16[4,256,128]{2,1,0:T(8,128)(2,1)S(1)}, u32[]{:S(2)}, u32[]{:S(2)}) async-start(bf16[4,256,128]{2,1,0:T(8,128)(2,1)} %attention.1), calls=%async_computation.2 | async-start | bytes 524288 | tf_op jit(solution)/shard_map/all_to_all | solution.py:204
  103.7 25.2 %all-to-all-start.3 = ((bf16[32,8,1024]{2,1,0:T(8,128)(2,1)}), bf16[32,8,1024]{2,1,0:T(8,128)(2,1)S(1)}, u32[]{:S(2)}, u32[]{:S(2)}) async-start(bf16[32,8,1024]{2,1,0:T(8,128)(2,1)} %bitcast.19), calls=%async_computation.3 | async-start | bytes 1048576 | tf_op jit(solution)/shard_map/all_to_all | solution.py:214

commit v5 on v4

--- a/solution.py
+++ b/solution.py
@@ -16,6 +16,8 @@
 QUAD = ("row_1", "col_1")
 LANES = 128
 CHUNK = 64
+TEXT_CHUNKS = 2
+TEXT_BLOCK = 32
 SCALE = 8192.0
 
 epsilon = 1e-06
@@ -82,6 +84,55 @@
     context = jnp.dot(probs, values, preferred_element_type=jnp.float32).astype(jnp.bfloat16)
     for k in range(contexts_ref.shape[0]):
         contexts_ref[k] = context
+
+
+def query_kernel(
+    origin_ref,
+    text_hbm_ref,
+    weight_hbm_ref,
+    gain_ref,
+    queries_ref,
+    residual_ref,
+    text_ref,
+    weight_ref,
+    normed_ref,
+    semaphores,
+):
+    tokens, width = text_ref.shape
+    chunk = tokens // TEXT_CHUNKS
+    places = [pl.ds(k * chunk, chunk) for k in range(TEXT_CHUNKS)]
+    copies = [
+        pltpu.make_async_copy(text_hbm_ref.at[here], text_ref.at[here], semaphores.at[k])
+        for k, here in enumerate(places)
+    ]
+    copies.append(pltpu.make_async_copy(weight_hbm_ref, weight_ref, semaphores.at[TEXT_CHUNKS]))
+    for copy in copies:
+        copy.start()
+    for k, here in enumerate(places):
+        copies[k].wait()
+
+        def normalize(step, carry, k=k):
+            block = pl.ds(pl.multiple_of(step * TEXT_BLOCK, TEXT_BLOCK), TEXT_BLOCK)
+            inside = pl.ds(pl.multiple_of(k * chunk + step * TEXT_BLOCK, TEXT_BLOCK), TEXT_BLOCK)
+            squares = jnp.zeros((TEXT_BLOCK, LANES), jnp.float32)
+            for n in range(0, width, LANES):
+                x = text_ref[inside, pl.ds(n, LANES)].astype(jnp.float32)
+                squares += x * x
+            scale = lax.rsqrt(jnp.sum(squares, axis=1, keepdims=True) / width + epsilon)
+            for n in range(0, width, LANES):
+                x = text_ref[inside, pl.ds(n, LANES)].astype(jnp.float32)
+                normed_ref[block, pl.ds(n, LANES)] = (x * scale * gain_ref[:, pl.ds(n, LANES)]).astype(jnp.bfloat16)
+            return carry
+
+        lax.fori_loop(0, chunk // TEXT_BLOCK, normalize, 0)
+        if k == 0:
+            copies[-1].wait()
+        queries_ref[here, :] = jnp.dot(
+            normed_ref[...], weight_ref[...], preferred_element_type=jnp.float32
+        ).astype(jnp.bfloat16)
+    count = residual_ref.shape[0]
+    pair = text_ref[pl.ds(pl.multiple_of(origin_ref[0] // 16 * 16, 16), 16), :].astype(jnp.float32)
+    residual_ref[...] = jnp.where(origin_ref[0] % 16 == 0, pair[:count], pair[count:])
 
 
 def pick_kernel(origins_ref, *refs):
@@ -166,13 +217,30 @@
     blocks = blocks.reshape(halves * rows, features, half_tokens)
     column = lax.all_to_all(blocks, ("dp_0",) + ROW, 0, 0, tiled=True)
     flat = text.reshape(text_tokens, DEC)
-    text_f = flat.astype(jnp.float32)
-    text_norm = (
-        text_f * lax.rsqrt(jnp.mean(text_f * text_f, axis=-1, keepdims=True) + epsilon) * text_gain
-    ).astype(jnp.bfloat16)
-    queries = jnp.dot(text_norm, query_weight, preferred_element_type=jnp.float32).astype(jnp.bfloat16)
-    residual = lax.dynamic_slice_in_dim(flat, lax.axis_index(MP) * tokens_here, tokens_here, 0)
-    residual = residual.astype(jnp.float32)
+    queries, residual = pl.pallas_call(
+        query_kernel,
+        out_shape=(
+            jax.ShapeDtypeStruct((text_tokens, HEAD_DIM), jnp.bfloat16),
+            jax.ShapeDtypeStruct((tokens_here, DEC), jnp.float32),
+        ),
+        in_specs=[pl.BlockSpec(memory_space=pltpu.SMEM)]
+        + [pl.BlockSpec(memory_space=pl.ANY)] * 2
+        + [pl.BlockSpec(memory_space=pltpu.VMEM)],
+        out_specs=[pl.BlockSpec(memory_space=pltpu.VMEM)] * 2,
+        scratch_shapes=[
+            pltpu.VMEM(flat.shape, jnp.bfloat16),
+            pltpu.VMEM(query_weight.shape, jnp.bfloat16),
+            pltpu.VMEM((text_tokens // TEXT_CHUNKS, DEC), jnp.bfloat16),
+            pltpu.SemaphoreType.DMA((TEXT_CHUNKS + 1,)),
+        ],
+        compiler_params=pltpu.CompilerParams(vmem_limit_bytes=8 << 20),
+        name="query",
+    )(
+        (lax.axis_index(MP) * tokens_here).reshape(1),
+        in_hbm(flat),
+        in_hbm(query_weight),
+        text_gain.reshape(1, DEC),
+    )
     gain = vis_gain.reshape(rows, cols, features).transpose(1, 0, 2).reshape(cols, rows * features)
     column = pl.pallas_call(
         turn_kernel,

time: 130 us -> 144 us (1.11)
  blocking collectives: 36.8 us -> 91.7 us
  starting transfers between devices: 44.3 us -> 18.7 us
  waiting for transfers between devices: 30.3 us -> 18.6 us
  other arithmetic: 3.59 us -> 0.66 us
  Pallas kernels: 9.24 us -> 12 us
  matrix products: 2.4 us -> 0 us
    all_to_all x0 -> x2, blocking collectives: none -> 48.4 us  [the longest x1 25.2 us: attend(): relayed = lax.all_to_all(relayed, 'dp_1', 0, 0, tiled=True)]
    all_to_all x2 -> x0, starting transfers between devices: 26 us -> none  [the longest x1 16.8 us: attend(): relayed = lax.all_to_all(relayed, 'dp_1', 0, 0, tiled=True)]
    all_to_all x2 -> x0, waiting for transfers between devices: 19.1 us -> none  [the longest x1 15.1 us: attend(): lax.all_to_all(part.reshape(devices, tokens_here, width), MP, 0, 0, tiled...]
    ppermute x1, waiting for transfers between devices: 0.01 us -> 14 us  [attend(): beyond = lax.ppermute(send, QUAD[0], swap)[0]]
    all_to_all x1, waiting for transfers between devices: 6.64 us -> 0.01 us  [attend(): column = lax.all_to_all(blocks, ('dp_0',) + ROW, 0, 0, tiled=True)]
    all_gather x1, blocking collectives: 36.8 us -> 43.3 us  [attend(): whole = lax.all_gather(column, COL, axis=0, tiled=True)]
    pallas_call x0 -> x1, Pallas kernels: none -> 3.53 us  [attend(): pl.pallas_call(query_kernel, out_shape=(jax.ShapeDtypeStruct((text_tokens...]
    dot_general x1 -> x0, matrix products: 2.4 us -> none  [attend(): jnp.dot(text_norm, query_weight, preferred_element_type=jnp.float32)]
  transfers between devices with their start and end apart: 6 -> 4, of which waited for: 4 -> 2; matrix products, arithmetic and copies ran while one was open for 5% -> 1% of each run, Pallas kernels for 5% -> 7%
where the time goes in v5:
time: 144 us
  blocking collectives  91.7 us (64%)
  starting transfers between devices  18.7 us (13%)
  waiting for transfers between devices  18.6 us (13%)
  Pallas kernels  12 us (8%)
  local copies, waits for them, and re-layouts  2.09 us (1%)
    all_gather x1, blocking collectives, attend(): whole = lax.all_gather(column, COL, axis=0, tiled=True)  43.3 us
    all_to_all x1, blocking collectives, attend(): relayed = lax.all_to_all(relayed, 'dp_1', 0, 0, tiled=True)  25.2 us
    all_to_all x1, blocking collectives, attend(): lax.all_to_all(part.reshape(devices, tokens_here, width), MP, 0, 0, tiled...  23.2 us
    ppermute x1, waiting for transfers between devices, attend(): beyond = lax.ppermute(send, QUAD[0], swap)[0]  14 us
    all_to_all x1, starting transfers between devices, attend(): column = lax.all_to_all(blocks, ('dp_0',) + ROW, 0, 0, tiled=True)  7.56 us
    all_to_all x1, starting transfers between devices, attend(): group = lax.all_to_all(contexts, QUAD, 0, 0, tiled=True)  4.77 us
    all_to_all x1, waiting for transfers between devices, attend(): group = lax.all_to_all(contexts, QUAD, 0, 0, tiled=True)  4.62 us
    pallas_call x1, Pallas kernels, attend(): pl.pallas_call(attention_kernel, out_shape=jax.ShapeDtypeStruct((quad, te...  4.21 us
  transfers between devices with their start and end apart: 4, of which 2 were waited for; matrix products, arithmetic and copies ran while one was open for 1% of the time, Pallas kernels for 7%

profile of v5, /device:TPU:2, one launch (start us, length us, event | category | flops | bytes accessed | tf_op | source)
XLA Modules:
  0.0 143.9 jit_solution(6531958556497597300)
XLA Ops:
  0.0 0.0 copy-start.1
  0.0 0.0 copy-start
  0.0 1.0 copy.15
  1.0 25.2 %all_to_all.20 = bf16[16,2,8,192]{3,2,1,0:T(8,128)(2,1)S(1)} all-to-all(bf16[16,2,8,192]{3,2,1,0:T(8,128)(2,1)S(1)} %copy.15), channel_id=1, replica_groups=mesh['dp_0'=2,'dp_1'=16,'row_0'=2,'row_1'=2,'col_0'=4,'col_1'=2] {'dp_1'}, dimensions={0} | all-to-all | bytes 196608 | tf_op jit(solution)/shard_map/all_to_all | solution.py:204
  26.2 0.1 copy.17
  26.4 0.8 broadcast_in_dim.8
  27.2 7.6 %all-to-all-start.1 = ((bf16[8,192,128]{2,1,0:T(8,128)(2,1)}), bf16[8,192,128]{2,1,0:T(8,128)(2,1)S(1)}, u32[]{:S(2)}, u32[]{:S(2)}) async-start(bf16[8,192,128]{2,1,0:T(8,128)(2,1)} %bitcast.5), calls=%async_computation.1 | async-start | bytes 786432 | tf_op jit(solution)/shard_map/all_to_all | solution.py:218
  34.7 1.0 pick.2
  35.8 3.9 %collective-permute-start = (bf16[1,128,2048]{2,1,0:T(8,128)(2,1)S(1)}, bf16[1,128,2048]{2,1,0:T(8,128)(2,1)S(1)}, u32[]{:S(2)}, u32[]{:S(2)}) collective-permute-start(bf16[1,128,2048]{2,1,0:T(8,128)(2,1)S(1)} %pick.2), channel_id=1, source_target_pairs={{0,8},{8,0},{1,9},{9,1},{2,10},{10,2},{3,11},{11,3},{4,12},{12,4},... | collective-permute-start | bytes 1572872 | tf_op jit(solution)/shard_map/ppermute | solution.py:210
  39.7 0.0 copy-done.1
  39.7 0.1 reshape.52
  39.8 0.1 reshape.53.gain_ref
  39.9 0.0 copy-done
  39.9 3.5 %query.1 = (bf16[256,128]{1,0:T(8,128)(2,1)S(1)}, f32[8,4096]{1,0:T(8,128)S(1)}) custom-call(s32[1]{0:T(128)} %bitcast.9.origin_ref, bf16[256,4096]{1,0:T(8,128)(2,1)} %bitcast.33, bf16[4096,128]{1,0:T(8,128)(2,1)} %weight_hbm_ref.1, f32[1,4096]{1,0:T(1,128)S(1)} %bitcast.32), custom_call_target="tpu_custom_call" | custom-call | tf_op jit(solution)/shard_map/query/pallas_call | solution.py:220
  43.4 0.1 pad_add_fusion.origins_ref
  43.5 14.0 %collective-permute-done = bf16[1,128,2048]{2,1,0:T(8,128)(2,1)S(1)} collective-permute-done((bf16[1,128,2048]{2,1,0:T(8,128)(2,1)S(1)}, bf16[1,128,2048]{2,1,0:T(8,128)(2,1)S(1)}, u32[]{:S(2)}, u32[]{:S(2)}) %collective-permute-start) | collective-permute-done | bytes 524320 | tf_op jit(solution)/shard_map/ppermute | solution.py:210
  57.5 1.6 %pick.3 = (bf16[2,128,1024]{2,1,0:T(8,128)(2,1)S(1)}, bf16[2,128,1024]{2,1,0:T(8,128)(2,1)S(1)}) custom-call(s32[4]{0:T(128)S(1)} %pad_add_fusion.origins_ref, bf16[128,4096]{1,0:T(8,128)(2,1)} %refs_0_.3, bf16[128,2048]{1,0:T(8,128)(2,1)S(1)} %bitcast.31), custom_call_target="tpu_custom_call" | custom-call | tf_op jit(solution)/shard_map/pick/pallas_call | solution.py:154
  59.2 2.4 %collective-permute-start.1 = (bf16[2,128,1024]{2,1,0:T(8,128)(2,1)S(1)}, bf16[2,128,1024]{2,1,0:T(8,128)(2,1)S(1)}, u32[]{:S(2)}, u32[]{:S(2)}) collective-permute-start(bf16[2,128,1024]{2,1,0:T(8,128)(2,1)S(1)} %get-tuple-element.11), channel_id=1, source_target_pairs={{0,1},{1,0},{2,3},{3,2},{4,5},{5,4},{6,7},{7,6},{8,9},{9,8},{10,11... | collective-permute-start | bytes 1572872 | tf_op jit(solution)/shard_map/ppermute | solution.py:213
  61.6 0.0 all-to-all-done.1
  61.6 0.2 turn.1
  61.8 0.1 multiply_convert_fusion
  61.9 43.3 %all-gather.1 = f16[2048,768]{1,0:T(8,128)(2,1)S(1)} all-gather(f16[256,768]{1,0:T(8,128)(2,1)S(1)} %multiply_convert_fusion), channel_id=1, replica_groups=mesh['dp_0'=2,'dp_1'=16,'row_0'=2,'row_1'=2,'col_0'=4,'col_1'=2] {'col_0..., dimensions={0}, use_global_device_ids=true | all-gather | bytes 3538944 | tf_op jit(solution)/shard_map/all_gather | solution.py:254
  105.2 0.5 convert_element_type.11
  105.7 4.2 %attention.1 = bf16[4,256,128]{2,1,0:T(8,128)(2,1)} custom-call(bf16[8,256,768]{2,1,0:T(8,128)(2,1)S(1)} %bitcast.27, f32[8,768]{1,0:T(8,128)S(1)} %reshape.53.gain_ref, bf16[256,128]{1,0:T(8,128)(2,1)S(1)} %get-tuple-element.9.queries_ref, bf16[32,192,128]{2,1,0:T(8,128)(2,1)} %bitcast.34, bf16[32,192,128]{2,1,0:T(8,128)(2,1)} %bitcast.35), custom_call_target="tpu_custom_call" | custom-call | tf_op jit(solution)/shard_map/attention/pallas_call | solution.py:258
  109.9 4.8 %all-to-all-start.2 = ((bf16[4,256,128]{2,1,0:T(8,128)(2,1)}), bf16[4,256,128]{2,1,0:T(8,128)(2,1)S(1)}, u32[]{:S(2)}, u32[]{:S(2)}) async-start(bf16[4,256,128]{2,1,0:T(8,128)(2,1)} %attention.1), calls=%async_computation.2 | async-start | bytes 524288 | tf_op jit(solution)/shard_map/all_to_all | solution.py:272
  114.7 0.0 collective-permute-done.1.refs_1_
  114.7 4.6 %all-to-all-done.2.group_ref = bf16[4,256,128]{2,1,0:T(8,128)(2,1)S(1)} async-done(((bf16[4,256,128]{2,1,0:T(8,128)(2,1)}), bf16[4,256,128]{2,1,0:T(8,128)(2,1)S(1)}, u32[]{:S(2)}, u32[]{:S(2)}) %all-to-all-start.2) | async-done | bytes 262176 | tf_op jit(solution)/shard_map/all_to_all | solution.py:272
  119.3 0.7 project.1
  120.0 23.2 %all_to_all.21 = bf16[32,8,1024]{2,1,0:T(8,128)(2,1)S(1)} all-to-all(bf16[32,8,1024]{2,1,0:T(8,128)(2,1)S(1)} %bitcast.29), channel_id=1, replica_groups=mesh['dp_0'=2,'dp_1'=16,'row_0'=2,'row_1'=2,'col_0'=4,'col_1'=2] {'row_0..., dimensions={0} | all-to-all | bytes 1048576 | tf_op jit(solution)/shard_map/all_to_all | solution.py:282
  143.2 0.7 finish.1
  (2 shorter events, 0.0 us)
Async XLA Ops:
  0.0 39.7 %copy-start.1 = (f32[6144]{0:T(1024)S(1)}, f32[6144]{0:T(1024)}, u32[]{:S(2)}) copy-start(f32[6144]{0:T(1024)} %param.9) | copy-start | bytes 73732
  0.0 39.9 %copy-start = (f32[4096]{0:T(1024)S(1)}, f32[4096]{0:T(1024)}, u32[]{:S(2)}) copy-start(f32[4096]{0:T(1024)} %param.11) | copy-start | bytes 49156
  27.2 34.5 %all-to-all-start.1 = ((bf16[8,192,128]{2,1,0:T(8,128)(2,1)}), bf16[8,192,128]{2,1,0:T(8,128)(2,1)S(1)}, u32[]{:S(2)}, u32[]{:S(2)}) async-start(bf16[8,192,128]{2,1,0:T(8,128)(2,1)} %bitcast.5), calls=%async_computation.1 | async-start | bytes 786432 | tf_op jit(solution)/shard_map/all_to_all | solution.py:218
  35.8 21.8 %collective-permute-start = (bf16[1,128,2048]{2,1,0:T(8,128)(2,1)S(1)}, bf16[1,128,2048]{2,1,0:T(8,128)(2,1)S(1)}, u32[]{:S(2)}, u32[]{:S(2)}) collective-permute-start(bf16[1,128,2048]{2,1,0:T(8,128)(2,1)S(1)} %pick.2), channel_id=1, source_target_pairs={{0,8},{8,0},{1,9},{9,1},{2,10},{10,2},{3,11},{11,3},{4,12},{12,4},... | collective-permute-start | bytes 1572872 | tf_op jit(solution)/shard_map/ppermute | solution.py:210
  59.2 55.5 %collective-permute-start.1 = (bf16[2,128,1024]{2,1,0:T(8,128)(2,1)S(1)}, bf16[2,128,1024]{2,1,0:T(8,128)(2,1)S(1)}, u32[]{:S(2)}, u32[]{:S(2)}) collective-permute-start(bf16[2,128,1024]{2,1,0:T(8,128)(2,1)S(1)} %get-tuple-element.11), channel_id=1, source_target_pairs={{0,1},{1,0},{2,3},{3,2},{4,5},{5,4},{6,7},{7,6},{8,9},{9,8},{10,11... | collective-permute-start | bytes 1572872 | tf_op jit(solution)/shard_map/ppermute | solution.py:213
  109.9 9.4 %all-to-all-start.2 = ((bf16[4,256,128]{2,1,0:T(8,128)(2,1)}), bf16[4,256,128]{2,1,0:T(8,128)(2,1)S(1)}, u32[]{:S(2)}, u32[]{:S(2)}) async-start(bf16[4,256,128]{2,1,0:T(8,128)(2,1)} %attention.1), calls=%async_computation.2 | async-start | bytes 524288 | tf_op jit(solution)/shard_map/all_to_all | solution.py:272

commit v6 on v5

--- a/solution.py
+++ b/solution.py
@@ -162,6 +162,23 @@
     )(jnp.stack(origins).astype(jnp.int32), in_hbm(sources[0]), *sources[1:])
 
 
+def deal_kernel(visual_ref, dealt_ref):
+    planes, halves = dealt_ref.shape[:2]
+    dealt = jnp.swapaxes(visual_ref[...].astype(jnp.float32), 0, 1).astype(jnp.bfloat16)
+    for h in range(halves):
+        for p in range(planes):
+            dealt_ref[p, h] = dealt[h * planes + p]
+
+
+def spread_kernel(relayed_ref, blocks_ref):
+    planes, halves, tokens, features = relayed_ref.shape
+    copies = blocks_ref.shape[0] // halves
+    for h in range(halves):
+        block = relayed_ref[:, h].astype(jnp.float32).reshape(planes * tokens, features).T.astype(jnp.bfloat16)
+        for k in range(copies):
+            blocks_ref[h * copies + k] = block
+
+
 def turn_kernel(column_ref, turned_ref):
     halves, _, half_tokens = column_ref.shape
     for h in range(halves):
@@ -172,10 +189,10 @@
 def project_kernel(member_ref, group_ref, *refs):
     *chunk_refs, part_ref = refs
     part = jnp.zeros(part_ref.shape, jnp.float32)
-    for across_x, chunk_ref in enumerate(chunk_refs):
-        for across_y in range(chunk_ref.shape[0]):
+    for across_y, chunk_ref in enumerate(chunk_refs):
+        for across_x in range(chunk_ref.shape[0]):
             there = member_ref[0] ^ (2 * across_y + across_x)
-            part += jnp.dot(group_ref[there], chunk_ref[across_y], preferred_element_type=jnp.float32)
+            part += jnp.dot(group_ref[there], chunk_ref[across_x], preferred_element_type=jnp.float32)
     part_ref[...] = part.astype(jnp.bfloat16)
 
 
@@ -183,7 +200,7 @@
     row_0, row_1, col_0, col_1, _, width = parts_ref.shape
     for r in range(row_1):
         for c in range(col_1):
-            here = pl.ds((r * col_1 + c) * width, width)
+            here = pl.ds((c * row_1 + r) * width, width)
             total = residual_ref[:, here]
             for i in range(row_0):
                 for j in range(col_0):
@@ -200,21 +217,33 @@
     tokens_here = text_tokens // devices
     width = DEC // quad
     member = lax.axis_index(QUAD)
-    relayed = visual.reshape(tokens, halves, planes, features).transpose(2, 1, 0, 3)
+    relayed = pl.pallas_call(
+        deal_kernel,
+        out_shape=jax.ShapeDtypeStruct((planes, halves, tokens, features), jnp.bfloat16),
+        in_specs=[pl.BlockSpec(memory_space=pltpu.VMEM)],
+        out_specs=pl.BlockSpec(memory_space=pltpu.VMEM),
+        compiler_params=pltpu.CompilerParams(vmem_limit_bytes=4 << 20),
+        name="deal",
+    )(visual)
     relayed = lax.all_to_all(relayed, "dp_1", 0, 0, tiled=True)
     row, col = (lax.axis_index(a) for a in QUAD)
     swap = [(0, 1), (1, 0)]
     half = DEC // 2
     quarter = jax.ShapeDtypeStruct((2, HEAD_DIM, width), jnp.bfloat16)
-    send = pick_columns([out_weight], [(1 - row) * half], jax.ShapeDtypeStruct((1, HEAD_DIM, half), jnp.bfloat16))[0]
-    beyond = lax.ppermute(send, QUAD[0], swap)[0]
-    origins = [[row * half + c * width, c * width] for c in (col, 1 - col)]
+    send = pick_columns([out_weight], [(1 - col) * half], jax.ShapeDtypeStruct((1, HEAD_DIM, half), jnp.bfloat16))[0]
+    beyond = lax.ppermute(send, QUAD[1], swap)[0]
+    origins = [[col * half + r * width, r * width] for r in (row, 1 - row)]
     keep, send = pick_columns([out_weight, beyond], origins[0] + origins[1], quarter, quarter)
-    out_rows = [keep, lax.ppermute(send, QUAD[1], swap)]
+    out_rows = [keep, lax.ppermute(send, QUAD[0], swap)]
     half_tokens = planes * tokens
-    blocks = relayed.transpose(1, 3, 0, 2).reshape(halves, 1, features, half_tokens)
-    blocks = jnp.broadcast_to(blocks, (halves, rows, features, half_tokens))
-    blocks = blocks.reshape(halves * rows, features, half_tokens)
+    blocks = pl.pallas_call(
+        spread_kernel,
+        out_shape=jax.ShapeDtypeStruct((halves * rows, features, half_tokens), jnp.bfloat16),
+        in_specs=[pl.BlockSpec(memory_space=pltpu.VMEM)],
+        out_specs=pl.BlockSpec(memory_space=pltpu.VMEM),
+        compiler_params=pltpu.CompilerParams(vmem_limit_bytes=4 << 20),
+        name="spread",
+    )(in_vmem(relayed))
     column = lax.all_to_all(blocks, ("dp_0",) + ROW, 0, 0, tiled=True)
     flat = text.reshape(text_tokens, DEC)
     queries, residual = pl.pallas_call(

time: 144 us -> 130 us (0.903)
  blocking collectives: 91.7 us -> 82.8 us
  waiting for transfers between devices: 18.6 us -> 14.4 us
    all_gather x1, blocking collectives: 43.3 us -> 35.2 us  [attend(): whole = lax.all_gather(column, COL, axis=0, tiled=True)]
    ppermute x2, waiting for transfers between devices: 14 us -> 9.82 us  [the longest x1 9.82 us: attend(): beyond = lax.ppermute(send, QUAD[1], swap)[0]]
  transfers between devices with their start and end apart: 4 -> 4, of which waited for: 2 -> 2; matrix products, arithmetic and copies ran while one was open for 1% -> 1% of each run, Pallas kernels for 7% -> 8%
where the time goes in v6:
time: 130 us
  blocking collectives  82.8 us (64%)
  starting transfers between devices  17.6 us (14%)
  waiting for transfers between devices  14.4 us (11%)
  Pallas kernels  12.9 us (10%)
    all_gather x1, blocking collectives, attend(): whole = lax.all_gather(column, COL, axis=0, tiled=True)  35.2 us
    all_to_all x1, blocking collectives, attend(): relayed = lax.all_to_all(relayed, 'dp_1', 0, 0, tiled=True)  25.2 us
    all_to_all x1, blocking collectives, attend(): lax.all_to_all(part.reshape(devices, tokens_here, width), MP, 0, 0, tiled...  22.4 us
    ppermute x1, waiting for transfers between devices, attend(): beyond = lax.ppermute(send, QUAD[1], swap)[0]  9.82 us
    all_to_all x1, starting transfers between devices, attend(): column = lax.all_to_all(blocks, ('dp_0',) + ROW, 0, 0, tiled=True)  7.56 us
    all_to_all x1, waiting for transfers between devices, attend(): group = lax.all_to_all(contexts, QUAD, 0, 0, tiled=True)  4.62 us
    pallas_call x1, Pallas kernels, attend(): pl.pallas_call(attention_kernel, out_shape=jax.ShapeDtypeStruct((quad, te...  4.23 us
    all_to_all x1, starting transfers between devices, attend(): group = lax.all_to_all(contexts, QUAD, 0, 0, tiled=True)  3.91 us
  transfers between devices with their start and end apart: 4, of which 2 were waited for; matrix products, arithmetic and copies ran while one was open for 1% of the time, Pallas kernels for 8%

profile of v6, /device:TPU:2, one launch (start us, length us, event | category | flops | bytes accessed | tf_op | source)
XLA Modules:
  0.0 129.6 jit_solution(8894323946480055472)
XLA Ops:
  0.0 0.0 copy-start
  0.0 0.9 copy-done
  0.9 0.0 copy-start.2
  0.9 0.0 copy-start.1
  0.9 0.1 deal.1
  1.0 25.2 %all_to_all.20.relayed_ref = bf16[16,2,8,192]{3,2,1,0:T(8,128)(2,1)S(1)} all-to-all(bf16[16,2,8,192]{3,2,1,0:T(8,128)(2,1)S(1)} %deal.1), channel_id=1, replica_groups=mesh['dp_0'=2,'dp_1'=16,'row_0'=2,'row_1'=2,'col_0'=4,'col_1'=2] {'dp_1'}, dimensions={0} | all-to-all | bytes 196608 | tf_op jit(solution)/shard_map/all_to_all | solution.py:228
  26.2 0.9 spread.1
  27.1 7.6 %all-to-all-start.1 = ((bf16[8,192,128]{2,1,0:T(8,128)(2,1)}), bf16[8,192,128]{2,1,0:T(8,128)(2,1)S(1)}, u32[]{:S(2)}, u32[]{:S(2)}) async-start(bf16[8,192,128]{2,1,0:T(8,128)(2,1)} %spread.1), calls=%async_computation.1 | async-start | bytes 786432 | tf_op jit(solution)/shard_map/all_to_all | solution.py:247
  34.6 1.0 pick.2
  35.7 2.4 %collective-permute-start = (bf16[1,128,2048]{2,1,0:T(8,128)(2,1)S(1)}, bf16[1,128,2048]{2,1,0:T(8,128)(2,1)S(1)}, u32[]{:S(2)}, u32[]{:S(2)}) collective-permute-start(bf16[1,128,2048]{2,1,0:T(8,128)(2,1)S(1)} %pick.2), channel_id=1, source_target_pairs={{0,1},{1,0},{2,3},{3,2},{4,5},{5,4},{6,7},{7,6},{8,9},{9,8},{10,11... | collective-permute-start | bytes 1572872 | tf_op jit(solution)/shard_map/ppermute | solution.py:234
  38.1 0.0 copy-done.2
  38.1 0.1 reshape.42
  38.2 0.1 reshape.43.gain_ref
  38.3 0.0 copy-done.1
  38.3 3.5 %query.1 = (bf16[256,128]{1,0:T(8,128)(2,1)S(1)}, f32[8,4096]{1,0:T(8,128)S(1)}) custom-call(s32[1]{0:T(128)} %bitcast.4.origin_ref, bf16[256,4096]{1,0:T(8,128)(2,1)} %bitcast.24, bf16[4096,128]{1,0:T(8,128)(2,1)} %weight_hbm_ref.1, f32[1,4096]{1,0:T(1,128)S(1)} %bitcast.23), custom_call_target="tpu_custom_call" | custom-call | tf_op jit(solution)/shard_map/query/pallas_call | solution.py:249
  41.9 0.1 pad_add_fusion.origins_ref
  42.0 9.8 %collective-permute-done = bf16[1,128,2048]{2,1,0:T(8,128)(2,1)S(1)} collective-permute-done((bf16[1,128,2048]{2,1,0:T(8,128)(2,1)S(1)}, bf16[1,128,2048]{2,1,0:T(8,128)(2,1)S(1)}, u32[]{:S(2)}, u32[]{:S(2)}) %collective-permute-start) | collective-permute-done | bytes 524320 | tf_op jit(solution)/shard_map/ppermute | solution.py:234
  51.8 1.6 %pick.3 = (bf16[2,128,1024]{2,1,0:T(8,128)(2,1)S(1)}, bf16[2,128,1024]{2,1,0:T(8,128)(2,1)S(1)}) custom-call(s32[4]{0:T(128)S(1)} %pad_add_fusion.origins_ref, bf16[128,4096]{1,0:T(8,128)(2,1)} %refs_0_.3, bf16[128,2048]{1,0:T(8,128)(2,1)S(1)} %bitcast.22), custom_call_target="tpu_custom_call" | custom-call | tf_op jit(solution)/shard_map/pick/pallas_call | solution.py:154
  53.4 3.6 %collective-permute-start.1 = (bf16[2,128,1024]{2,1,0:T(8,128)(2,1)S(1)}, bf16[2,128,1024]{2,1,0:T(8,128)(2,1)S(1)}, u32[]{:S(2)}, u32[]{:S(2)}) collective-permute-start(bf16[2,128,1024]{2,1,0:T(8,128)(2,1)S(1)} %get-tuple-element.11), channel_id=1, source_target_pairs={{0,8},{8,0},{1,9},{9,1},{2,10},{10,2},{3,11},{11,3},{4,12},{12,4},... | collective-permute-start | bytes 1572872 | tf_op jit(solution)/shard_map/ppermute | solution.py:237
  57.1 0.0 all-to-all-done.1
  57.1 0.2 turn.1
  57.2 0.1 multiply_convert_fusion
  57.3 35.2 %all-gather.1 = f16[2048,768]{1,0:T(8,128)(2,1)S(1)} all-gather(f16[256,768]{1,0:T(8,128)(2,1)S(1)} %multiply_convert_fusion), channel_id=1, replica_groups=mesh['dp_0'=2,'dp_1'=16,'row_0'=2,'row_1'=2,'col_0'=4,'col_1'=2] {'col_0..., dimensions={0}, use_global_device_ids=true | all-gather | bytes 3538944 | tf_op jit(solution)/shard_map/all_gather | solution.py:283
  92.6 0.5 convert_element_type.11
  93.0 4.2 %attention.1 = bf16[4,256,128]{2,1,0:T(8,128)(2,1)} custom-call(bf16[8,256,768]{2,1,0:T(8,128)(2,1)S(1)} %bitcast.18, f32[8,768]{1,0:T(8,128)S(1)} %reshape.43.gain_ref, bf16[256,128]{1,0:T(8,128)(2,1)S(1)} %get-tuple-element.9.queries_ref, bf16[32,192,128]{2,1,0:T(8,128)(2,1)} %bitcast.25, bf16[32,192,128]{2,1,0:T(8,128)(2,1)} %bitcast.26), custom_call_target="tpu_custom_call" | custom-call | tf_op jit(solution)/shard_map/attention/pallas_call | solution.py:287
  97.3 3.9 %all-to-all-start.2 = ((bf16[4,256,128]{2,1,0:T(8,128)(2,1)}), bf16[4,256,128]{2,1,0:T(8,128)(2,1)S(1)}, u32[]{:S(2)}, u32[]{:S(2)}) async-start(bf16[4,256,128]{2,1,0:T(8,128)(2,1)} %attention.1), calls=%async_computation.2 | async-start | bytes 524288 | tf_op jit(solution)/shard_map/all_to_all | solution.py:301
  101.2 0.0 collective-permute-done.1.refs_1_
  101.2 4.6 %all-to-all-done.2.group_ref = bf16[4,256,128]{2,1,0:T(8,128)(2,1)S(1)} async-done(((bf16[4,256,128]{2,1,0:T(8,128)(2,1)}), bf16[4,256,128]{2,1,0:T(8,128)(2,1)S(1)}, u32[]{:S(2)}, u32[]{:S(2)}) %all-to-all-start.2) | async-done | bytes 262176 | tf_op jit(solution)/shard_map/all_to_all | solution.py:301
  105.8 0.7 project.1
  106.5 22.4 %all_to_all.21 = bf16[32,8,1024]{2,1,0:T(8,128)(2,1)S(1)} all-to-all(bf16[32,8,1024]{2,1,0:T(8,128)(2,1)S(1)} %bitcast.20), channel_id=1, replica_groups=mesh['dp_0'=2,'dp_1'=16,'row_0'=2,'row_1'=2,'col_0'=4,'col_1'=2] {'row_0..., dimensions={0} | all-to-all | bytes 1048576 | tf_op jit(solution)/shard_map/all_to_all | solution.py:311
  128.9 0.7 finish.1
  (1 shorter events, 0.0 us)
Async XLA Ops:
  0.0 0.9 copy-start
  0.9 37.2 %copy-start.2 = (f32[6144]{0:T(1024)S(1)}, f32[6144]{0:T(1024)}, u32[]{:S(2)}) copy-start(f32[6144]{0:T(1024)} %param.9) | copy-start | bytes 73732
  0.9 37.4 %copy-start.1 = (f32[4096]{0:T(1024)S(1)}, f32[4096]{0:T(1024)}, u32[]{:S(2)}) copy-start(f32[4096]{0:T(1024)} %param.11) | copy-start | bytes 49156
  27.1 30.0 %all-to-all-start.1 = ((bf16[8,192,128]{2,1,0:T(8,128)(2,1)}), bf16[8,192,128]{2,1,0:T(8,128)(2,1)S(1)}, u32[]{:S(2)}, u32[]{:S(2)}) async-start(bf16[8,192,128]{2,1,0:T(8,128)(2,1)} %spread.1), calls=%async_computation.1 | async-start | bytes 786432 | tf_op jit(solution)/shard_map/all_to_all | solution.py:247
  35.7 16.1 %collective-permute-start = (bf16[1,128,2048]{2,1,0:T(8,128)(2,1)S(1)}, bf16[1,128,2048]{2,1,0:T(8,128)(2,1)S(1)}, u32[]{:S(2)}, u32[]{:S(2)}) collective-permute-start(bf16[1,128,2048]{2,1,0:T(8,128)(2,1)S(1)} %pick.2), channel_id=1, source_target_pairs={{0,1},{1,0},{2,3},{3,2},{4,5},{5,4},{6,7},{7,6},{8,9},{9,8},{10,11... | collective-permute-start | bytes 1572872 | tf_op jit(solution)/shard_map/ppermute | solution.py:234
  53.4 47.8 %collective-permute-start.1 = (bf16[2,128,1024]{2,1,0:T(8,128)(2,1)S(1)}, bf16[2,128,1024]{2,1,0:T(8,128)(2,1)S(1)}, u32[]{:S(2)}, u32[]{:S(2)}) collective-permute-start(bf16[2,128,1024]{2,1,0:T(8,128)(2,1)S(1)} %get-tuple-element.11), channel_id=1, source_target_pairs={{0,8},{8,0},{1,9},{9,1},{2,10},{10,2},{3,11},{11,3},{4,12},{12,4},... | collective-permute-start | bytes 1572872 | tf_op jit(solution)/shard_map/ppermute | solution.py:237
  97.3 8.5 %all-to-all-start.2 = ((bf16[4,256,128]{2,1,0:T(8,128)(2,1)}), bf16[4,256,128]{2,1,0:T(8,128)(2,1)S(1)}, u32[]{:S(2)}, u32[]{:S(2)}) async-start(bf16[4,256,128]{2,1,0:T(8,128)(2,1)} %attention.1), calls=%async_computation.2 | async-start | bytes 524288 | tf_op jit(solution)/shard_map/all_to_all | solution.py:301

commit v7 on v6

--- a/solution.py
+++ b/solution.py
@@ -9,7 +9,6 @@
 
 DEC = 4096
 HEAD_DIM = 128
-DP = ("dp_0", "dp_1")
 ROW = ("row_0", "row_1")
 COL = ("col_0", "col_1")
 MP = ROW + COL
@@ -163,27 +162,18 @@
 
 
 def deal_kernel(visual_ref, dealt_ref):
-    planes, halves = dealt_ref.shape[:2]
-    dealt = jnp.swapaxes(visual_ref[...].astype(jnp.float32), 0, 1).astype(jnp.bfloat16)
-    for h in range(halves):
-        for p in range(planes):
-            dealt_ref[p, h] = dealt[h * planes + p]
+    dealt_ref[...] = jnp.swapaxes(visual_ref[...].astype(jnp.float32), 0, 1).astype(jnp.bfloat16)
 
 
 def spread_kernel(relayed_ref, blocks_ref):
-    planes, halves, tokens, features = relayed_ref.shape
-    copies = blocks_ref.shape[0] // halves
-    for h in range(halves):
-        block = relayed_ref[:, h].astype(jnp.float32).reshape(planes * tokens, features).T.astype(jnp.bfloat16)
-        for k in range(copies):
-            blocks_ref[h * copies + k] = block
+    images, tokens, features = relayed_ref.shape
+    block = relayed_ref[...].astype(jnp.float32).reshape(images * tokens, features).T.astype(jnp.bfloat16)
+    for k in range(blocks_ref.shape[0]):
+        blocks_ref[k] = block
 
 
 def turn_kernel(column_ref, turned_ref):
-    halves, _, half_tokens = column_ref.shape
-    for h in range(halves):
-        turned = column_ref[h].astype(jnp.float32).T
-        turned_ref[pl.ds(h * half_tokens, half_tokens), :] = turned.astype(jnp.bfloat16)
+    turned_ref[...] = column_ref[...].astype(jnp.float32).T.astype(jnp.bfloat16)
 
 
 def project_kernel(member_ref, group_ref, *refs):
@@ -210,7 +200,7 @@
 
 def attend(visual, vis_gain, text, text_gain, query_weight, key_weight, value_weight, out_weight):
     rows, cols, quad = (lax.axis_size(a) for a in (ROW, COL, QUAD))
-    halves, planes = (lax.axis_size(a) for a in DP)
+    images = lax.axis_size("dp")
     devices = rows * cols
     tokens, _, features = visual.shape
     text_tokens = text.shape[0]
@@ -219,13 +209,13 @@
     member = lax.axis_index(QUAD)
     relayed = pl.pallas_call(
         deal_kernel,
-        out_shape=jax.ShapeDtypeStruct((planes, halves, tokens, features), jnp.bfloat16),
+        out_shape=jax.ShapeDtypeStruct((images, tokens, features), jnp.bfloat16),
         in_specs=[pl.BlockSpec(memory_space=pltpu.VMEM)],
         out_specs=pl.BlockSpec(memory_space=pltpu.VMEM),
         compiler_params=pltpu.CompilerParams(vmem_limit_bytes=4 << 20),
         name="deal",
     )(visual)
-    relayed = lax.all_to_all(relayed, "dp_1", 0, 0, tiled=True)
+    relayed = lax.all_to_all(relayed, "dp", 0, 0, tiled=True)
     row, col = (lax.axis_index(a) for a in QUAD)
     swap = [(0, 1), (1, 0)]
     half = DEC // 2
@@ -235,16 +225,16 @@
     origins = [[col * half + r * width, r * width] for r in (row, 1 - row)]
     keep, send = pick_columns([out_weight, beyond], origins[0] + origins[1], quarter, quarter)
     out_rows = [keep, lax.ppermute(send, QUAD[0], swap)]
-    half_tokens = planes * tokens
+    vis_tokens = images * tokens
     blocks = pl.pallas_call(
         spread_kernel,
-        out_shape=jax.ShapeDtypeStruct((halves * rows, features, half_tokens), jnp.bfloat16),
+        out_shape=jax.ShapeDtypeStruct((rows, features, vis_tokens), jnp.bfloat16),
         in_specs=[pl.BlockSpec(memory_space=pltpu.VMEM)],
         out_specs=pl.BlockSpec(memory_space=pltpu.VMEM),
         compiler_params=pltpu.CompilerParams(vmem_limit_bytes=4 << 20),
         name="spread",
     )(in_vmem(relayed))
-    column = lax.all_to_all(blocks, ("dp_0",) + ROW, 0, 0, tiled=True)
+    column = lax.all_to_all(blocks, ROW, 0, 0, tiled=True)
     flat = text.reshape(text_tokens, DEC)
     queries, residual = pl.pallas_call(
         query_kernel,
@@ -273,15 +263,15 @@
     gain = vis_gain.reshape(rows, cols, features).transpose(1, 0, 2).reshape(cols, rows * features)
     column = pl.pallas_call(
         turn_kernel,
-        out_shape=jax.ShapeDtypeStruct((halves * half_tokens, rows * features), jnp.bfloat16),
+        out_shape=jax.ShapeDtypeStruct((vis_tokens, rows * features), jnp.bfloat16),
         in_specs=[pl.BlockSpec(memory_space=pltpu.VMEM)],
         out_specs=pl.BlockSpec(memory_space=pltpu.VMEM),
         compiler_params=pltpu.CompilerParams(vmem_limit_bytes=4 << 20),
         name="turn",
-    )(in_vmem(column.reshape(halves, rows * features, half_tokens)))
+    )(in_vmem(column.reshape(rows * features, vis_tokens)))
     column = (column.astype(jnp.float32) * SCALE).astype(jnp.float16)
     whole = lax.all_gather(column, COL, axis=0, tiled=True)
-    whole = whole.astype(jnp.bfloat16).reshape(cols, halves * half_tokens, rows * features)
+    whole = whole.astype(jnp.bfloat16).reshape(cols, vis_tokens, rows * features)
     operands = [in_vmem(v) for v in (whole, gain, queries)]
     operands += [in_hbm(w.reshape(devices, features, HEAD_DIM)) for w in (key_weight, value_weight)]
     contexts = pl.pallas_call(
@@ -322,16 +312,16 @@
 
 
 def solution(mesh):
-    split = Mesh(mesh.devices.reshape(2, mesh.shape["dp"] // 2, 2, 2, 4, 2), DP + MP)
+    split = Mesh(mesh.devices.reshape(mesh.shape["dp"], 2, 2, 4, 2), ("dp",) + MP)
     in_specs = (
-        P(DP, None, MP),
+        P("dp", None, MP),
         P(),
-        P(None, DP, None),
+        P(None, "dp", None),
         P(),
         P(None, MP),
         P(None, MP),
         P(None, MP),
         P(MP, None),
     )
-    out_specs = P(MP, DP, None)
+    out_specs = P(MP, "dp", None)
     return jax.shard_map(attend, mesh=split, in_specs=in_specs, out_specs=out_specs, check_vma=False)

time: 130 us -> 135 us (1.038)
  blocking collectives: 82.8 us -> 91.5 us
  starting transfers between devices: 17.6 us -> 14.8 us
    all_to_all x1, blocking collectives: 25.2 us -> 35.6 us  [attend(): relayed = lax.all_to_all(relayed, 'dp', 0, 0, tiled=True)]
    all_to_all x1, starting transfers between devices: 7.56 us -> 3.46 us  [attend(): column = lax.all_to_all(blocks, ROW, 0, 0, tiled=True)]
where the time goes in v7:
time: 135 us
  blocking collectives  91.5 us (68%)
  starting transfers between devices  14.8 us (11%)
  waiting for transfers between devices  13.4 us (10%)
  Pallas kernels  12.9 us (10%)
    all_to_all x1, blocking collectives, attend(): relayed = lax.all_to_all(relayed, 'dp', 0, 0, tiled=True)  35.6 us
    all_gather x1, blocking collectives, attend(): whole = lax.all_gather(column, COL, axis=0, tiled=True)  34.6 us
    all_to_all x1, blocking collectives, attend(): lax.all_to_all(part.reshape(devices, tokens_here, width), MP, 0, 0, tiled...  21.3 us
    ppermute x1, waiting for transfers between devices, attend(): beyond = lax.ppermute(send, QUAD[1], swap)[0]  8.77 us
    all_to_all x1, starting transfers between devices, attend(): group = lax.all_to_all(contexts, QUAD, 0, 0, tiled=True)  4.86 us
    all_to_all x1, waiting for transfers between devices, attend(): group = lax.all_to_all(contexts, QUAD, 0, 0, tiled=True)  4.62 us
    pallas_call x1, Pallas kernels, attend(): pl.pallas_call(attention_kernel, out_shape=jax.ShapeDtypeStruct((quad, te...  4.22 us
    ppermute x1, starting transfers between devices, attend(): out_rows = [keep, lax.ppermute(send, QUAD[0], swap)]  4.04 us
  transfers between devices with their start and end apart: 4, of which 2 were waited for; matrix products, arithmetic and copies ran while one was open for 1% of the time, Pallas kernels for 8%

profile of v7, /device:TPU:2, one launch (start us, length us, event | category | flops | bytes accessed | tf_op | source)
XLA Modules:
  0.0 134.5 jit_solution(5998542639463026191)
XLA Ops:
  0.0 0.0 copy-start
  0.0 0.9 copy-done
  0.9 0.0 copy-start.2
  0.9 0.0 copy-start.1
  0.9 0.1 deal.1
  1.0 35.6 %all_to_all.20.relayed_ref = bf16[32,8,192]{2,1,0:T(8,128)(2,1)S(1)} all-to-all(bf16[32,8,192]{2,1,0:T(8,128)(2,1)S(1)} %deal.1), channel_id=1, replica_groups=mesh['dp'=32,'row_0'=2,'row_1'=2,'col_0'=4,'col_1'=2] {'dp'}, dimensions={0} | all-to-all | bytes 196608 | tf_op jit(solution)/shard_map/all_to_all | solution.py:218
  36.6 0.9 spread.1
  37.5 3.5 %all-to-all-start.1 = ((bf16[4,192,256]{2,1,0:T(8,128)(2,1)}), bf16[4,192,256]{2,1,0:T(8,128)(2,1)S(1)}, u32[]{:S(2)}, u32[]{:S(2)}) async-start(bf16[4,192,256]{2,1,0:T(8,128)(2,1)} %spread.1), calls=%async_computation.1 | async-start | bytes 786432 | tf_op jit(solution)/shard_map/all_to_all | solution.py:237
  40.9 1.1 pick.2
  42.0 2.4 %collective-permute-start = (bf16[1,128,2048]{2,1,0:T(8,128)(2,1)S(1)}, bf16[1,128,2048]{2,1,0:T(8,128)(2,1)S(1)}, u32[]{:S(2)}, u32[]{:S(2)}) collective-permute-start(bf16[1,128,2048]{2,1,0:T(8,128)(2,1)S(1)} %pick.2), channel_id=1, source_target_pairs={{0,1},{1,0},{2,3},{3,2},{4,5},{5,4},{6,7},{7,6},{8,9},{9,8},{10,11... | collective-permute-start | bytes 1572872 | tf_op jit(solution)/shard_map/ppermute | solution.py:224
  44.5 0.0 copy-done.2
  44.5 0.1 reshape.42
  44.6 0.1 reshape.43.gain_ref
  44.7 0.0 copy-done.1
  44.7 3.5 %query.1 = (bf16[256,128]{1,0:T(8,128)(2,1)S(1)}, f32[8,4096]{1,0:T(8,128)S(1)}) custom-call(s32[1]{0:T(128)} %bitcast.4.origin_ref, bf16[256,4096]{1,0:T(8,128)(2,1)} %bitcast.24, bf16[4096,128]{1,0:T(8,128)(2,1)} %weight_hbm_ref.1, f32[1,4096]{1,0:T(1,128)S(1)} %bitcast.23), custom_call_target="tpu_custom_call" | custom-call | tf_op jit(solution)/shard_map/query/pallas_call | solution.py:239
  48.2 0.1 pad_add_fusion.origins_ref
  48.3 8.8 %collective-permute-done = bf16[1,128,2048]{2,1,0:T(8,128)(2,1)S(1)} collective-permute-done((bf16[1,128,2048]{2,1,0:T(8,128)(2,1)S(1)}, bf16[1,128,2048]{2,1,0:T(8,128)(2,1)S(1)}, u32[]{:S(2)}, u32[]{:S(2)}) %collective-permute-start) | collective-permute-done | bytes 524320 | tf_op jit(solution)/shard_map/ppermute | solution.py:224
  57.1 1.6 %pick.3 = (bf16[2,128,1024]{2,1,0:T(8,128)(2,1)S(1)}, bf16[2,128,1024]{2,1,0:T(8,128)(2,1)S(1)}) custom-call(s32[4]{0:T(128)S(1)} %pad_add_fusion.origins_ref, bf16[128,4096]{1,0:T(8,128)(2,1)} %refs_0_.3, bf16[128,2048]{1,0:T(8,128)(2,1)S(1)} %bitcast.22), custom_call_target="tpu_custom_call" | custom-call | tf_op jit(solution)/shard_map/pick/pallas_call | solution.py:153
  58.7 4.0 %collective-permute-start.1 = (bf16[2,128,1024]{2,1,0:T(8,128)(2,1)S(1)}, bf16[2,128,1024]{2,1,0:T(8,128)(2,1)S(1)}, u32[]{:S(2)}, u32[]{:S(2)}) collective-permute-start(bf16[2,128,1024]{2,1,0:T(8,128)(2,1)S(1)} %get-tuple-element.11), channel_id=1, source_target_pairs={{0,8},{8,0},{1,9},{9,1},{2,10},{10,2},{3,11},{11,3},{4,12},{12,4},... | collective-permute-start | bytes 1572872 | tf_op jit(solution)/shard_map/ppermute | solution.py:227
  62.7 0.0 all-to-all-done.1
  62.7 0.2 turn.1
  62.9 0.1 multiply_convert_fusion
  63.0 34.6 %all-gather.1 = f16[2048,768]{1,0:T(8,128)(2,1)S(1)} all-gather(f16[256,768]{1,0:T(8,128)(2,1)S(1)} %multiply_convert_fusion), channel_id=1, replica_groups=mesh['dp'=32,'row_0'=2,'row_1'=2,'col_0'=4,'col_1'=2] {'col_0','col_1'}, dimensions={0}, use_global_device_ids=true | all-gather | bytes 3538944 | tf_op jit(solution)/shard_map/all_gather | solution.py:273
  97.6 0.5 convert_element_type.11
  98.1 4.2 %attention.1 = bf16[4,256,128]{2,1,0:T(8,128)(2,1)} custom-call(bf16[8,256,768]{2,1,0:T(8,128)(2,1)S(1)} %bitcast.18, f32[8,768]{1,0:T(8,128)S(1)} %reshape.43.gain_ref, bf16[256,128]{1,0:T(8,128)(2,1)S(1)} %get-tuple-element.9.queries_ref, bf16[32,192,128]{2,1,0:T(8,128)(2,1)} %bitcast.25, bf16[32,192,128]{2,1,0:T(8,128)(2,1)} %bitcast.26), custom_call_target="tpu_custom_call" | custom-call | tf_op jit(solution)/shard_map/attention/pallas_call | solution.py:277
  102.3 4.9 %all-to-all-start.2 = ((bf16[4,256,128]{2,1,0:T(8,128)(2,1)}), bf16[4,256,128]{2,1,0:T(8,128)(2,1)S(1)}, u32[]{:S(2)}, u32[]{:S(2)}) async-start(bf16[4,256,128]{2,1,0:T(8,128)(2,1)} %attention.1), calls=%async_computation.2 | async-start | bytes 524288 | tf_op jit(solution)/shard_map/all_to_all | solution.py:291
  107.2 0.0 collective-permute-done.1.refs_1_
  107.2 4.6 %all-to-all-done.2.group_ref = bf16[4,256,128]{2,1,0:T(8,128)(2,1)S(1)} async-done(((bf16[4,256,128]{2,1,0:T(8,128)(2,1)}), bf16[4,256,128]{2,1,0:T(8,128)(2,1)S(1)}, u32[]{:S(2)}, u32[]{:S(2)}) %all-to-all-start.2) | async-done | bytes 262176 | tf_op jit(solution)/shard_map/all_to_all | solution.py:291
  111.8 0.7 project.1
  112.5 21.3 %all_to_all.21 = bf16[32,8,1024]{2,1,0:T(8,128)(2,1)S(1)} all-to-all(bf16[32,8,1024]{2,1,0:T(8,128)(2,1)S(1)} %bitcast.20), channel_id=1, replica_groups=mesh['dp'=32,'row_0'=2,'row_1'=2,'col_0'=4,'col_1'=2] {'row_0','row_1','..., dimensions={0} | all-to-all | bytes 1048576 | tf_op jit(solution)/shard_map/all_to_all | solution.py:301
  133.8 0.7 finish.1
  (1 shorter events, 0.0 us)
Async XLA Ops:
  0.0 0.9 copy-start
  0.9 43.6 %copy-start.2 = (f32[6144]{0:T(1024)S(1)}, f32[6144]{0:T(1024)}, u32[]{:S(2)}) copy-start(f32[6144]{0:T(1024)} %param.9) | copy-start | bytes 73732
  0.9 43.8 %copy-start.1 = (f32[4096]{0:T(1024)S(1)}, f32[4096]{0:T(1024)}, u32[]{:S(2)}) copy-start(f32[4096]{0:T(1024)} %param.11) | copy-start | bytes 49156
  37.5 25.3 %all-to-all-start.1 = ((bf16[4,192,256]{2,1,0:T(8,128)(2,1)}), bf16[4,192,256]{2,1,0:T(8,128)(2,1)S(1)}, u32[]{:S(2)}, u32[]{:S(2)}) async-start(bf16[4,192,256]{2,1,0:T(8,128)(2,1)} %spread.1), calls=%async_computation.1 | async-start | bytes 786432 | tf_op jit(solution)/shard_map/all_to_all | solution.py:237
  42.0 15.0 %collective-permute-start = (bf16[1,128,2048]{2,1,0:T(8,128)(2,1)S(1)}, bf16[1,128,2048]{2,1,0:T(8,128)(2,1)S(1)}, u32[]{:S(2)}, u32[]{:S(2)}) collective-permute-start(bf16[1,128,2048]{2,1,0:T(8,128)(2,1)S(1)} %pick.2), channel_id=1, source_target_pairs={{0,1},{1,0},{2,3},{3,2},{4,5},{5,4},{6,7},{7,6},{8,9},{9,8},{10,11... | collective-permute-start | bytes 1572872 | tf_op jit(solution)/shard_map/ppermute | solution.py:224
  58.7 48.5 %collective-permute-start.1 = (bf16[2,128,1024]{2,1,0:T(8,128)(2,1)S(1)}, bf16[2,128,1024]{2,1,0:T(8,128)(2,1)S(1)}, u32[]{:S(2)}, u32[]{:S(2)}) collective-permute-start(bf16[2,128,1024]{2,1,0:T(8,128)(2,1)S(1)} %get-tuple-element.11), channel_id=1, source_target_pairs={{0,8},{8,0},{1,9},{9,1},{2,10},{10,2},{3,11},{11,3},{4,12},{12,4},... | collective-permute-start | bytes 1572872 | tf_op jit(solution)/shard_map/ppermute | solution.py:227
  102.3 9.5 %all-to-all-start.2 = ((bf16[4,256,128]{2,1,0:T(8,128)(2,1)}), bf16[4,256,128]{2,1,0:T(8,128)(2,1)S(1)}, u32[]{:S(2)}, u32[]{:S(2)}) async-start(bf16[4,256,128]{2,1,0:T(8,128)(2,1)} %attention.1), calls=%async_computation.2 | async-start | bytes 524288 | tf_op jit(solution)/shard_map/all_to_all | solution.py:291

commit v8 on v7

--- a/solution.py
+++ b/solution.py
@@ -41,41 +41,54 @@
     value_ref,
     semaphores,
     normed_ref,
-    scale_ref,
+    mean_ref,
+    square_ref,
 ):
-    key_copy = pltpu.make_async_copy(key_hbm_ref, key_ref, semaphores.at[0])
-    value_copy = pltpu.make_async_copy(value_hbm_ref, value_ref, semaphores.at[1])
-    key_copy.start()
-    value_copy.start()
     cols, tokens, depth = whole_ref.shape
-    rows = key_ref.shape[0] // cols
+    rows = key_ref.shape[0]
     count = cols * depth
-    places = [(c, pl.ds(k, LANES)) for c in range(cols) for k in range(0, depth, LANES)]
-
-    def normalize(step, carry):
+    copies = [
+        [
+            pltpu.make_async_copy(source.at[:, c], target.at[:, c], semaphores.at[k, c])
+            for k, (source, target) in enumerate(((key_hbm_ref, key_ref), (value_hbm_ref, value_ref)))
+        ]
+        for c in range(cols)
+    ]
+    for pair in copies:
+        for copy in pair:
+            copy.start()
+
+    def average(step, carry):
         here = pl.ds(pl.multiple_of(step * CHUNK, CHUNK), CHUNK)
         sums = jnp.zeros((CHUNK, LANES), jnp.float32)
-        for c, k in places:
-            sums += whole_ref[c, here, k].astype(jnp.float32)
-        mean = jnp.sum(sums, axis=1, keepdims=True) / count
-        squares = jnp.zeros((CHUNK, LANES), jnp.float32)
-        for c, k in places:
-            centred = whole_ref[c, here, k].astype(jnp.float32) - mean
-            squares += centred * centred
-            normed_ref[c, here, k] = (centred * gain_ref[c : c + 1, k]).astype(jnp.bfloat16)
-        spread = jnp.sum(squares, axis=1, keepdims=True) / count
-        scale_ref[here, :] = jnp.broadcast_to(lax.rsqrt(spread + epsilon * SCALE * SCALE), (CHUNK, LANES))
+        for c in range(cols):
+            for k in range(0, depth, LANES):
+                sums += whole_ref[c, here, pl.ds(k, LANES)].astype(jnp.float32)
+        mean_ref[here, :] = jnp.broadcast_to(jnp.sum(sums, axis=1, keepdims=True) / count, (CHUNK, LANES))
         return carry
 
-    lax.fori_loop(0, tokens // CHUNK, normalize, 0)
-    key_copy.wait()
-    value_copy.wait()
+    lax.fori_loop(0, tokens // CHUNK, average, 0)
     projected = jnp.zeros((tokens, 2 * HEAD_DIM), jnp.float32)
     for c in range(cols):
-        both = [jnp.concatenate([ref[r * cols + c] for r in range(rows)], axis=0) for ref in (key_ref, value_ref)]
+        for t in range(0, tokens, CHUNK):
+            here = pl.ds(t, CHUNK)
+            mean = mean_ref[here, :]
+            squares = square_ref[here, :] if c else jnp.zeros((CHUNK, LANES), jnp.float32)
+            for k in range(0, depth, LANES):
+                centred = whole_ref[c, here, pl.ds(k, LANES)].astype(jnp.float32) - mean
+                squares += centred * centred
+                normed_ref[c, here, pl.ds(k, LANES)] = (centred * gain_ref[c : c + 1, pl.ds(k, LANES)]).astype(
+                    jnp.bfloat16
+                )
+            square_ref[here, :] = squares
+        for copy in copies[c]:
+            copy.wait()
+        both = [jnp.concatenate([ref[r, c] for r in range(rows)], axis=0) for ref in (key_ref, value_ref)]
         projected += jnp.dot(normed_ref[c], jnp.concatenate(both, axis=1), preferred_element_type=jnp.float32)
-    keys = (projected[:, :HEAD_DIM] * scale_ref[...]).astype(jnp.bfloat16)
-    values = (projected[:, HEAD_DIM:] * scale_ref[...]).astype(jnp.bfloat16)
+    spread = jnp.sum(square_ref[...], axis=1, keepdims=True) / count
+    scale = lax.rsqrt(spread + epsilon * SCALE * SCALE)
+    keys = (projected[:, :HEAD_DIM] * scale).astype(jnp.bfloat16)
+    values = (projected[:, HEAD_DIM:] * scale).astype(jnp.bfloat16)
     scores = lax.dot_general(queries_ref[...], keys, (((1,), (1,)), ((), ())), preferred_element_type=jnp.float32)
     scores *= HEAD_DIM**-0.5
     weights = jnp.exp(scores - jnp.max(scores, axis=1, keepdims=True))
@@ -161,10 +174,6 @@
     )(jnp.stack(origins).astype(jnp.int32), in_hbm(sources[0]), *sources[1:])
 
 
-def deal_kernel(visual_ref, dealt_ref):
-    dealt_ref[...] = jnp.swapaxes(visual_ref[...].astype(jnp.float32), 0, 1).astype(jnp.bfloat16)
-
-
 def spread_kernel(relayed_ref, blocks_ref):
     images, tokens, features = relayed_ref.shape
     block = relayed_ref[...].astype(jnp.float32).reshape(images * tokens, features).T.astype(jnp.bfloat16)
@@ -207,14 +216,7 @@
     tokens_here = text_tokens // devices
     width = DEC // quad
     member = lax.axis_index(QUAD)
-    relayed = pl.pallas_call(
-        deal_kernel,
-        out_shape=jax.ShapeDtypeStruct((images, tokens, features), jnp.bfloat16),
-        in_specs=[pl.BlockSpec(memory_space=pltpu.VMEM)],
-        out_specs=pl.BlockSpec(memory_space=pltpu.VMEM),
-        compiler_params=pltpu.CompilerParams(vmem_limit_bytes=4 << 20),
-        name="deal",
-    )(visual)
+    relayed = visual.transpose(1, 0, 2)
     relayed = lax.all_to_all(relayed, "dp", 0, 0, tiled=True)
     row, col = (lax.axis_index(a) for a in QUAD)
     swap = [(0, 1), (1, 0)]
@@ -273,7 +275,7 @@
     whole = lax.all_gather(column, COL, axis=0, tiled=True)
     whole = whole.astype(jnp.bfloat16).reshape(cols, vis_tokens, rows * features)
     operands = [in_vmem(v) for v in (whole, gain, queries)]
-    operands += [in_hbm(w.reshape(devices, features, HEAD_DIM)) for w in (key_weight, value_weight)]
+    operands += [in_hbm(w.reshape(rows, cols, features, HEAD_DIM)) for w in (key_weight, value_weight)]
     contexts = pl.pallas_call(
         attention_kernel,
         out_shape=jax.ShapeDtypeStruct((quad, text_tokens, HEAD_DIM), jnp.bfloat16),
@@ -281,9 +283,9 @@
         out_specs=pl.BlockSpec(memory_space=pltpu.VMEM),
         scratch_shapes=[
             *(pltpu.VMEM(w.shape, jnp.bfloat16) for w in operands[3:]),
-            pltpu.SemaphoreType.DMA((2,)),
+            pltpu.SemaphoreType.DMA((2, cols)),
             pltpu.VMEM(whole.shape, jnp.bfloat16),
-            pltpu.VMEM((whole.shape[1], LANES), jnp.float32),
+            *[pltpu.VMEM((vis_tokens, LANES), jnp.float32)] * 2,
         ],
         compiler_params=pltpu.CompilerParams(vmem_limit_bytes=12 << 20),
         name="attention",

time: 135 us -> 136 us (level)
  no operation moved by 1% of the time
where the time goes in v8:
time: 136 us; the launch traced here: 135 us
  blocking collectives  91.5 us (67%)
  starting transfers between devices  14.8 us (11%)
  waiting for transfers between devices  13.4 us (10%)
  Pallas kernels  13.3 us (10%)
    all_to_all x1, blocking collectives, attend(): relayed = lax.all_to_all(relayed, 'dp', 0, 0, tiled=True)  35.6 us
    all_gather x1, blocking collectives, attend(): whole = lax.all_gather(column, COL, axis=0, tiled=True)  34.6 us
    all_to_all x1, blocking collectives, attend(): lax.all_to_all(part.reshape(devices, tokens_here, width), MP, 0, 0, tiled...  21.3 us
    ppermute x1, waiting for transfers between devices, attend(): beyond = lax.ppermute(send, QUAD[1], swap)[0]  8.78 us
    all_to_all x1, starting transfers between devices, attend(): group = lax.all_to_all(contexts, QUAD, 0, 0, tiled=True)  4.86 us
    pallas_call x1, Pallas kernels, attend(): pl.pallas_call(attention_kernel, out_shape=jax.ShapeDtypeStruct((quad, te...  4.73 us
    all_to_all x1, waiting for transfers between devices, attend(): group = lax.all_to_all(contexts, QUAD, 0, 0, tiled=True)  4.62 us
    ppermute x1, starting transfers between devices, attend(): out_rows = [keep, lax.ppermute(send, QUAD[0], swap)]  4.04 us
  transfers between devices with their start and end apart: 4, of which 2 were waited for; matrix products, arithmetic and copies ran while one was open for 1% of the time, Pallas kernels for 8%

profile of v8, /device:TPU:2, one launch (start us, length us, event | category | flops | bytes accessed | tf_op | source)
XLA Modules:
  0.0 135.0 jit_solution(2184894531029110388)
XLA Ops:
  0.0 0.0 copy-start.1
  0.0 0.0 copy-start
  0.0 1.0 copy.13
  1.0 35.6 %all_to_all.20.relayed_ref = bf16[32,8,192]{2,1,0:T(8,128)(2,1)S(1)} all-to-all(bf16[32,8,192]{2,1,0:T(8,128)(2,1)S(1)} %bitcast.30), channel_id=1, replica_groups=mesh['dp'=32,'row_0'=2,'row_1'=2,'col_0'=4,'col_1'=2] {'dp'}, dimensions={0} | all-to-all | bytes 196608 | tf_op jit(solution)/shard_map/all_to_all | solution.py:220
  36.6 0.8 spread.1
  37.5 3.5 %all-to-all-start.1 = ((bf16[4,192,256]{2,1,0:T(8,128)(2,1)}), bf16[4,192,256]{2,1,0:T(8,128)(2,1)S(1)}, u32[]{:S(2)}, u32[]{:S(2)}) async-start(bf16[4,192,256]{2,1,0:T(8,128)(2,1)} %spread.1), calls=%async_computation.1 | async-start | bytes 786432 | tf_op jit(solution)/shard_map/all_to_all | solution.py:239
  41.0 1.1 pick.2
  42.0 2.4 %collective-permute-start = (bf16[1,128,2048]{2,1,0:T(8,128)(2,1)S(1)}, bf16[1,128,2048]{2,1,0:T(8,128)(2,1)S(1)}, u32[]{:S(2)}, u32[]{:S(2)}) collective-permute-start(bf16[1,128,2048]{2,1,0:T(8,128)(2,1)S(1)} %pick.2), channel_id=1, source_target_pairs={{0,1},{1,0},{2,3},{3,2},{4,5},{5,4},{6,7},{7,6},{8,9},{9,8},{10,11... | collective-permute-start | bytes 1572872 | tf_op jit(solution)/shard_map/ppermute | solution.py:226
  44.5 0.0 copy-done.1
  44.5 0.1 reshape.42
  44.6 0.1 reshape.43.gain_ref
  44.7 0.0 copy-done
  44.7 3.5 %query.1 = (bf16[256,128]{1,0:T(8,128)(2,1)S(1)}, f32[8,4096]{1,0:T(8,128)S(1)}) custom-call(s32[1]{0:T(128)} %bitcast.5.origin_ref, bf16[256,4096]{1,0:T(8,128)(2,1)} %bitcast.27, bf16[4096,128]{1,0:T(8,128)(2,1)} %weight_hbm_ref.1, f32[1,4096]{1,0:T(1,128)S(1)} %bitcast.26), custom_call_target="tpu_custom_call" | custom-call | tf_op jit(solution)/shard_map/query/pallas_call | solution.py:241
  48.2 0.1 pad_add_fusion.origins_ref
  48.3 8.8 %collective-permute-done = bf16[1,128,2048]{2,1,0:T(8,128)(2,1)S(1)} collective-permute-done((bf16[1,128,2048]{2,1,0:T(8,128)(2,1)S(1)}, bf16[1,128,2048]{2,1,0:T(8,128)(2,1)S(1)}, u32[]{:S(2)}, u32[]{:S(2)}) %collective-permute-start) | collective-permute-done | bytes 524320 | tf_op jit(solution)/shard_map/ppermute | solution.py:226
  57.1 1.6 %pick.3 = (bf16[2,128,1024]{2,1,0:T(8,128)(2,1)S(1)}, bf16[2,128,1024]{2,1,0:T(8,128)(2,1)S(1)}) custom-call(s32[4]{0:T(128)S(1)} %pad_add_fusion.origins_ref, bf16[128,4096]{1,0:T(8,128)(2,1)} %refs_0_.3, bf16[128,2048]{1,0:T(8,128)(2,1)S(1)} %bitcast.25), custom_call_target="tpu_custom_call" | custom-call | tf_op jit(solution)/shard_map/pick/pallas_call | solution.py:166
  58.7 4.0 %collective-permute-start.1 = (bf16[2,128,1024]{2,1,0:T(8,128)(2,1)S(1)}, bf16[2,128,1024]{2,1,0:T(8,128)(2,1)S(1)}, u32[]{:S(2)}, u32[]{:S(2)}) collective-permute-start(bf16[2,128,1024]{2,1,0:T(8,128)(2,1)S(1)} %get-tuple-element.11), channel_id=1, source_target_pairs={{0,8},{8,0},{1,9},{9,1},{2,10},{10,2},{3,11},{11,3},{4,12},{12,4},... | collective-permute-start | bytes 1572872 | tf_op jit(solution)/shard_map/ppermute | solution.py:229
  62.7 0.0 all-to-all-done.1
  62.8 0.2 turn.1
  62.9 0.1 multiply_convert_fusion
  63.0 34.6 %all-gather.1 = f16[2048,768]{1,0:T(8,128)(2,1)S(1)} all-gather(f16[256,768]{1,0:T(8,128)(2,1)S(1)} %multiply_convert_fusion), channel_id=1, replica_groups=mesh['dp'=32,'row_0'=2,'row_1'=2,'col_0'=4,'col_1'=2] {'col_0','col_1'}, dimensions={0}, use_global_device_ids=true | all-gather | bytes 3538944 | tf_op jit(solution)/shard_map/all_gather | solution.py:275
  97.6 0.5 convert_element_type.11
  98.1 4.7 %attention.1 = bf16[4,256,128]{2,1,0:T(8,128)(2,1)} custom-call(bf16[8,256,768]{2,1,0:T(8,128)(2,1)S(1)} %bitcast.21, f32[8,768]{1,0:T(8,128)S(1)} %reshape.43.gain_ref, bf16[256,128]{1,0:T(8,128)(2,1)S(1)} %get-tuple-element.9.queries_ref, bf16[4,8,192,128]{3,2,1,0:T(8,128)(2,1)} %bitcast.28, bf16[4,8,192,128]{3,2,1,0:T(8,128)(2,1)} %bitcast.29), custom_call_target="tpu_custom_call" | custom-call | tf_op jit(solution)/shard_map/attention/pallas_call | solution.py:279
  102.8 4.9 %all-to-all-start.2 = ((bf16[4,256,128]{2,1,0:T(8,128)(2,1)}), bf16[4,256,128]{2,1,0:T(8,128)(2,1)S(1)}, u32[]{:S(2)}, u32[]{:S(2)}) async-start(bf16[4,256,128]{2,1,0:T(8,128)(2,1)} %attention.1), calls=%async_computation.2 | async-start | bytes 524288 | tf_op jit(solution)/shard_map/all_to_all | solution.py:293
  107.7 0.0 collective-permute-done.1.refs_1_
  107.7 4.6 %all-to-all-done.2.group_ref = bf16[4,256,128]{2,1,0:T(8,128)(2,1)S(1)} async-done(((bf16[4,256,128]{2,1,0:T(8,128)(2,1)}), bf16[4,256,128]{2,1,0:T(8,128)(2,1)S(1)}, u32[]{:S(2)}, u32[]{:S(2)}) %all-to-all-start.2) | async-done | bytes 262176 | tf_op jit(solution)/shard_map/all_to_all | solution.py:293
  112.3 0.7 project.1
  113.0 21.3 %all_to_all.21 = bf16[32,8,1024]{2,1,0:T(8,128)(2,1)S(1)} all-to-all(bf16[32,8,1024]{2,1,0:T(8,128)(2,1)S(1)} %bitcast.23), channel_id=1, replica_groups=mesh['dp'=32,'row_0'=2,'row_1'=2,'col_0'=4,'col_1'=2] {'row_0','row_1','..., dimensions={0} | all-to-all | bytes 1048576 | tf_op jit(solution)/shard_map/all_to_all | solution.py:303
  134.3 0.7 finish.1
  (1 shorter events, 0.0 us)
Async XLA Ops:
  0.0 44.5 %copy-start.1 = (f32[6144]{0:T(1024)S(1)}, f32[6144]{0:T(1024)}, u32[]{:S(2)}) copy-start(f32[6144]{0:T(1024)} %param.9) | copy-start | bytes 73732
  0.0 44.7 %copy-start = (f32[4096]{0:T(1024)S(1)}, f32[4096]{0:T(1024)}, u32[]{:S(2)}) copy-start(f32[4096]{0:T(1024)} %param.11) | copy-start | bytes 49156
  37.5 25.3 %all-to-all-start.1 = ((bf16[4,192,256]{2,1,0:T(8,128)(2,1)}), bf16[4,192,256]{2,1,0:T(8,128)(2,1)S(1)}, u32[]{:S(2)}, u32[]{:S(2)}) async-start(bf16[4,192,256]{2,1,0:T(8,128)(2,1)} %spread.1), calls=%async_computation.1 | async-start | bytes 786432 | tf_op jit(solution)/shard_map/all_to_all | solution.py:239
  42.0 15.0 %collective-permute-start = (bf16[1,128,2048]{2,1,0:T(8,128)(2,1)S(1)}, bf16[1,128,2048]{2,1,0:T(8,128)(2,1)S(1)}, u32[]{:S(2)}, u32[]{:S(2)}) collective-permute-start(bf16[1,128,2048]{2,1,0:T(8,128)(2,1)S(1)} %pick.2), channel_id=1, source_target_pairs={{0,1},{1,0},{2,3},{3,2},{4,5},{5,4},{6,7},{7,6},{8,9},{9,8},{10,11... | collective-permute-start | bytes 1572872 | tf_op jit(solution)/shard_map/ppermute | solution.py:226
  58.7 49.0 %collective-permute-start.1 = (bf16[2,128,1024]{2,1,0:T(8,128)(2,1)S(1)}, bf16[2,128,1024]{2,1,0:T(8,128)(2,1)S(1)}, u32[]{:S(2)}, u32[]{:S(2)}) collective-permute-start(bf16[2,128,1024]{2,1,0:T(8,128)(2,1)S(1)} %get-tuple-element.11), channel_id=1, source_target_pairs={{0,8},{8,0},{1,9},{9,1},{2,10},{10,2},{3,11},{11,3},{4,12},{12,4},... | collective-permute-start | bytes 1572872 | tf_op jit(solution)/shard_map/ppermute | solution.py:229
  102.8 9.5 %all-to-all-start.2 = ((bf16[4,256,128]{2,1,0:T(8,128)(2,1)}), bf16[4,256,128]{2,1,0:T(8,128)(2,1)S(1)}, u32[]{:S(2)}, u32[]{:S(2)}) async-start(bf16[4,256,128]{2,1,0:T(8,128)(2,1)} %attention.1), calls=%async_computation.2 | async-start | bytes 524288 | tf_op jit(solution)/shard_map/all_to_all | solution.py:293

commit v9 on v6

--- a/solution.py
+++ b/solution.py
@@ -15,7 +15,7 @@
 MP = ROW + COL
 QUAD = ("row_1", "col_1")
 LANES = 128
-CHUNK = 64
+CHUNK = 128
 TEXT_CHUNKS = 2
 TEXT_BLOCK = 32
 SCALE = 8192.0
@@ -298,6 +298,7 @@
         compiler_params=pltpu.CompilerParams(vmem_limit_bytes=12 << 20),
         name="attention",
     )(*operands)
+    contexts, member, *out_rows = lax.optimization_barrier((contexts, member.reshape(1), *out_rows))
     group = lax.all_to_all(contexts, QUAD, 0, 0, tiled=True)
     operands = [in_vmem(v) for v in (group, *out_rows)]
     part = pl.pallas_call(
@@ -307,7 +308,7 @@
         out_specs=pl.BlockSpec(memory_space=pltpu.VMEM),
         compiler_params=pltpu.CompilerParams(vmem_limit_bytes=12 << 20),
         name="project",
-    )(member.reshape(1), *operands)
+    )(member, *operands)
     parts = lax.all_to_all(part.reshape(devices, tokens_here, width), MP, 0, 0, tiled=True)
     parts = parts.reshape(*(lax.axis_size(a) for a in MP), tokens_here, width)
     mixed = pl.pallas_call(

time: 130 us -> 128 us (0.985)
  blocking collectives: 82.8 us -> 90.4 us
  waiting for transfers between devices: 14.4 us -> 9.83 us
  starting transfers between devices: 17.6 us -> 13.6 us
    all_to_all x0 -> x1, blocking collectives: none -> 7.71 us  [attend(): group = lax.all_to_all(contexts, QUAD, 0, 0, tiled=True)]
    all_to_all x1 -> x0, waiting for transfers between devices: 4.62 us -> none  [attend(): group = lax.all_to_all(contexts, QUAD, 0, 0, tiled=True)]
    all_to_all x1 -> x0, starting transfers between devices: 3.91 us -> none  [attend(): group = lax.all_to_all(contexts, QUAD, 0, 0, tiled=True)]
  transfers between devices with their start and end apart: 4 -> 3, of which waited for: 2 -> 1; matrix products, arithmetic and copies ran while one was open for 1% -> 1% of each run, Pallas kernels for 8% -> 8%
where the time goes in v9:
time: 128 us
  blocking collectives  90.4 us (71%)
  starting transfers between devices  13.6 us (11%)
  Pallas kernels  12.1 us (9%)
  waiting for transfers between devices  9.83 us (8%)
    all_gather x1, blocking collectives, attend(): whole = lax.all_gather(column, COL, axis=0, tiled=True)  35.2 us
    all_to_all x1, blocking collectives, attend(): relayed = lax.all_to_all(relayed, 'dp_1', 0, 0, tiled=True)  25.2 us
    all_to_all x1, blocking collectives, attend(): lax.all_to_all(part.reshape(devices, tokens_here, width), MP, 0, 0, tiled...  22.2 us
    ppermute x1, waiting for transfers between devices, attend(): beyond = lax.ppermute(send, QUAD[1], swap)[0]  9.82 us
    all_to_all x1, blocking collectives, attend(): group = lax.all_to_all(contexts, QUAD, 0, 0, tiled=True)  7.71 us
    all_to_all x1, starting transfers between devices, attend(): column = lax.all_to_all(blocks, ('dp_0',) + ROW, 0, 0, tiled=True)  7.56 us
    ppermute x1, starting transfers between devices, attend(): out_rows = [keep, lax.ppermute(send, QUAD[0], swap)]  3.65 us
    pallas_call x1, Pallas kernels, attend(): pl.pallas_call(query_kernel, out_shape=(jax.ShapeDtypeStruct((text_tokens...  3.53 us
  transfers between devices with their start and end apart: 3, of which 1 were waited for; matrix products, arithmetic and copies ran while one was open for 1% of the time, Pallas kernels for 8%

profile of v9, /device:TPU:2, one launch (start us, length us, event | category | flops | bytes accessed | tf_op | source)
XLA Modules:
  0.0 127.8 jit_solution(8455408639565875307)
XLA Ops:
  0.0 0.0 copy-start
  0.0 0.9 copy-done
  0.9 0.0 copy-start.2
  0.9 0.0 copy-start.1
  0.9 0.1 deal.1
  1.0 25.2 %all_to_all.20.relayed_ref = bf16[16,2,8,192]{3,2,1,0:T(8,128)(2,1)S(1)} all-to-all(bf16[16,2,8,192]{3,2,1,0:T(8,128)(2,1)S(1)} %deal.1), channel_id=1, replica_groups=mesh['dp_0'=2,'dp_1'=16,'row_0'=2,'row_1'=2,'col_0'=4,'col_1'=2] {'dp_1'}, dimensions={0} | all-to-all | bytes 196608 | tf_op jit(solution)/shard_map/all_to_all | solution.py:228
  26.2 0.9 spread.1
  27.1 7.6 %all-to-all-start.1 = ((bf16[8,192,128]{2,1,0:T(8,128)(2,1)}), bf16[8,192,128]{2,1,0:T(8,128)(2,1)S(1)}, u32[]{:S(2)}, u32[]{:S(2)}) async-start(bf16[8,192,128]{2,1,0:T(8,128)(2,1)} %spread.1), calls=%async_computation.1 | async-start | bytes 786432 | tf_op jit(solution)/shard_map/all_to_all | solution.py:247
  34.6 1.0 pick.2
  35.7 2.4 %collective-permute-start = (bf16[1,128,2048]{2,1,0:T(8,128)(2,1)S(1)}, bf16[1,128,2048]{2,1,0:T(8,128)(2,1)S(1)}, u32[]{:S(2)}, u32[]{:S(2)}) collective-permute-start(bf16[1,128,2048]{2,1,0:T(8,128)(2,1)S(1)} %pick.2), channel_id=1, source_target_pairs={{0,1},{1,0},{2,3},{3,2},{4,5},{5,4},{6,7},{7,6},{8,9},{9,8},{10,11... | collective-permute-start | bytes 1572872 | tf_op jit(solution)/shard_map/ppermute | solution.py:234
  38.1 0.0 copy-done.2
  38.1 0.1 reshape.41
  38.2 0.1 reshape.42.gain_ref
  38.3 0.0 copy-done.1
  38.3 3.5 %query.1 = (bf16[256,128]{1,0:T(8,128)(2,1)S(1)}, f32[8,4096]{1,0:T(8,128)S(1)}) custom-call(s32[1]{0:T(128)} %bitcast.3.origin_ref, bf16[256,4096]{1,0:T(8,128)(2,1)} %bitcast.24, bf16[4096,128]{1,0:T(8,128)(2,1)} %weight_hbm_ref.1, f32[1,4096]{1,0:T(1,128)S(1)} %bitcast.23), custom_call_target="tpu_custom_call" | custom-call | tf_op jit(solution)/shard_map/query/pallas_call | solution.py:249
  41.9 0.1 pad_add_fusion.origins_ref
  41.9 9.8 %collective-permute-done = bf16[1,128,2048]{2,1,0:T(8,128)(2,1)S(1)} collective-permute-done((bf16[1,128,2048]{2,1,0:T(8,128)(2,1)S(1)}, bf16[1,128,2048]{2,1,0:T(8,128)(2,1)S(1)}, u32[]{:S(2)}, u32[]{:S(2)}) %collective-permute-start) | collective-permute-done | bytes 524320 | tf_op jit(solution)/shard_map/ppermute | solution.py:234
  51.8 1.6 %pick.3 = (bf16[2,128,1024]{2,1,0:T(8,128)(2,1)S(1)}, bf16[2,128,1024]{2,1,0:T(8,128)(2,1)S(1)}) custom-call(s32[4]{0:T(128)S(1)} %pad_add_fusion.origins_ref, bf16[128,4096]{1,0:T(8,128)(2,1)} %refs_0_.3, bf16[128,2048]{1,0:T(8,128)(2,1)S(1)} %bitcast.22), custom_call_target="tpu_custom_call" | custom-call | tf_op jit(solution)/shard_map/pick/pallas_call | solution.py:154
  53.4 3.6 %collective-permute-start.1 = (bf16[2,128,1024]{2,1,0:T(8,128)(2,1)S(1)}, bf16[2,128,1024]{2,1,0:T(8,128)(2,1)S(1)}, u32[]{:S(2)}, u32[]{:S(2)}) collective-permute-start(bf16[2,128,1024]{2,1,0:T(8,128)(2,1)S(1)} %get-tuple-element.15), channel_id=1, source_target_pairs={{0,8},{8,0},{1,9},{9,1},{2,10},{10,2},{3,11},{11,3},{4,12},{12,4},... | collective-permute-start | bytes 1572872 | tf_op jit(solution)/shard_map/ppermute | solution.py:237
  57.0 0.0 all-to-all-done.1
  57.1 0.2 turn.1
  57.2 0.1 multiply_convert_fusion
  57.3 35.2 %all-gather.1 = f16[2048,768]{1,0:T(8,128)(2,1)S(1)} all-gather(f16[256,768]{1,0:T(8,128)(2,1)S(1)} %multiply_convert_fusion), channel_id=1, replica_groups=mesh['dp_0'=2,'dp_1'=16,'row_0'=2,'row_1'=2,'col_0'=4,'col_1'=2] {'col_0..., dimensions={0}, use_global_device_ids=true | all-gather | bytes 3538944 | tf_op jit(solution)/shard_map/all_gather | solution.py:283
  92.5 0.5 convert_element_type.11
  93.0 3.5 %attention.1 = bf16[4,256,128]{2,1,0:T(8,128)(2,1)S(1)} custom-call(bf16[8,256,768]{2,1,0:T(8,128)(2,1)S(1)} %bitcast.18, f32[8,768]{1,0:T(8,128)S(1)} %reshape.42.gain_ref, bf16[256,128]{1,0:T(8,128)(2,1)S(1)} %get-tuple-element.13.queries_ref, bf16[32,192,128]{2,1,0:T(8,128)(2,1)} %bitcast.25, bf16[32,192,128]{2,1,0:T(8,128)(2,1)} %bitcast.26), custom_call_target="tpu_custom_call" | custom-call | tf_op jit(solution)/shard_map/attention/pallas_call | solution.py:287
  96.5 0.0 collective-permute-done.1.refs_1_
  96.5 7.7 %all_to_all.21.group_ref = bf16[4,256,128]{2,1,0:T(8,128)(2,1)S(1)} all-to-all(bf16[4,256,128]{2,1,0:T(8,128)(2,1)S(1)} %attention.1), channel_id=1, replica_groups=mesh['dp_0'=2,'dp_1'=16,'row_0'=2,'row_1'=2,'col_0'=4,'col_1'=2] {'row_1..., dimensions={0} | all-to-all | bytes 524288 | tf_op jit(solution)/shard_map/all_to_all | solution.py:302
  104.2 0.7 project.1
  104.9 22.2 %all_to_all.22 = bf16[32,8,1024]{2,1,0:T(8,128)(2,1)S(1)} all-to-all(bf16[32,8,1024]{2,1,0:T(8,128)(2,1)S(1)} %bitcast.20), channel_id=1, replica_groups=mesh['dp_0'=2,'dp_1'=16,'row_0'=2,'row_1'=2,'col_0'=4,'col_1'=2] {'row_0..., dimensions={0} | all-to-all | bytes 1048576 | tf_op jit(solution)/shard_map/all_to_all | solution.py:312
  127.1 0.7 finish.1
  (1 shorter events, 0.0 us)
Async XLA Ops:
  0.0 0.9 copy-start
  0.9 37.2 %copy-start.2 = (f32[6144]{0:T(1024)S(1)}, f32[6144]{0:T(1024)}, u32[]{:S(2)}) copy-start(f32[6144]{0:T(1024)} %param.9) | copy-start | bytes 73732
  0.9 37.4 %copy-start.1 = (f32[4096]{0:T(1024)S(1)}, f32[4096]{0:T(1024)}, u32[]{:S(2)}) copy-start(f32[4096]{0:T(1024)} %param.11) | copy-start | bytes 49156
  27.1 30.0 %all-to-all-start.1 = ((bf16[8,192,128]{2,1,0:T(8,128)(2,1)}), bf16[8,192,128]{2,1,0:T(8,128)(2,1)S(1)}, u32[]{:S(2)}, u32[]{:S(2)}) async-start(bf16[8,192,128]{2,1,0:T(8,128)(2,1)} %spread.1), calls=%async_computation.1 | async-start | bytes 786432 | tf_op jit(solution)/shard_map/all_to_all | solution.py:247
  35.7 16.1 %collective-permute-start = (bf16[1,128,2048]{2,1,0:T(8,128)(2,1)S(1)}, bf16[1,128,2048]{2,1,0:T(8,128)(2,1)S(1)}, u32[]{:S(2)}, u32[]{:S(2)}) collective-permute-start(bf16[1,128,2048]{2,1,0:T(8,128)(2,1)S(1)} %pick.2), channel_id=1, source_target_pairs={{0,1},{1,0},{2,3},{3,2},{4,5},{5,4},{6,7},{7,6},{8,9},{9,8},{10,11... | collective-permute-start | bytes 1572872 | tf_op jit(solution)/shard_map/ppermute | solution.py:234
  53.4 43.1 %collective-permute-start.1 = (bf16[2,128,1024]{2,1,0:T(8,128)(2,1)S(1)}, bf16[2,128,1024]{2,1,0:T(8,128)(2,1)S(1)}, u32[]{:S(2)}, u32[]{:S(2)}) collective-permute-start(bf16[2,128,1024]{2,1,0:T(8,128)(2,1)S(1)} %get-tuple-element.15), channel_id=1, source_target_pairs={{0,8},{8,0},{1,9},{9,1},{2,10},{10,2},{3,11},{11,3},{4,12},{12,4},... | collective-permute-start | bytes 1572872 | tf_op jit(solution)/shard_map/ppermute | solution.py:237

commit v10 on v9

--- a/solution.py
+++ b/solution.py
@@ -162,12 +162,21 @@
     )(jnp.stack(origins).astype(jnp.int32), in_hbm(sources[0]), *sources[1:])
 
 
-def deal_kernel(visual_ref, dealt_ref):
-    planes, halves = dealt_ref.shape[:2]
-    dealt = jnp.swapaxes(visual_ref[...].astype(jnp.float32), 0, 1).astype(jnp.bfloat16)
+def deal_kernel(visual_hbm_ref, dealt_hbm_ref, visual_ref, dealt_ref, semaphores):
+    planes, halves = dealt_hbm_ref.shape[:2]
+    loads, stores = [], []
     for h in range(halves):
-        for p in range(planes):
-            dealt_ref[p, h] = dealt[h * planes + p]
+        here = pl.ds(h * planes, planes)
+        loads.append(pltpu.make_async_copy(visual_hbm_ref.at[:, here], visual_ref.at[:, here], semaphores.at[0, h]))
+        stores.append(pltpu.make_async_copy(dealt_ref.at[h], dealt_hbm_ref.at[:, h], semaphores.at[1, h]))
+        loads[h].start()
+    for h in range(halves):
+        loads[h].wait()
+        half = visual_ref[:, pl.ds(h * planes, planes)].astype(jnp.float32)
+        dealt_ref[h] = jnp.swapaxes(half, 0, 1).astype(jnp.bfloat16)
+        stores[h].start()
+    for store in stores:
+        store.wait()
 
 
 def spread_kernel(relayed_ref, blocks_ref):
@@ -220,11 +229,16 @@
     relayed = pl.pallas_call(
         deal_kernel,
         out_shape=jax.ShapeDtypeStruct((planes, halves, tokens, features), jnp.bfloat16),
-        in_specs=[pl.BlockSpec(memory_space=pltpu.VMEM)],
-        out_specs=pl.BlockSpec(memory_space=pltpu.VMEM),
+        in_specs=[pl.BlockSpec(memory_space=pl.ANY)],
+        out_specs=pl.BlockSpec(memory_space=pl.ANY),
+        scratch_shapes=[
+            pltpu.VMEM(visual.shape, jnp.bfloat16),
+            pltpu.VMEM((halves, planes, tokens, features), jnp.bfloat16),
+            pltpu.SemaphoreType.DMA((2, halves)),
+        ],
         compiler_params=pltpu.CompilerParams(vmem_limit_bytes=4 << 20),
         name="deal",
-    )(visual)
+    )(in_hbm(visual))
     relayed = lax.all_to_all(relayed, "dp_1", 0, 0, tiled=True)
     row, col = (lax.axis_index(a) for a in QUAD)
     swap = [(0, 1), (1, 0)]

time: 128 us -> 128 us (level)
  no operation moved by 1% of the time
where the time goes in v10:
time: 128 us
  blocking collectives  90.4 us (71%)
  starting transfers between devices  13.6 us (11%)
  Pallas kernels  13 us (10%)
  waiting for transfers between devices  9.83 us (8%)
    all_gather x1, blocking collectives, attend(): whole = lax.all_gather(column, COL, axis=0, tiled=True)  35.2 us
    all_to_all x1, blocking collectives, attend(): relayed = lax.all_to_all(relayed, 'dp_1', 0, 0, tiled=True)  25.2 us
    all_to_all x1, blocking collectives, attend(): lax.all_to_all(part.reshape(devices, tokens_here, width), MP, 0, 0, tiled...  22.2 us
    ppermute x1, waiting for transfers between devices, attend(): beyond = lax.ppermute(send, QUAD[1], swap)[0]  9.82 us
    all_to_all x1, blocking collectives, attend(): group = lax.all_to_all(contexts, QUAD, 0, 0, tiled=True)  7.71 us
    all_to_all x1, starting transfers between devices, attend(): column = lax.all_to_all(blocks, ('dp_0',) + ROW, 0, 0, tiled=True)  7.56 us
    ppermute x1, starting transfers between devices, attend(): out_rows = [keep, lax.ppermute(send, QUAD[0], swap)]  3.65 us
    pallas_call x1, Pallas kernels, attend(): pl.pallas_call(query_kernel, out_shape=(jax.ShapeDtypeStruct((text_tokens...  3.53 us
  transfers between devices with their start and end apart: 3, of which 1 were waited for; matrix products, arithmetic and copies ran while one was open for 1% of the time, Pallas kernels for 8%

profile of v10, /device:TPU:2, one launch (start us, length us, event | category | flops | bytes accessed | tf_op | source)
XLA Modules:
  0.0 127.8 jit_solution(614475851855994322)
XLA Ops:
  0.0 0.0 copy-start.1
  0.0 0.0 copy-start
  0.0 1.0 deal.1
  1.0 25.2 %all_to_all.20.relayed_ref = bf16[16,2,8,192]{3,2,1,0:T(8,128)(2,1)S(1)} all-to-all(bf16[16,2,8,192]{3,2,1,0:T(8,128)(2,1)S(1)} %deal.1), channel_id=1, replica_groups=mesh['dp_0'=2,'dp_1'=16,'row_0'=2,'row_1'=2,'col_0'=4,'col_1'=2] {'dp_1'}, dimensions={0} | all-to-all | bytes 196608 | tf_op jit(solution)/shard_map/all_to_all | solution.py:242
  26.2 0.9 spread.1
  27.1 7.6 %all-to-all-start.1 = ((bf16[8,192,128]{2,1,0:T(8,128)(2,1)}), bf16[8,192,128]{2,1,0:T(8,128)(2,1)S(1)}, u32[]{:S(2)}, u32[]{:S(2)}) async-start(bf16[8,192,128]{2,1,0:T(8,128)(2,1)} %spread.1), calls=%async_computation.1 | async-start | bytes 786432 | tf_op jit(solution)/shard_map/all_to_all | solution.py:261
  34.6 1.0 pick.2
  35.7 2.4 %collective-permute-start = (bf16[1,128,2048]{2,1,0:T(8,128)(2,1)S(1)}, bf16[1,128,2048]{2,1,0:T(8,128)(2,1)S(1)}, u32[]{:S(2)}, u32[]{:S(2)}) collective-permute-start(bf16[1,128,2048]{2,1,0:T(8,128)(2,1)S(1)} %pick.2), channel_id=1, source_target_pairs={{0,1},{1,0},{2,3},{3,2},{4,5},{5,4},{6,7},{7,6},{8,9},{9,8},{10,11... | collective-permute-start | bytes 1572872 | tf_op jit(solution)/shard_map/ppermute | solution.py:248
  38.1 0.0 copy-done.1
  38.1 0.1 reshape.41
  38.2 0.1 reshape.42.gain_ref
  38.3 0.0 copy-done
  38.3 3.5 %query.1 = (bf16[256,128]{1,0:T(8,128)(2,1)S(1)}, f32[8,4096]{1,0:T(8,128)S(1)}) custom-call(s32[1]{0:T(128)} %bitcast.3.origin_ref, bf16[256,4096]{1,0:T(8,128)(2,1)} %bitcast.24, bf16[4096,128]{1,0:T(8,128)(2,1)} %weight_hbm_ref.1, f32[1,4096]{1,0:T(1,128)S(1)} %bitcast.23), custom_call_target="tpu_custom_call" | custom-call | tf_op jit(solution)/shard_map/query/pallas_call | solution.py:263
  41.9 0.1 pad_add_fusion.origins_ref
  42.0 9.8 %collective-permute-done = bf16[1,128,2048]{2,1,0:T(8,128)(2,1)S(1)} collective-permute-done((bf16[1,128,2048]{2,1,0:T(8,128)(2,1)S(1)}, bf16[1,128,2048]{2,1,0:T(8,128)(2,1)S(1)}, u32[]{:S(2)}, u32[]{:S(2)}) %collective-permute-start) | collective-permute-done | bytes 524320 | tf_op jit(solution)/shard_map/ppermute | solution.py:248
  51.8 1.6 %pick.3 = (bf16[2,128,1024]{2,1,0:T(8,128)(2,1)S(1)}, bf16[2,128,1024]{2,1,0:T(8,128)(2,1)S(1)}) custom-call(s32[4]{0:T(128)S(1)} %pad_add_fusion.origins_ref, bf16[128,4096]{1,0:T(8,128)(2,1)} %refs_0_.3, bf16[128,2048]{1,0:T(8,128)(2,1)S(1)} %bitcast.22), custom_call_target="tpu_custom_call" | custom-call | tf_op jit(solution)/shard_map/pick/pallas_call | solution.py:154
  53.4 3.6 %collective-permute-start.1 = (bf16[2,128,1024]{2,1,0:T(8,128)(2,1)S(1)}, bf16[2,128,1024]{2,1,0:T(8,128)(2,1)S(1)}, u32[]{:S(2)}, u32[]{:S(2)}) collective-permute-start(bf16[2,128,1024]{2,1,0:T(8,128)(2,1)S(1)} %get-tuple-element.15), channel_id=1, source_target_pairs={{0,8},{8,0},{1,9},{9,1},{2,10},{10,2},{3,11},{11,3},{4,12},{12,4},... | collective-permute-start | bytes 1572872 | tf_op jit(solution)/shard_map/ppermute | solution.py:251
  57.1 0.0 all-to-all-done.1
  57.1 0.2 turn.1
  57.2 0.1 multiply_convert_fusion
  57.3 35.2 %all-gather.1 = f16[2048,768]{1,0:T(8,128)(2,1)S(1)} all-gather(f16[256,768]{1,0:T(8,128)(2,1)S(1)} %multiply_convert_fusion), channel_id=1, replica_groups=mesh['dp_0'=2,'dp_1'=16,'row_0'=2,'row_1'=2,'col_0'=4,'col_1'=2] {'col_0..., dimensions={0}, use_global_device_ids=true | all-gather | bytes 3538944 | tf_op jit(solution)/shard_map/all_gather | solution.py:297
  92.6 0.5 convert_element_type.11
  93.0 3.5 %attention.1 = bf16[4,256,128]{2,1,0:T(8,128)(2,1)S(1)} custom-call(bf16[8,256,768]{2,1,0:T(8,128)(2,1)S(1)} %bitcast.18, f32[8,768]{1,0:T(8,128)S(1)} %reshape.42.gain_ref, bf16[256,128]{1,0:T(8,128)(2,1)S(1)} %get-tuple-element.13.queries_ref, bf16[32,192,128]{2,1,0:T(8,128)(2,1)} %bitcast.25, bf16[32,192,128]{2,1,0:T(8,128)(2,1)} %bitcast.26), custom_call_target="tpu_custom_call" | custom-call | tf_op jit(solution)/shard_map/attention/pallas_call | solution.py:301
  96.5 0.0 collective-permute-done.1.refs_1_
  96.5 7.7 %all_to_all.21.group_ref = bf16[4,256,128]{2,1,0:T(8,128)(2,1)S(1)} all-to-all(bf16[4,256,128]{2,1,0:T(8,128)(2,1)S(1)} %attention.1), channel_id=1, replica_groups=mesh['dp_0'=2,'dp_1'=16,'row_0'=2,'row_1'=2,'col_0'=4,'col_1'=2] {'row_1..., dimensions={0} | all-to-all | bytes 524288 | tf_op jit(solution)/shard_map/all_to_all | solution.py:316
  104.2 0.7 project.1
  104.9 22.2 %all_to_all.22 = bf16[32,8,1024]{2,1,0:T(8,128)(2,1)S(1)} all-to-all(bf16[32,8,1024]{2,1,0:T(8,128)(2,1)S(1)} %bitcast.20), channel_id=1, replica_groups=mesh['dp_0'=2,'dp_1'=16,'row_0'=2,'row_1'=2,'col_0'=4,'col_1'=2] {'row_0..., dimensions={0} | all-to-all | bytes 1048576 | tf_op jit(solution)/shard_map/all_to_all | solution.py:326
  127.1 0.7 finish.1
  (1 shorter events, 0.0 us)
Async XLA Ops:
  0.0 38.1 %copy-start.1 = (f32[6144]{0:T(1024)S(1)}, f32[6144]{0:T(1024)}, u32[]{:S(2)}) copy-start(f32[6144]{0:T(1024)} %param.9) | copy-start | bytes 73732
  0.0 38.3 %copy-start = (f32[4096]{0:T(1024)S(1)}, f32[4096]{0:T(1024)}, u32[]{:S(2)}) copy-start(f32[4096]{0:T(1024)} %param.11) | copy-start | bytes 49156
  27.1 30.0 %all-to-all-start.1 = ((bf16[8,192,128]{2,1,0:T(8,128)(2,1)}), bf16[8,192,128]{2,1,0:T(8,128)(2,1)S(1)}, u32[]{:S(2)}, u32[]{:S(2)}) async-start(bf16[8,192,128]{2,1,0:T(8,128)(2,1)} %spread.1), calls=%async_computation.1 | async-start | bytes 786432 | tf_op jit(solution)/shard_map/all_to_all | solution.py:261
  35.7 16.1 %collective-permute-start = (bf16[1,128,2048]{2,1,0:T(8,128)(2,1)S(1)}, bf16[1,128,2048]{2,1,0:T(8,128)(2,1)S(1)}, u32[]{:S(2)}, u32[]{:S(2)}) collective-permute-start(bf16[1,128,2048]{2,1,0:T(8,128)(2,1)S(1)} %pick.2), channel_id=1, source_target_pairs={{0,1},{1,0},{2,3},{3,2},{4,5},{5,4},{6,7},{7,6},{8,9},{9,8},{10,11... | collective-permute-start | bytes 1572872 | tf_op jit(solution)/shard_map/ppermute | solution.py:248
  53.4 43.1 %collective-permute-start.1 = (bf16[2,128,1024]{2,1,0:T(8,128)(2,1)S(1)}, bf16[2,128,1024]{2,1,0:T(8,128)(2,1)S(1)}, u32[]{:S(2)}, u32[]{:S(2)}) collective-permute-start(bf16[2,128,1024]{2,1,0:T(8,128)(2,1)S(1)} %get-tuple-element.15), channel_id=1, source_target_pairs={{0,8},{8,0},{1,9},{9,1},{2,10},{10,2},{3,11},{11,3},{4,12},{12,4},... | collective-permute-start | bytes 1572872 | tf_op jit(solution)/shard_map/ppermute | solution.py:251
